TPU v7x, 512 devices: a whole 4x4x16 slice. The times are simulated.
512 devices in a mesh: scen: 32 (over y, x, core), space: 8 (over z_lo), tm: 2 (over z_hi).
Axes of the slice: x: 4, y: 4, z: 16 (z_hi: 2, z_lo: 8; z = z_hi * 8 + z_lo), core: 2. Of those that a mesh axis runs over, the one named last changes fastest.
Arguments:
- coupling: bfloat16 [32, 4, 8, 128, 512], P('scen', 'tm', 'space'), may hold values from -0.09375 to 0.09375
- leaf_rhs: float32 [32, 4, 8, 128], P('scen', 'tm', 'space'), may hold values from -6 to 6
- conductance: float32 [32, 4, 8, 128], P('scen', 'tm', 'space'), may hold values from 0.42 to 0.52
- compressor: int32 [32, 4, 8], P('scen', 'tm', 'space'), may hold values 0 or 1
- blocks: float32 [32, 4, 8, 128, 128], P('scen', 'tm', 'space'), may hold values from -2 to 8, as said below
- parent_of: int32 [32], P('scen'), may hold values from 0 to 7, as said below
- parent_mat: float32 [8, 512, 512], P(None, ('space', 'tm')), may hold values from -2 to 8, as said below
- parent_rhs: float32 [8, 512], P(None, ('space', 'tm')), may hold values from -6 to 6
- link: float32 [8, 512, 256], P(None, ('space', 'tm')), may hold values from -0.25 to 0.25
- root_mat: float32 [256, 256], replicated, may hold values from -2 to 8, as said below
- root_rhs: float32 [256], replicated, may hold values from -6 to 6
Outputs:
- leaf_move: float32 [32, 4, 8, 128], P('scen', 'tm', 'space')
- parent_at_leaf: float32 [32, 512], P('scen', ('space', 'tm'))
- root_step: float32 [256], replicated
Inputs may be any that keep to these rules, and one draw needn't show every extreme that they name: `parent_of`: leaves come in aligned runs of 4 in a row; all leaves of a run share one parent, and each parent owns exactly one run. `blocks`: each block is symmetric with eigenvalues of 1 or more. `parent_mat`: each matrix is symmetric with eigenvalues of 1 or more. `root_mat`: symmetric with eigenvalues of 1 or more.
All inputs are finite; a program needn't handle non-finite values. No bound on the sum of `compressor` on one device may be relied on, other than what follows from the above.
Results may differ from a plain program's by a relative error of at most 0.0003.
Values sent between devices are 32-bit elements; how exact they have to be, the bound alone decides.
No kernel may reach another device: no remote copies, remote signals or barrier semaphores. Data moves between devices by JAX's collectives and lax.ppermute only.
A program may use at most 64 MiB of HBM per device.

v0:
```python
import jax
import jax.numpy as jnp
from jax import lax
from jax.sharding import PartitionSpec as P

PARENTS = 8
ITERS = 6


HIGH = lax.Precision.HIGHEST


def extended(cells, sides, width):
    for axis, dim in sides:
        count = lax.axis_size(axis)
        ends = count - 1
        head = lax.slice_in_dim(cells, 0, width, axis=dim)
        tail = lax.slice_in_dim(cells, cells.shape[dim] - width, cells.shape[dim], axis=dim)
        cells = jnp.concatenate(
            [
                lax.ppermute(tail, axis, [(i, (i + 1) % count) for i in range(ends)]),
                cells,
                lax.ppermute(head, axis, [((i + 1) % count, i) for i in range(ends)]),
            ],
            axis=dim,
        )
    return cells


def from_partner(block, axis, bit):
    count = lax.axis_size(axis)
    route = []
    for low in range(count):
        high = low | 1 << bit
        if high != low and high < count:
            route += [(low, high), (high, low)]
    return lax.ppermute(block, axis, route)


def factor_solve(matrix, right):
    factor = lax.linalg.cholesky(matrix)
    forward = lax.linalg.triangular_solve(factor, right, left_side=True, lower=True)
    return lax.linalg.triangular_solve(
        factor, forward, left_side=True, lower=True, transpose_a=True
    )


def invert_blocks(matrices):
    identity = jnp.broadcast_to(jnp.eye(matrices.shape[-1], dtype=matrices.dtype), matrices.shape)
    return factor_solve(matrices, identity)


def beside_all(padded):
    return padded[2:, 1:-1] + padded[:-2, 1:-1] + padded[1:-1, 2:] + padded[1:-1, :-2]


def block_apply(inverse, field):
    if field.ndim == 4:
        return jnp.einsum("tsij,tsjc->tsic", inverse, field, precision=HIGH)
    return jnp.einsum("tsij,tsj->tsi", inverse, field, precision=HIGH)


def body(
    coupling,
    leaf_rhs,
    conductance,
    compressor,
    blocks,
    parent_of,
    parent_mat,
    parent_rhs,
    link,
    root_mat,
    root_rhs,
):
    dense = coupling[0].astype(jnp.float32)
    right = leaf_rhs[0]
    weight = conductance[0] * (1.0 + compressor[0].astype(jnp.float32)[..., None]) * 0.5
    column_weight = weight[..., None]
    own_blocks = blocks[0]
    inverse = invert_blocks(own_blocks)
    solved = block_apply(inverse, dense)
    pulled = block_apply(inverse, right)
    for sweep_index in range(ITERS - 1):
        outer, outer_vector = (
            extended(solved * column_weight, (("space", 1), ("tm", 0)), 1),
            extended(pulled * weight, (("space", 1), ("tm", 0)), 1),
        )
        solved = block_apply(inverse, dense + beside_all(outer) * column_weight)
        pulled = block_apply(inverse, right + beside_all(outer_vector) * weight)
    schur = jnp.einsum("tsic,tsid->cd", dense, solved, precision=HIGH)
    gather_term = jnp.einsum("tsic,tsi->c", dense, pulled, precision=HIGH)
    strip, gather_strip = (
        lax.psum_scatter(schur, ("space", "tm"), scatter_dimension=0, tiled=True),
        lax.psum_scatter(gather_term, ("space", "tm"), scatter_dimension=0, tiled=True),
    )
    parent_label = parent_of[0]
    parent_slots = (jnp.arange(PARENTS, dtype=jnp.int32) == parent_label).astype(jnp.float32)
    group = lax.axis_size("scen") // PARENTS
    for bit_index in range(group.bit_length() - 1):
        partner, partner_vector = from_partner((strip, gather_strip), "scen", bit_index)
        strip = strip + partner
        gather_strip = gather_strip + partner_vector
    hess_strip = jnp.einsum("p,pij->ij", parent_slots, parent_mat, precision=HIGH) + strip
    right_strip = gather_strip - jnp.einsum("p,pi->i", parent_slots, parent_rhs, precision=HIGH)
    link_strip = jnp.einsum("p,pin->in", parent_slots, link, precision=HIGH)
    hessian, reduced, own_link = (
        lax.all_gather(hess_strip, ("space", "tm"), axis=0, tiled=True),
        lax.all_gather(right_strip, ("space", "tm"), axis=0, tiled=True),
        lax.all_gather(link_strip, ("space", "tm"), axis=0, tiled=True),
    )
    link_solved = factor_solve(hessian, own_link)
    vector_solved = factor_solve(hessian, reduced[:, None])[:, 0]
    leader = (lax.axis_index("scen") % group == 0).astype(jnp.float32)
    root_term, right_term = lax.psum(
        (
            jnp.einsum("in,im->nm", own_link, link_solved, precision=HIGH) * leader,
            jnp.einsum("in,i->n", own_link, vector_solved, precision=HIGH) * leader,
        ),
        "scen",
    )
    root_step = factor_solve(root_mat + root_term, (root_rhs - right_term)[:, None])[:, 0]
    parent_step = vector_solved + jnp.einsum("in,n->i", link_solved, root_step, precision=HIGH)
    share_rows = parent_step.shape[0] // (lax.axis_size("space") * lax.axis_size("tm"))
    strip_index = lax.axis_index("space") * lax.axis_size("tm") + lax.axis_index("tm")
    parent_at_leaf = lax.dynamic_slice_in_dim(parent_step, strip_index * share_rows, share_rows)[
        None
    ]
    leaf_move = pulled - jnp.einsum("tsic,c->tsi", solved, parent_step, precision=HIGH)
    return (leaf_move[None], parent_at_leaf, root_step)


def solution(mesh):
    return jax.shard_map(
        body,
        mesh=mesh,
        in_specs=(
            P("scen", "tm", "space", None, None),
            P("scen", "tm", "space", None),
            P("scen", "tm", "space", None),
            P("scen", "tm", "space"),
            P("scen", "tm", "space", None, None),
            P("scen"),
            P(None, ("space", "tm"), None),
            P(None, ("space", "tm")),
            P(None, ("space", "tm"), None),
            P(),
            P(),
        ),
        out_specs=(P("scen", "tm", "space", None), P("scen", ("space", "tm")), P()),
        check_vma=False,
    )
```

profile of v0, /device:TPU:1, one launch (start us, length us, event | category | flops | bytes accessed | tf_op | source)
XLA Modules:
  0.0 1398.3 jit_solution(3951500692941909314)
XLA Ops:
  8.5 23.5 %custom-call.49 = f32[2,1,128,128]{3,2,1,0:T(8,128)S(1)} custom-call(f32[2,1,128,128]{3,2,1,0:T(8,128)S(1)} %fusion.111), custom_call_target="Cholesky" | custom-call | tf_op jit(solution)/shard_map/cholesky | solution.py:41
  32.2 19.7 %custom-call.50 = f32[2,1,1,128,128]{3,4,2,1,0:T(8,128)S(1)} custom-call(f32[2,1,1,128,128]{4,3,2,1,0:T(8,128)S(1)} %fusion.119), custom_call_target="InvertDiagBlocksLowerTriangular" | custom-call | tf_op jit(solution)/shard_map/triangular_solve | solution.py:43
  70.1 17.1 %collective-permute-start.23 = (f32[1,3,128,512]{3,2,0,1:T(8,128)S(1)}, f32[1,3,128,512]{3,2,0,1:T(8,128)S(1)}, u32[]{:S(2)}, u32[]{:S(2)}) collective-permute-start(f32[1,3,128,512]{3,2,0,1:T(8,128)S(1)} %get-tuple-element.52), channel_id=1, source_target_pairs={{0,1},{2,3},{4,5},{6,7},{8,9},{10,11},{12,13},{14,15},{16,17},{18,... | collective-permute-start | bytes 2359304 | tf_op jit(solution)/shard_map/ppermute | solution.py:21
  88.5 17.9 %collective-permute-done.23 = f32[1,3,128,512]{3,2,0,1:T(8,128)S(1)} collective-permute-done((f32[1,3,128,512]{3,2,0,1:T(8,128)S(1)}, f32[1,3,128,512]{3,2,0,1:T(8,128)S(1)}, u32[]{:S(2)}, u32[]{:S(2)}) %collective-permute-start.23) | collective-permute-done | bytes 786464 | tf_op jit(solution)/shard_map/ppermute | solution.py:21
  106.4 17.5 %collective-permute-done.22 = f32[1,3,128,512]{3,2,0,1:T(8,128)S(1)} collective-permute-done((f32[1,3,128,512]{3,2,0,1:T(8,128)S(1)}, f32[1,3,128,512]{3,2,0,1:T(8,128)S(1)}, u32[]{:S(2)}, u32[]{:S(2)}) %collective-permute-start.22) | collective-permute-done | bytes 786464 | tf_op jit(solution)/shard_map/ppermute | solution.py:23
  124.6 43.4 %collective-permute-start.24 = (f32[2,1,128,512]{3,2,0,1:T(8,128)S(1)}, f32[2,1,128,512]{3,2,0,1:T(8,128)S(1)}, u32[]{:S(2)}, u32[]{:S(2)}) collective-permute-start(f32[2,1,128,512]{3,2,0,1:T(8,128)S(1)} %fusion.4), channel_id=1, source_target_pairs={{0,2},{2,4},{4,6},{6,8},{8,10},{10,12},{12,14},{1,3},{3,5},{5,7},{... | collective-permute-start | bytes 1572872 | tf_op jit(solution)/shard_map/ppermute | solution.py:21
  192.4 61.9 %collective-permute-done.26 = f32[1,3,128,512]{3,2,0,1:T(8,128)S(1)} collective-permute-done((f32[1,3,128,512]{3,2,0,1:T(8,128)S(1)}, f32[1,3,128,512]{3,2,0,1:T(8,128)S(1)}, u32[]{:S(2)}, u32[]{:S(2)}) %collective-permute-start.26) | collective-permute-done | bytes 786464 | tf_op jit(solution)/shard_map/ppermute | solution.py:23
  291.8 14.2 %collective-permute-done.30 = f32[1,3,128,512]{3,2,0,1:T(8,128)S(1)} collective-permute-done((f32[1,3,128,512]{3,2,0,1:T(8,128)S(1)}, f32[1,3,128,512]{3,2,0,1:T(8,128)S(1)}, u32[]{:S(2)}, u32[]{:S(2)}) %collective-permute-start.30) | collective-permute-done | bytes 786464 | tf_op jit(solution)/shard_map/ppermute | solution.py:23
  306.8 53.8 %collective-permute-start.32 = (f32[2,1,128,512]{3,2,0,1:T(8,128)S(1)}, f32[2,1,128,512]{3,2,0,1:T(8,128)S(1)}, u32[]{:S(2)}, u32[]{:S(2)}) collective-permute-start(f32[2,1,128,512]{3,2,0,1:T(8,128)S(1)} %fusion.2), channel_id=1, source_target_pairs={{0,2},{2,4},{4,6},{6,8},{8,10},{10,12},{12,14},{1,3},{3,5},{5,7},{... | collective-permute-start | bytes 1572872 | tf_op jit(solution)/shard_map/ppermute | solution.py:21
  382.7 18.1 %collective-permute-done = f32[2,1,128]{2,0,1:T(2,128)S(1)} collective-permute-done((f32[2,1,128]{2,0,1:T(2,128)S(1)}, f32[2,1,128]{2,0,1:T(2,128)S(1)}, u32[]{:S(2)}, u32[]{:S(2)}) %collective-permute-start) | collective-permute-done | bytes 1056 | tf_op jit(solution)/shard_map/ppermute | solution.py:21
  400.8 44.3 %collective-permute-done.1 = f32[2,1,128]{2,0,1:T(2,128)S(1)} collective-permute-done((f32[2,1,128]{2,0,1:T(2,128)S(1)}, f32[2,1,128]{2,0,1:T(2,128)S(1)}, u32[]{:S(2)}, u32[]{:S(2)}) %collective-permute-start.1) | collective-permute-done | bytes 1056 | tf_op jit(solution)/shard_map/ppermute | solution.py:23
  474.4 12.5 collective-permute-start.39
  491.7 129.8 %all_gather.11 = f32[512,256]{1,0:T(8,128)S(1)} all-gather(f32[32,256]{1,0:T(8,128)S(1)} %bitcast.421), channel_id=1, replica_groups=mesh['scen'=32,'space'=8,'tm'=2] {'space','tm'}, dimensions={0}, use_global_device_ids=true | all-gather | bytes 557056 | tf_op jit(solution)/shard_map/all_gather | solution.py:110
  658.2 11.7 collective-permute-done.10
  682.1 133.1 %reduce-scatter.4.cloned.1.call-done = f32[32,512]{1,0:T(8,128)} async-done(((f32[512,512]{1,0:T(8,128)}), f32[32,512]{1,0:T(8,128)}) %reduce-scatter.4.cloned.1.call-update) | async-done | bytes 65552
  816.2 18.8 %collective-permute-start.40 = (f32[32,512]{0,1:T(8,128)S(1)}, f32[32,512]{0,1:T(8,128)S(1)}, u32[]{:S(2)}, u32[]{:S(2)}) collective-permute-start(f32[32,512]{0,1:T(8,128)S(1)} %copy.80), channel_id=1, source_target_pairs={{0,16},{16,0},{32,48},{48,32},{64,80},{80,64},{96,112},{112,96},{1... | collective-permute-start | bytes 196616 | tf_op jit(solution)/shard_map/ppermute | solution.py:37
  875.5 61.5 %all-reduce.3 = f32[512]{0:T(512)S(1)} all-reduce(f32[512]{0:T(512)S(1)} %bitcast.439), channel_id=3, replica_groups=mesh['scen'=32,'space'=8,'tm'=2] {'space','tm'}, use_global_device_ids=true, to_apply=%region_11.14.clone | all-reduce | flops 512 | bytes 4096
  937.0 18.8 %collective-permute-start.42 = (f32[32]{0:T(128)S(1)}, f32[32]{0:T(128)S(1)}, u32[]{:S(2)}, u32[]{:S(2)}) collective-permute-start(f32[32]{0:T(128)S(1)} %dynamic-slice.8), channel_id=1, source_target_pairs={{0,16},{16,0},{32,48},{48,32},{64,80},{80,64},{96,112},{112,96},{1... | collective-permute-start | bytes 392 | tf_op jit(solution)/shard_map/ppermute | solution.py:37
  961.1 65.8 %all-reduce.2 = f32[512]{0:T(512)S(1)} all-reduce(f32[512]{0:T(512)S(1)} %subtract_dynamic-update-slice_fusion), channel_id=1, replica_groups=mesh['scen'=32,'space'=8,'tm'=2] {'space','tm'}, use_global_device_ids=true, to_apply=%add.2 | all-reduce | flops 512 | bytes 4096
  1100.8 11.9 custom-call.61
  1127.7 40.1 %custom-call.51 = f32[4,128,128]{1,2,0:T(8,128)S(1)} custom-call(f32[4,128,128]{2,1,0:T(8,128)} %get-tuple-element.12), custom_call_target="InvertDiagBlocksLowerTriangular" | custom-call | tf_op jit(solution)/shard_map/triangular_solve | solution.py:43
  1177.4 75.5 %psum.15 = f32[256]{0:T(256)S(1)} all-reduce(f32[256]{0:T(256)S(1)} %broadcast_multiply_fusion), channel_id=1, replica_groups=mesh['scen'=32,'space'=8,'tm'=2] {'scen'}, use_global_device_ids=true, to_apply=%region_17.20 | all-reduce | flops 256 | bytes 2048 | tf_op jit(solution)/shard_map/psum | solution.py:115
  1252.9 70.8 %all-reduce.6.cloned.1.call-done = f32[256,256]{0,1:T(8,128)} async-done(((f32[256,256]{0,1:T(8,128)}), f32[256,256]{0,1:T(8,128)}) %all-reduce.6.cloned.1.call-update) | async-done | bytes 262160 | tf_op jit(solution)/shard_map/psum | solution.py:115
  1366.6 20.8 %custom-call.52 = f32[2,128,128]{1,2,0:T(8,128)S(1)} custom-call(f32[2,128,128]{2,1,0:T(8,128)} %get-tuple-element.20), custom_call_target="InvertDiagBlocksLowerTriangular" | custom-call | tf_op jit(solution)/shard_map/triangular_solve | solution.py:43
  (298 shorter events, 390.1 us)
Async XLA Ops:
  7.2 808.0 %reduce-scatter.4.cloned.1.call-start = ((), (), s32[]{:S(2)}) async-start(), calls=%async_computation.3 | async-start | bytes 1114112
  70.1 36.3 %collective-permute-start.23 = (f32[1,3,128,512]{3,2,0,1:T(8,128)S(1)}, f32[1,3,128,512]{3,2,0,1:T(8,128)S(1)}, u32[]{:S(2)}, u32[]{:S(2)}) collective-permute-start(f32[1,3,128,512]{3,2,0,1:T(8,128)S(1)} %get-tuple-element.52), channel_id=1, source_target_pairs={{0,1},{2,3},{4,5},{6,7},{8,9},{10,11},{12,13},{14,15},{16,17},{18,... | collective-permute-start | bytes 2359304 | tf_op jit(solution)/shard_map/ppermute | solution.py:21
  87.2 36.7 %collective-permute-start.22 = (f32[1,3,128,512]{3,2,0,1:T(8,128)S(1)}, f32[1,3,128,512]{3,2,0,1:T(8,128)S(1)}, u32[]{:S(2)}, u32[]{:S(2)}) collective-permute-start(f32[1,3,128,512]{3,2,0,1:T(8,128)S(1)} %get-tuple-element.51), channel_id=1, source_target_pairs={{1,0},{3,2},{5,4},{7,6},{9,8},{11,10},{13,12},{15,14},{17,16},{19,... | collective-permute-start | bytes 2359304 | tf_op jit(solution)/shard_map/ppermute | solution.py:23
  124.6 52.9 %collective-permute-start.24 = (f32[2,1,128,512]{3,2,0,1:T(8,128)S(1)}, f32[2,1,128,512]{3,2,0,1:T(8,128)S(1)}, u32[]{:S(2)}, u32[]{:S(2)}) collective-permute-start(f32[2,1,128,512]{3,2,0,1:T(8,128)S(1)} %fusion.4), channel_id=1, source_target_pairs={{0,2},{2,4},{4,6},{6,8},{8,10},{10,12},{12,14},{1,3},{3,5},{5,7},{... | collective-permute-start | bytes 1572872 | tf_op jit(solution)/shard_map/ppermute | solution.py:21
  183.6 70.8 %collective-permute-start.26 = (f32[1,3,128,512]{3,2,0,1:T(8,128)S(1)}, f32[1,3,128,512]{3,2,0,1:T(8,128)S(1)}, u32[]{:S(2)}, u32[]{:S(2)}) collective-permute-start(f32[1,3,128,512]{3,2,0,1:T(8,128)S(1)} %get-tuple-element.49), channel_id=1, source_target_pairs={{1,0},{3,2},{5,4},{7,6},{9,8},{11,10},{13,12},{15,14},{17,16},{19,... | collective-permute-start | bytes 2359304 | tf_op jit(solution)/shard_map/ppermute | solution.py:23
  255.1 17.9 %collective-permute-start.28 = (f32[2,1,128,512]{3,2,0,1:T(8,128)S(1)}, f32[2,1,128,512]{3,2,0,1:T(8,128)S(1)}, u32[]{:S(2)}, u32[]{:S(2)}) collective-permute-start(f32[2,1,128,512]{3,2,0,1:T(8,128)S(1)} %fusion.3), channel_id=1, source_target_pairs={{0,2},{2,4},{4,6},{6,8},{8,10},{10,12},{12,14},{1,3},{3,5},{5,7},{... | collective-permute-start | bytes 1572872 | tf_op jit(solution)/shard_map/ppermute | solution.py:21
  277.3 14.5 %collective-permute-start.31 = (f32[1,3,128,512]{3,2,0,1:T(8,128)S(1)}, f32[1,3,128,512]{3,2,0,1:T(8,128)S(1)}, u32[]{:S(2)}, u32[]{:S(2)}) collective-permute-start(f32[1,3,128,512]{3,2,0,1:T(8,128)S(1)} %get-tuple-element.48), channel_id=1, source_target_pairs={{0,1},{2,3},{4,5},{6,7},{8,9},{10,11},{12,13},{14,15},{16,17},{18,... | collective-permute-start | bytes 2359304 | tf_op jit(solution)/shard_map/ppermute | solution.py:21
  278.6 27.4 %collective-permute-start.30 = (f32[1,3,128,512]{3,2,0,1:T(8,128)S(1)}, f32[1,3,128,512]{3,2,0,1:T(8,128)S(1)}, u32[]{:S(2)}, u32[]{:S(2)}) collective-permute-start(f32[1,3,128,512]{3,2,0,1:T(8,128)S(1)} %get-tuple-element.47), channel_id=1, source_target_pairs={{1,0},{3,2},{5,4},{7,6},{9,8},{11,10},{13,12},{15,14},{17,16},{19,... | collective-permute-start | bytes 2359304 | tf_op jit(solution)/shard_map/ppermute | solution.py:23
  306.8 64.4 %collective-permute-start.32 = (f32[2,1,128,512]{3,2,0,1:T(8,128)S(1)}, f32[2,1,128,512]{3,2,0,1:T(8,128)S(1)}, u32[]{:S(2)}, u32[]{:S(2)}) collective-permute-start(f32[2,1,128,512]{3,2,0,1:T(8,128)S(1)} %fusion.2), channel_id=1, source_target_pairs={{0,2},{2,4},{4,6},{6,8},{8,10},{10,12},{12,14},{1,3},{3,5},{5,7},{... | collective-permute-start | bytes 1572872 | tf_op jit(solution)/shard_map/ppermute | solution.py:21
  375.4 82.8 %collective-permute-start.35 = (f32[1,3,128,512]{3,2,0,1:T(8,128)S(1)}, f32[1,3,128,512]{3,2,0,1:T(8,128)S(1)}, u32[]{:S(2)}, u32[]{:S(2)}) collective-permute-start(f32[1,3,128,512]{3,2,0,1:T(8,128)S(1)} %get-tuple-element.46), channel_id=1, source_target_pairs={{0,1},{2,3},{4,5},{6,7},{8,9},{10,11},{12,13},{14,15},{16,17},{18,... | collective-permute-start | bytes 2359304 | tf_op jit(solution)/shard_map/ppermute | solution.py:21
  377.3 81.0 %collective-permute-start.34 = (f32[1,3,128,512]{3,2,0,1:T(8,128)S(1)}, f32[1,3,128,512]{3,2,0,1:T(8,128)S(1)}, u32[]{:S(2)}, u32[]{:S(2)}) collective-permute-start(f32[1,3,128,512]{3,2,0,1:T(8,128)S(1)} %get-tuple-element.45), channel_id=1, source_target_pairs={{1,0},{3,2},{5,4},{7,6},{9,8},{11,10},{13,12},{15,14},{17,16},{19,... | collective-permute-start | bytes 2359304 | tf_op jit(solution)/shard_map/ppermute | solution.py:23
  378.6 22.2 %collective-permute-start = (f32[2,1,128]{2,0,1:T(2,128)S(1)}, f32[2,1,128]{2,0,1:T(2,128)S(1)}, u32[]{:S(2)}, u32[]{:S(2)}) collective-permute-start(f32[2,1,128]{2,0,1:T(2,128)S(1)} %get-tuple-element.37), channel_id=1, source_target_pairs={{0,2},{2,4},{4,6},{6,8},{8,10},{10,12},{12,14},{1,3},{3,5},{5,7},{... | collective-permute-start | bytes 3080 | tf_op jit(solution)/shard_map/ppermute | solution.py:21
  380.8 64.3 %collective-permute-start.1 = (f32[2,1,128]{2,0,1:T(2,128)S(1)}, f32[2,1,128]{2,0,1:T(2,128)S(1)}, u32[]{:S(2)}, u32[]{:S(2)}) collective-permute-start(f32[2,1,128]{2,0,1:T(2,128)S(1)} %get-tuple-element.37), channel_id=1, source_target_pairs={{2,0},{4,2},{6,4},{8,6},{10,8},{12,10},{14,12},{3,1},{5,3},{7,5},{... | collective-permute-start | bytes 3080 | tf_op jit(solution)/shard_map/ppermute | solution.py:23
  445.1 17.1 %collective-permute-start.3 = (f32[1,3,128]{2,0,1:T(1,128)S(1)}, f32[1,3,128]{2,0,1:T(1,128)S(1)}, u32[]{:S(2)}, u32[]{:S(2)}) collective-permute-start(f32[1,3,128]{2,0,1:T(1,128)S(1)} %get-tuple-element.76), channel_id=1, source_target_pairs={{0,1},{2,3},{4,5},{6,7},{8,9},{10,11},{12,13},{14,15},{16,17},{18,... | collective-permute-start | bytes 4616 | tf_op jit(solution)/shard_map/ppermute | solution.py:21
  474.4 153.9 %collective-permute-start.39 = (f32[1,3,128,512]{3,2,0,1:T(8,128)S(1)}, f32[1,3,128,512]{3,2,0,1:T(8,128)S(1)}, u32[]{:S(2)}, u32[]{:S(2)}) collective-permute-start(f32[1,3,128,512]{3,2,0,1:T(8,128)S(1)} %get-tuple-element.44), channel_id=1, source_target_pairs={{0,1},{2,3},{4,5},{6,7},{8,9},{10,11},{12,13},{14,15},{16,17},{18,... | collective-permute-start | bytes 2359304 | tf_op jit(solution)/shard_map/ppermute | solution.py:21
  486.9 141.4 %collective-permute-start.38 = (f32[1,3,128,512]{3,2,0,1:T(8,128)S(1)}, f32[1,3,128,512]{3,2,0,1:T(8,128)S(1)}, u32[]{:S(2)}, u32[]{:S(2)}) collective-permute-start(f32[1,3,128,512]{3,2,0,1:T(8,128)S(1)} %get-tuple-element.43), channel_id=1, source_target_pairs={{1,0},{3,2},{5,4},{7,6},{9,8},{11,10},{13,12},{15,14},{17,16},{19,... | collective-permute-start | bytes 2359304 | tf_op jit(solution)/shard_map/ppermute | solution.py:23
  488.2 133.3 %collective-permute-start.4 = (f32[2,1,128]{2,0,1:T(2,128)S(1)}, f32[2,1,128]{2,0,1:T(2,128)S(1)}, u32[]{:S(2)}, u32[]{:S(2)}) collective-permute-start(f32[2,1,128]{2,0,1:T(2,128)S(1)} %multiply_bitcast_fusion.3), channel_id=1, source_target_pairs={{0,2},{2,4},{4,6},{6,8},{8,10},{10,12},{12,14},{1,3},{3,5},{5,7},{... | collective-permute-start | bytes 3080 | tf_op jit(solution)/shard_map/ppermute | solution.py:21
  490.4 131.1 %collective-permute-start.5 = (f32[2,1,128]{2,0,1:T(2,128)S(1)}, f32[2,1,128]{2,0,1:T(2,128)S(1)}, u32[]{:S(2)}, u32[]{:S(2)}) collective-permute-start(f32[2,1,128]{2,0,1:T(2,128)S(1)} %multiply_bitcast_fusion.3), channel_id=1, source_target_pairs={{2,0},{4,2},{6,4},{8,6},{10,8},{12,10},{14,12},{3,1},{5,3},{7,5},{... | collective-permute-start | bytes 3080 | tf_op jit(solution)/shard_map/ppermute | solution.py:23
  631.8 395.2 %all-gather.2.cloned.1.call-start = ((), (), s32[]{:S(2)}) async-start(), calls=%async_computation.1 | async-start | bytes 1114112 | tf_op jit(solution)/shard_map/all_gather | solution.py:108
  670.3 164.7 %collective-permute-start.12 = (f32[2,1,128]{2,0,1:T(2,128)S(1)}, f32[2,1,128]{2,0,1:T(2,128)S(1)}, u32[]{:S(2)}, u32[]{:S(2)}) collective-permute-start(f32[2,1,128]{2,0,1:T(2,128)S(1)} %multiply_bitcast_fusion.1), channel_id=1, source_target_pairs={{0,2},{2,4},{4,6},{6,8},{8,10},{10,12},{12,14},{1,3},{3,5},{5,7},{... | collective-permute-start | bytes 3080 | tf_op jit(solution)/shard_map/ppermute | solution.py:21
  680.6 154.4 %collective-permute-start.13 = (f32[2,1,128]{2,0,1:T(2,128)S(1)}, f32[2,1,128]{2,0,1:T(2,128)S(1)}, u32[]{:S(2)}, u32[]{:S(2)}) collective-permute-start(f32[2,1,128]{2,0,1:T(2,128)S(1)} %multiply_bitcast_fusion.1), channel_id=1, source_target_pairs={{2,0},{4,2},{6,4},{8,6},{10,8},{12,10},{14,12},{3,1},{5,3},{7,5},{... | collective-permute-start | bytes 3080 | tf_op jit(solution)/shard_map/ppermute | solution.py:23
  816.2 19.9 %collective-permute-start.40 = (f32[32,512]{0,1:T(8,128)S(1)}, f32[32,512]{0,1:T(8,128)S(1)}, u32[]{:S(2)}, u32[]{:S(2)}) collective-permute-start(f32[32,512]{0,1:T(8,128)S(1)} %copy.80), channel_id=1, source_target_pairs={{0,16},{16,0},{32,48},{48,32},{64,80},{80,64},{96,112},{112,96},{1... | collective-permute-start | bytes 196616 | tf_op jit(solution)/shard_map/ppermute | solution.py:37
  846.4 477.3 %all-reduce.6.cloned.1.call-start = ((), (), s32[]{:S(2)}) async-start(), calls=%async_computation.2 | async-start | bytes 524288 | tf_op jit(solution)/shard_map/psum | solution.py:115
  937.0 19.6 %collective-permute-start.42 = (f32[32]{0:T(128)S(1)}, f32[32]{0:T(128)S(1)}, u32[]{:S(2)}, u32[]{:S(2)}) collective-permute-start(f32[32]{0:T(128)S(1)} %dynamic-slice.8), channel_id=1, source_target_pairs={{0,16},{16,0},{32,48},{48,32},{64,80},{80,64},{96,112},{112,96},{1... | collective-permute-start | bytes 392 | tf_op jit(solution)/shard_map/ppermute | solution.py:37
  (38 other events, 1576.6 us)
Sparse Core Ops, SparseCore 0:
  631.9 183.3 reduce-scatter.3
  846.5 164.8 all-gather.1
  1177.2 146.4 all-reduce.5
where the time goes:
time: 1410 us; the launch traced here: 1400 us
  waiting for transfers between devices  506 us (36%)
  blocking collectives  333 us (24%)
  starting transfers between devices  263 us (19%)
  other arithmetic  222 us (16%)
  local copies, waits for them, and re-layouts  27 us (2%)
  matrix products  26.3 us (2%)
  between operations  21.4 us (2%)
    ppermute x20, waiting for transfers between devices, extended(): lax.ppermute(head, axis, [((i + 1) % count, i) for i in range(ends)])  207 us
    ppermute x20, starting transfers between devices, extended(): lax.ppermute(tail, axis, [(i, (i + 1) % count) for i in range(ends)])  195 us
    another operation x25, other arithmetic, factor_solve(): factor = lax.linalg.cholesky(matrix)  137 us
    unnamed x4, waiting for transfers between devices  133 us
    all_gather x1, blocking collectives, body(): lax.all_gather(link_strip, ('space', 'tm'), axis=0, tiled=True)  130 us
    unnamed x2, blocking collectives  127 us
    ppermute x20, waiting for transfers between devices, extended(): lax.ppermute(tail, axis, [(i, (i + 1) % count) for i in range(ends)])  87.8 us
    another operation x11, other arithmetic, factor_solve(): lax.linalg.triangular_solve(factor, forward, left_side=True, lower=True,...  81.4 us
  transfers between devices with their start and end apart: 47, of which 30 were waited for; matrix products, arithmetic and copies ran while one was open for 1% of the time, Pallas kernels for 0%

commit v1 on v0

v1 whole, which is shorter than its diff:
```python
import functools

import jax
import jax.numpy as jnp
from jax import lax
from jax.experimental import pallas as pl
from jax.experimental.pallas import tpu as pltpu
from jax.sharding import PartitionSpec as P

AXES = ("scen", "space", "tm")
Z_AXES = ("space", "tm")
F32 = jnp.float32
HIGH = lax.Precision.HIGHEST

QUARTER = (0, 2, 1, 3)
LEAF_OF_QUARTER = (0, 2, 1, 3)
Z_SHIFT = 2


def linear(scen, z):
    return (scen * 8 + z % 8) * 2 + z // 8


def home(group, leaf, half, cell):
    return linear(group * 4 + leaf, half * 8 + cell)


def away(group, leaf, half, cell):
    column = half ^ (leaf // 2)
    z = (4 * QUARTER[leaf] + 3 - cell // 2 + Z_SHIFT) % 16
    return linear(group * 4 + column * 2 + cell % 2, z)


def every_cell():
    for group in range(8):
        for leaf in range(4):
            for half in range(2):
                for cell in range(8):
                    yield group, leaf, half, cell


MOVE_OUT = [(home(*at), away(*at)) for at in every_cell()]
MOVE_BACK = [(there, here) for here, there in MOVE_OUT]
TO_CORE = [(away(g, l, h, c), away(g, l, h, c ^ 1)) for g, l, h, c in every_cell()]
TO_HALF = [(away(g, l, h, c), away(g, l, h ^ 1, c)) for g, l, h, c in every_cell()]
TO_CHIP = [
    (away(g, l, h, c), away(g, l, h, c + (1 if c % 2 else -1)))
    for g, l, h, c in every_cell()
    if 0 <= c + (1 if c % 2 else -1) < 8
]


def flip(bit):
    return [(i, i ^ bit) for i in range(32)]


def dot(a, b, dims=((1,), (0,)), precision=HIGH):
    return lax.dot_general(a, b, (dims, ((), ())), precision=precision, preferred_element_type=F32)


NT = ((1,), (1,))
TN = ((0,), (0,))


def sweep8(matrix, lane, sub):
    top = matrix[:8]
    columns = [jnp.broadcast_to(matrix[:, k : k + 1], (128, 128)) for k in range(8)]
    small = [c[:8] for c in columns]
    rows = jnp.where(lane < 8, (sub == lane).astype(F32), top)
    for k in range(8):
        scale = 1.0 / small[k][k : k + 1]
        pivot_row = rows[k : k + 1] * scale
        factor = jnp.where(sub == k, 0.0, small[k])
        rows = jnp.where(sub == k, pivot_row, rows - factor * pivot_row)
        for j in range(k + 1, 8):
            entry = small[j][k : k + 1] * scale
            small[j] = jnp.where(sub == k, entry, small[j] - factor * entry)
    rest = jnp.where(lane < 8, 0.0, matrix[8:])
    for k in range(8):
        rest = rest - columns[k][8:] * rows[k : k + 1]
    return jnp.concatenate([rest, rows], axis=0)


def inverses(matrices):
    lane = lax.broadcasted_iota(jnp.int32, (1, 128), 1)
    sub = lax.broadcasted_iota(jnp.int32, (8, 1), 0)

    def step(_, carry):
        return tuple(pltpu.roll(sweep8(m, lane, sub), 120, 1) for m in carry)

    return lax.fori_loop(0, 16, step, tuple(matrices))


def call(kernel, name, shapes, *operands, scratch=(), scalars=0):
    smem = pl.BlockSpec(memory_space=pltpu.SMEM)
    vmem = pl.BlockSpec(memory_space=pltpu.VMEM)
    return pl.pallas_call(
        kernel,
        name=name,
        out_shape=[jax.ShapeDtypeStruct(s, F32) for s in shapes],
        in_specs=[smem] * scalars + [vmem] * (len(operands) - scalars),
        out_specs=[vmem] * len(shapes),
        scratch_shapes=list(scratch),
    )(*operands)


def invert_kernel(pack, inverse, scaled, half_scaled):
    found = inverses([pack[0:128], pack[128:256]])
    for t in range(2):
        across = jnp.broadcast_to(pack[258 + t : 259 + t], (128, 128))
        down = across.T
        rows = slice(t * 128, t * 128 + 128)
        inverse[rows] = found[t]
        half_scaled[rows] = down * found[t]
        scaled[rows] = down * found[t] * across


def put_rows(out, first, second):
    out[256:264] = jnp.zeros((8, 512), F32)
    out[256:257, 0:128] = first
    out[256:257, 128:256] = second


def put_half(half, out, blocks, rows):
    early = half == 0
    out[0:128] = jnp.where(early, blocks[1], blocks[0])
    out[128:136] = jnp.zeros((8, 512), F32)
    out[128:129, 0:128] = jnp.where(early, rows[1], rows[0])


def start_kernel(flags, pack, inverse, half_scaled, coupling, first, message, to_half):
    blocks, rows = [], []
    for t in range(2):
        at = slice(t * 128, t * 128 + 128)
        first[at] = dot(inverse[at], coupling[at])
        blocks.append(dot(half_scaled[at], coupling[at]))
        message[at] = blocks[t]
        rows.append(dot(pack[256 + t : 257 + t], half_scaled[at], NT))
    put_rows(message, *rows)
    put_half(flags[0], to_half, blocks, rows)


def beside(half, own, core, chip, other):
    late = (half == 1).astype(F32)
    weights = (late, 1.0 - late)
    blocks, rows = [], []
    for t in range(2):
        at = slice(t * 128, t * 128 + 128)
        back = slice(128 - t * 128, 256 - t * 128)
        blocks.append(own[back] + core[at] + chip[at] + other[0:128] * weights[t])
        rows.append(
            own[256:257, back] + core[256:257, at] + chip[256:257, at] + other[128:129, 0:128] * weights[t]
        )
    return blocks, rows


def sweep_kernel(flags, scaled, own, core, chip, other, near, message, to_half):
    blocks, rows = beside(flags[0], own, core, chip, other)
    new, new_rows = [], []
    for t in range(2):
        at = slice(t * 128, t * 128 + 128)
        near[at] = blocks[t]
        new.append(dot(scaled[at], blocks[t]))
        message[at] = new[t]
        new_rows.append(dot(rows[t], scaled[at]))
    put_rows(near, *rows)
    put_rows(message, *new_rows)
    put_half(flags[0], to_half, new, new_rows)


def ring_columns(ref, b, count):
    parts = [ref[0:256, ((b + m) % 4) * 128 : ((b + m) % 4) * 128 + 128] for m in range(count)]
    return jnp.concatenate(parts, axis=1)


def gram_early_kernel(pack, coupling, first, own, near, gram, gather):
    for b in range(4):
        count = 3 if b < 2 else 2
        at = slice(b * 128, b * 128 + 128)
        part = dot(coupling[0:256, at], ring_columns(first, b, count), TN)
        part = part + dot(own[0:256, at], ring_columns(near, b, count), TN)
        gram[at, 0 : count * 128] = part
        if count == 2:
            gram[at, 256:384] = jnp.zeros((128, 128), F32)
    row = jnp.zeros((1, 512), F32)
    for t in range(2):
        at = slice(t * 128, t * 128 + 128)
        row = row + dot(pack[256 + t : 257 + t], first[at])
        row = row + dot(near[256:257, at], own[at])
    gather[0:8] = jnp.broadcast_to(row, (8, 512))


def gram_late_kernel(
    flags, gram, gather, right, own0, own2, near1, own2_core, chip, other, near2, keep, send, total, both, fields
):
    blocks, rows = beside(flags[0], own2, own2_core, chip, other)
    both[...] = own0[0:256] + own2[0:256]
    row = gather[0:1]
    for t in range(2):
        at = slice(t * 128, t * 128 + 128)
        near2[at] = blocks[t]
        fields[at] = near1[at] + blocks[t]
        row = row + dot(rows[t] + near1[256:257, at], both[at])
    put_rows(near2, *rows)
    for b in range(4):
        count = 3 if b < 2 else 2
        at = slice(b * 128, b * 128 + 128)
        part = gram[at, 0 : count * 128] + dot(both[0:256, at], ring_columns(fields, b, count), TN)
        for m in range(4):
            for j in range(4):
                source = part[m * 32 + j * 8 : m * 32 + j * 8 + 8]
                total[j % 2, j // 2, b * 32 + m * 8 : b * 32 + m * 8 + 8, 0 : count * 128] = source
                if count == 2:
                    extra = jnp.zeros((8, 128), F32)
                    if b == 2 and m == 0 and j == 0:
                        four = jnp.concatenate([row[:, i * 128 : i * 128 + 128] for i in range(4)], axis=0)
                        extra = jnp.concatenate([four - right[0:4], jnp.zeros((4, 128), F32)], axis=0)
                    total[j % 2, j // 2, b * 32 + m * 8 : b * 32 + m * 8 + 8, 256:384] = extra
    keep[...] = total[flags[1]]
    send[...] = total[1 - flags[1]]


def halve_kernel(flags, mine, theirs, keep, send):
    keep[...] = mine[flags[2]] + theirs[flags[2]]
    send[...] = mine[1 - flags[2]] + theirs[1 - flags[2]]


def parent_kernel(flags, mine, across_x, across_core, root_part, upper, solved, solved_row, held):
    leaf = flags[3]
    held[:, leaf] = mine[...]
    held[:, leaf ^ 2] = across_x[...]
    held[:, leaf ^ 1] = across_core[0]
    held[:, leaf ^ 3] = across_core[1]

    def block(b, m):
        return held[4 * b : 4 * b + 4, :, :, m * 128 : m * 128 + 128].reshape(128, 128)

    entry = {}
    for b in range(4):
        for j in range(b, 4):
            entry[b, j] = block(3, 1).T if (b, j) == (0, 3) else block(b, j - b)
    rhs = [held[4 * b : 4 * b + 4, :, :, 384:640].reshape(128, 256) for b in range(4)]
    reduced = held[8, 0, :, 256:384]
    rows = [reduced[b : b + 1] for b in range(4)]
    part = jnp.zeros((256, 256), F32)
    part_row = jnp.zeros((1, 256), F32)
    upper[...] = jnp.zeros((384, 512), F32)
    for b in range(4):
        (inverse,) = inverses([entry[b, b]])
        wide = jnp.concatenate([entry[b, j] for j in range(b + 1, 4)] + [rhs[b]], axis=1)
        wide = dot(inverse, wide)
        span = (3 - b) * 128
        done = wide[:, span:]
        solved[b * 128 : b * 128 + 128] = done
        row = dot(rows[b], inverse)
        solved_row[0:8, b * 128 : b * 128 + 128] = jnp.broadcast_to(row, (8, 128))
        for i in range(b + 1, 4):
            left = entry[b, i]
            skip = (i - b - 1) * 128
            change = dot(left, wide[:, skip:], TN)
            for j in range(i, 4):
                entry[i, j] = entry[i, j] - change[:, (j - i) * 128 : (j - i) * 128 + 128]
            rhs[i] = rhs[i] - change[:, (4 - i) * 128 :]
            rows[i] = rows[i] - dot(row, left)
            upper[b * 128 : b * 128 + 128, i * 128 : i * 128 + 128] = wide[:, skip : skip + 128]
        part = part + dot(rhs[b], done, TN)
        part_row = part_row + dot(row, rhs[b])
    root_part[0:256] = part
    root_part[256:264] = jnp.broadcast_to(part_row, (8, 256))


def root_kernel(
    flags, mine, theirs, matrix, right, upper, solved, solved_row, pack, coupling, near0, near1, near2, scaled,
    step, parent, source, message, to_half,
):
    total = matrix[...] + (mine[0:256] + theirs[0:256])
    vector = right[0:1] - (mine[256:257] + theirs[256:257])
    side = total[0:128, 128:256]
    (first,) = inverses([total[0:128, 0:128]])
    pushed = dot(first, side)
    (second,) = inverses([total[128:256, 128:256] - dot(side, pushed, TN)])
    head = dot(vector[:, 0:128], first)
    tail = dot(vector[:, 128:256] - dot(head, side), second)
    head = head - dot(tail, pushed, NT)
    root = jnp.concatenate([head, tail], axis=1)
    step[...] = jnp.broadcast_to(root, (8, 256))
    pieces = [None] * 4
    for b in range(3, -1, -1):
        at = slice(b * 128, b * 128 + 128)
        value = solved_row[0:1, at] + dot(root, solved[at], NT)
        for j in range(b + 1, 4):
            value = value - dot(pieces[j], upper[at, j * 128 : j * 128 + 128], NT)
        pieces[b] = value
    whole = jnp.concatenate(pieces, axis=1)
    parent[...] = jnp.broadcast_to(whole, (8, 512))
    source_rows, message_rows = [], []
    for t in range(2):
        at = slice(t * 128, t * 128 + 128)
        last = near2[256:257, at] - dot(whole, near2[at], NT)
        early = near0[256:257, at] + near1[256:257, at] - dot(whole, near0[at] + near1[at], NT)
        weight = pack[258 + t : 259 + t]
        source_rows.append(pack[256 + t : 257 + t] - dot(whole, coupling[at], NT) + weight * (early + last))
        message_rows.append(dot(last, scaled[at]))
    source[...] = jnp.broadcast_to(jnp.concatenate(source_rows, axis=1), (8, 256))
    message[...] = jnp.broadcast_to(jnp.concatenate(message_rows, axis=1), (8, 256))
    other = jnp.where(flags[0] == 0, message_rows[1], message_rows[0])
    to_half[...] = jnp.broadcast_to(other, (8, 128))


def beside_rows(half, own, core, chip, other):
    late = (half == 1).astype(F32)
    weights = (late, 1.0 - late)
    rows = []
    for t in range(2):
        at = slice(t * 128, t * 128 + 128)
        back = slice(128 - t * 128, 256 - t * 128)
        rows.append(own[0:1, back] + core[0:1, at] + chip[0:1, at] + other[0:1] * weights[t])
    return rows


def vector_kernel(flags, pack, scaled, source, own, core, chip, other, new_source, message, to_half):
    rows = beside_rows(flags[0], own, core, chip, other)
    new = []
    for t in range(2):
        at = slice(t * 128, t * 128 + 128)
        new_source[0:8, at] = jnp.broadcast_to(source[0:1, at] + pack[258 + t : 259 + t] * rows[t], (8, 128))
        new.append(dot(rows[t], scaled[at]))
    message[...] = jnp.broadcast_to(jnp.concatenate(new, axis=1), (8, 256))
    to_half[...] = jnp.broadcast_to(jnp.where(flags[0] == 0, new[1], new[0]), (8, 128))


def finish_kernel(flags, pack, inverse, source, own, core, chip, other, out):
    rows = beside_rows(flags[0], own, core, chip, other)
    for t in range(2):
        at = slice(t * 128, t * 128 + 128)
        full = source[0:1, at] + pack[258 + t : 259 + t] * rows[t]
        out[0:8, at] = jnp.broadcast_to(dot(full, inverse[at]), (8, 128))


def neighbours(message, to_half):
    return (
        lax.ppermute(message, AXES, TO_CORE),
        lax.ppermute(message, AXES, TO_CHIP),
        lax.ppermute(to_half, AXES, TO_HALF),
    )


def body(
    coupling, leaf_rhs, conductance, compressor, blocks, parent_of, parent_mat, parent_rhs, link, root_mat, root_rhs
):
    scen = lax.axis_index("scen")
    space = lax.axis_index("space")
    tm = lax.axis_index("tm")
    z = tm * 8 + space
    strip = space * 2 + tm
    quarter = ((z - Z_SHIFT) % 16) // 4
    core = scen % 2
    column = (scen // 2) % 2
    half = column ^ (quarter % 2)
    flags = jnp.stack([half, core, column, scen % 4]).astype(jnp.int32)

    weight = conductance[0] * (1.0 + compressor[0].astype(F32)[..., None]) * 0.5
    pack = jnp.concatenate(
        [
            blocks[0].reshape(256, 128),
            leaf_rhs[0].reshape(2, 128),
            weight.reshape(2, 128),
            jnp.zeros((4, 128), F32),
        ],
        axis=0,
    )
    pack = lax.ppermute(pack, AXES, MOVE_OUT)
    field = lax.ppermute(coupling[0].reshape(256, 512).astype(F32), AXES, MOVE_OUT)

    label = parent_of[0]
    sibling = scen % 4
    row_block = strip // 4
    matrix_rows = lax.dynamic_slice(parent_mat, (label, sibling * 8, 0), (1, 8, 512))[0]
    matrix_rows = lax.dynamic_slice(
        jnp.concatenate([matrix_rows, matrix_rows], axis=1), (0, row_block * 128), (8, 384)
    )
    spare = (row_block >= 2) & (lax.broadcasted_iota(jnp.int32, (8, 384), 1) >= 256)
    matrix_rows = jnp.where(spare, 0.0, matrix_rows)
    link_rows = lax.dynamic_slice(link, (label, sibling * 8, 0), (1, 8, 256))[0]
    right = lax.dynamic_slice(parent_rhs, (label, 0), (1, 32))[0] * (sibling == 0).astype(F32)
    right = lax.dynamic_update_slice(jnp.zeros((512,), F32), right, (strip * 32,)).reshape(4, 128)
    right = jnp.concatenate([right, jnp.zeros((4, 128), F32)], axis=0)

    inverse, scaled, half_scaled = call(invert_kernel, "invert", [(256, 128)] * 3, pack)
    shapes = [(256, 512), (264, 512), (136, 512)]
    first, own0, half0 = call(
        start_kernel, "start", shapes, flags, pack, inverse, half_scaled, field, scalars=1
    )
    shapes = [(264, 512), (264, 512), (136, 512)]
    near0, own1, half1 = call(
        sweep_kernel, "sweep", shapes, flags, scaled, own0, *neighbours(own0, half0), scalars=1
    )
    around1 = neighbours(own1, half1)
    gram, gather = call(
        gram_early_kernel, "gram_early", [(512, 384), (8, 512)], pack, field, first, own0, near0
    )
    near1, own2, half2 = call(
        sweep_kernel, "sweep", shapes, flags, scaled, own1, *around1, scalars=1
    )
    near2, keep, send = call(
        gram_late_kernel,
        "gram_late",
        [(264, 512), (2, 128, 384), (2, 128, 384)],
        flags, gram, gather, right, own0, own2, near1, *neighbours(own2, half2),
        scalars=1,
        scratch=[pltpu.VMEM((2, 2, 128, 384), F32), pltpu.VMEM((256, 512), F32), pltpu.VMEM((256, 512), F32)],
    )

    keep, send = call(
        halve_kernel, "halve", [(128, 384)] * 2, flags, keep, lax.ppermute(send, "scen", flip(1)), scalars=1
    )
    quarter_sum = keep + lax.ppermute(send, "scen", flip(2))
    shares = lax.all_to_all(quarter_sum.reshape(16, 8, 384), Z_AXES, 0, 0)
    share = jnp.concatenate([jnp.sum(shares, axis=0) + matrix_rows, link_rows], axis=1)
    mine = lax.all_to_all(jnp.broadcast_to(share[None], (16, 8, 640)), Z_AXES, 0, 0)
    across_x = lax.ppermute(mine, "scen", flip(2))
    across_core = lax.ppermute(jnp.stack([mine, across_x]), "scen", flip(1))

    part, upper, solved, solved_row = call(
        parent_kernel,
        "parent",
        [(264, 256), (384, 512), (512, 256), (8, 512)],
        flags, mine, across_x, across_core,
        scalars=1,
        scratch=[pltpu.VMEM((16, 4, 8, 640), F32)],
    )
    part = part + lax.ppermute(part, "scen", flip(4))
    part = part + lax.ppermute(part, "scen", flip(8))
    step, parent, source, message, to_half = call(
        root_kernel,
        "root",
        [(8, 256), (8, 512), (8, 256), (8, 256), (8, 128)],
        flags, part, lax.ppermute(part, "scen", flip(16)), root_mat,
        jnp.broadcast_to(root_rhs[None], (8, 256)), upper, solved, solved_row, pack, field, near0, near1, near2, scaled,
        scalars=1,
    )
    source, message, to_half = call(
        vector_kernel,
        "vector",
        [(8, 256), (8, 256), (8, 128)],
        flags, pack, scaled, source, message, *neighbours(message, to_half),
        scalars=1,
    )
    (move,) = call(
        finish_kernel,
        "finish",
        [(8, 256)],
        flags, pack, inverse, source, message, *neighbours(message, to_half),
        scalars=1,
    )
    move = lax.ppermute(move, AXES, MOVE_BACK)
    parent_at_leaf = lax.dynamic_slice(parent, (0, strip * 32), (1, 32))
    return move[0].reshape(1, 2, 1, 128), parent_at_leaf, step[0]


def solution(mesh):
    return jax.shard_map(
        body,
        mesh=mesh,
        in_specs=(
            P("scen", "tm", "space", None, None),
            P("scen", "tm", "space", None),
            P("scen", "tm", "space", None),
            P("scen", "tm", "space"),
            P("scen", "tm", "space", None, None),
            P("scen"),
            P(None, ("space", "tm"), None),
            P(None, ("space", "tm")),
            P(None, ("space", "tm"), None),
            P(),
            P(),
        ),
        out_specs=(P("scen", "tm", "space", None), P("scen", ("space", "tm")), P()),
        check_vma=False,
    )
```

time: 1410 us -> 334 us (0.24)
  waiting for transfers between devices: 506 us -> 84.7 us
  blocking collectives: 333 us -> 23.8 us
  other arithmetic: 222 us -> 5.43 us
  starting transfers between devices: 263 us -> 121 us
  Pallas kernels: 0 us -> 75.4 us
  matrix products: 26.3 us -> 0 us
  between operations: 21.4 us -> 1.86 us
    ppermute x44 -> x25, waiting for transfers between devices: 302 us -> 71.5 us  [the longest x1 24.5 us: body(): pack = lax.ppermute(pack, AXES, MOVE_OUT)]
    another operation x36 -> x2, other arithmetic: 218 us -> 0.71 us  [the longest x1 0.67 us: body(): flags = jnp.stack([half, core, column, scen % 4]).astype(jnp.int32)]
    ppermute x44 -> x25, starting transfers between devices: 263 us -> 111 us  [the longest x5 28.7 us: neighbours(): lax.ppermute(message, AXES, TO_CHIP)]
    unnamed x4 -> x0, waiting for transfers between devices: 133 us -> none
    all_gather x1 -> x0, blocking collectives: 130 us -> none  [body(): lax.all_gather(link_strip, ('space', 'tm'), axis=0, tiled=True)]
    unnamed x2 -> x0, blocking collectives: 127 us -> none
    psum x1 -> x0, blocking collectives: 75.5 us -> none  [body(): lax.psum((jnp.einsum('in,im->nm', own_link, link_solved, precision=HIGH)...]
    pallas_call x0 -> x11, Pallas kernels: none -> 75.4 us  [call(): pl.pallas_call(kernel, name=name, out_shape=[jax.ShapeDtypeStruct(s, F32)...]
  transfers between devices with their start and end apart: 47 -> 26, of which waited for: 30 -> 15; matrix products, arithmetic and copies ran while one was open for 1% -> 2% of each run, Pallas kernels for 0% -> 4%
where the time goes in v1:
time: 334 us; the launch traced here: 328 us
  starting transfers between devices  121 us (36%)
  waiting for transfers between devices  84.7 us (25%)
  Pallas kernels  75.4 us (23%)
  blocking collectives  23.8 us (7%)
  local copies, waits for them, and re-layouts  15.9 us (5%)
  other arithmetic  5.43 us (2%)
    pallas_call x11, Pallas kernels, call(): pl.pallas_call(kernel, name=name, out_shape=[jax.ShapeDtypeStruct(s, F32)...  75.4 us
    ppermute x5, starting transfers between devices, neighbours(): lax.ppermute(message, AXES, TO_CHIP)  28.7 us
    ppermute x1, waiting for transfers between devices, body(): pack = lax.ppermute(pack, AXES, MOVE_OUT)  24.5 us
    all_to_all x1, blocking collectives, body(): lax.all_to_all(jnp.broadcast_to(share[None], (16, 8, 640)), Z_AXES, 0, 0)  23.8 us
    ppermute x5, starting transfers between devices, neighbours(): lax.ppermute(message, AXES, TO_CORE)  22 us
    ppermute x5, waiting for transfers between devices, neighbours(): lax.ppermute(to_half, AXES, TO_HALF)  15.2 us
    ppermute x1, starting transfers between devices, body(): lax.ppermute(coupling[0].reshape(256, 512).astype(F32), AXES, MOVE_OUT)  13.4 us
    all_to_all x1, waiting for transfers between devices, body(): shares = lax.all_to_all(quarter_sum.reshape(16, 8, 384), Z_AXES, 0, 0)  13.1 us
  transfers between devices with their start and end apart: 26, of which 15 were waited for; matrix products, arithmetic and copies ran while one was open for 2% of the time, Pallas kernels for 4%

profile of v1, /device:TPU:1, one launch (start us, length us, event | category | flops | bytes accessed | tf_op | source)
XLA Modules:
  0.0 327.9 jit_solution(9837395846521975696)
XLA Ops:
  1.7 13.4 %collective-permute-start.1 = (f32[256,512]{1,0:T(8,128)S(1)}, f32[256,512]{1,0:T(8,128)S(1)}, u32[]{:S(2)}, u32[]{:S(2)}) collective-permute-start(f32[256,512]{1,0:T(8,128)S(1)} %bitcast_convert_fusion), channel_id=1, source_target_pairs={{0,10},{2,26},{4,8},{6,24},{8,6},{10,22},{12,4},{14,20},{1,42},{3,... | collective-permute-start | bytes 1572872 | tf_op jit(solution)/shard_map/ppermute | solution.py:373
  19.5 24.5 %collective-permute-done.pack = f32[264,128]{1,0:T(8,128)S(1)} collective-permute-done((f32[264,128]{1,0:T(8,128)S(1)}, f32[264,128]{1,0:T(8,128)S(1)}, u32[]{:S(2)}, u32[]{:S(2)}) %collective-permute-start) | collective-permute-done | bytes 135200 | tf_op jit(solution)/shard_map/ppermute | solution.py:372
  44.6 10.4 %invert.1 = (f32[256,128]{1,0:T(8,128)}, f32[256,128]{1,0:T(8,128)}, f32[256,128]{1,0:T(8,128)}) custom-call(f32[264,128]{1,0:T(8,128)} %copy-done.1), custom_call_target="tpu_custom_call" | custom-call | tf_op jit(solution)/shard_map/invert/pallas_call | solution.py:97
  59.1 8.1 %collective-permute-start.2 = (f32[264,512]{1,0:T(8,128)}, f32[264,512]{1,0:T(8,128)S(1)}, u32[]{:S(2)}, u32[]{:S(2)}) collective-permute-start(f32[264,512]{1,0:T(8,128)} %get-tuple-element.38.own.own0), channel_id=1, source_target_pairs={{10,26},{26,10},{8,24},{24,8},{6,22},{22,6},{4,20},{20,4},{42,58},... | collective-permute-start | bytes 1622024 | tf_op jit(solution)/shard_map/ppermute | solution.py:342
  67.2 12.5 %collective-permute-start.3 = (f32[264,512]{1,0:T(8,128)}, f32[264,512]{1,0:T(8,128)S(1)}, u32[]{:S(2)}, u32[]{:S(2)}) collective-permute-start(f32[264,512]{1,0:T(8,128)} %get-tuple-element.38.own.own0), channel_id=1, source_target_pairs={{26,8},{8,26},{24,6},{6,24},{22,4},{4,22},{58,40},{40,58},{56,38},... | collective-permute-start | bytes 1622024 | tf_op jit(solution)/shard_map/ppermute | solution.py:343
  81.6 5.6 %collective-permute-done.4.other = f32[136,512]{1,0:T(8,128)S(1)} collective-permute-done((f32[136,512]{1,0:T(8,128)}, f32[136,512]{1,0:T(8,128)S(1)}, u32[]{:S(2)}, u32[]{:S(2)}) %collective-permute-start.4) | collective-permute-done | bytes 278560 | tf_op jit(solution)/shard_map/ppermute | solution.py:344
  93.4 5.9 %collective-permute-start.6 = (f32[264,512]{1,0:T(8,128)}, f32[264,512]{1,0:T(8,128)S(1)}, u32[]{:S(2)}, u32[]{:S(2)}) collective-permute-start(f32[264,512]{1,0:T(8,128)} %get-tuple-element.43.own), channel_id=1, source_target_pairs={{26,8},{8,26},{24,6},{6,24},{22,4},{4,22},{58,40},{40,58},{56,38},... | collective-permute-start | bytes 1622024 | tf_op jit(solution)/shard_map/ppermute | solution.py:343
  101.2 5.6 %collective-permute-done.7.other = f32[136,512]{1,0:T(8,128)S(1)} collective-permute-done((f32[136,512]{1,0:T(8,128)}, f32[136,512]{1,0:T(8,128)S(1)}, u32[]{:S(2)}, u32[]{:S(2)}) %collective-permute-start.7) | collective-permute-done | bytes 278560 | tf_op jit(solution)/shard_map/ppermute | solution.py:344
  113.5 5.1 %collective-permute-start.9 = (f32[264,512]{1,0:T(8,128)}, f32[264,512]{1,0:T(8,128)S(1)}, u32[]{:S(2)}, u32[]{:S(2)}) collective-permute-start(f32[264,512]{1,0:T(8,128)} %get-tuple-element.45.own2), channel_id=1, source_target_pairs={{26,8},{8,26},{24,6},{6,24},{22,4},{4,22},{58,40},{40,58},{56,38},... | collective-permute-start | bytes 1622024 | tf_op jit(solution)/shard_map/ppermute | solution.py:343
  141.9 5.2 %collective-permute-done.12 = f32[128,384]{1,0:T(8,128)S(1)} collective-permute-done((f32[128,384]{1,0:T(8,128)}, f32[128,384]{1,0:T(8,128)S(1)}, u32[]{:S(2)}, u32[]{:S(2)}) %collective-permute-start.12) | collective-permute-done | bytes 196640 | tf_op jit(solution)/shard_map/ppermute | solution.py:417
  148.7 10.0 %all-to-all-start = ((f32[16,8,384]{2,1,0:T(8,128)}), f32[16,8,384]{2,1,0:T(8,128)S(1)}, u32[]{:S(2)}, u32[]{:S(2)}) async-start(f32[16,8,384]{2,1,0:T(8,128)} %add_bitcast_fusion), calls=%async_computation | async-start | bytes 393216 | tf_op jit(solution)/shard_map/all_to_all | solution.py:418
  159.5 13.1 %all-to-all-done = f32[16,8,384]{2,1,0:T(8,128)S(1)} async-done(((f32[16,8,384]{2,1,0:T(8,128)}), f32[16,8,384]{2,1,0:T(8,128)S(1)}, u32[]{:S(2)}, u32[]{:S(2)}) %all-to-all-start) | async-done | bytes 196640 | tf_op jit(solution)/shard_map/all_to_all | solution.py:418
  172.7 23.8 %all_to_all.10.mine = f32[16,8,640]{2,1,0:T(8,128)S(1)} all-to-all(f32[16,8,640]{2,1,0:T(8,128)S(1)} %broadcast_in_dim.22), channel_id=1, replica_groups=mesh['scen'=32,'space'=8,'tm'=2] {'space','tm'}, dimensions={0} | all-to-all | bytes 655360 | tf_op jit(solution)/shard_map/all_to_all | solution.py:420
  199.1 5.2 %collective-permute-done.13.across_x = f32[16,8,640]{2,1,0:T(8,128)S(1)} collective-permute-done((f32[16,8,640]{2,1,0:T(8,128)S(1)}, f32[16,8,640]{2,1,0:T(8,128)S(1)}, u32[]{:S(2)}, u32[]{:S(2)}) %collective-permute-start.13) | collective-permute-done | bytes 327712 | tf_op jit(solution)/shard_map/ppermute | solution.py:421
  205.0 9.2 %collective-permute-start.14 = (f32[2,16,8,640]{3,2,1,0:T(8,128)S(1)}, f32[2,16,8,640]{3,2,1,0:T(8,128)S(1)}, u32[]{:S(2)}, u32[]{:S(2)}) collective-permute-start(f32[2,16,8,640]{3,2,1,0:T(8,128)S(1)} %pad_maximum_fusion), channel_id=1, source_target_pairs={{0,16},{16,0},{32,48},{48,32},{64,80},{80,64},{96,112},{112,96},{1... | collective-permute-start | bytes 1966088 | tf_op jit(solution)/shard_map/ppermute | solution.py:422
  216.6 25.3 %parent.1 = (f32[264,256]{1,0:T(8,128)}, f32[384,512]{1,0:T(8,128)}, f32[512,256]{1,0:T(8,128)}, f32[8,512]{1,0:T(8,128)}) custom-call(s32[4]{0:T(128)} %pad_add_fusion.flags, f32[16,8,640]{2,1,0:T(8,128)} %copy-done.3, f32[16,8,640]{2,1,0:T(8,128)} %copy-done.4, f32[2,16,8,640]{3,2,1,0:T(8,128)} %copy-done.6), custom_call_target="tpu_custom_call" | custom-call | tf_op jit(solution)/shard_map/parent/pallas_call | solution.py:97
  241.9 4.6 %collective-permute-start.15 = (f32[264,256]{1,0:T(8,128)}, f32[264,256]{1,0:T(8,128)S(1)}, u32[]{:S(2)}, u32[]{:S(2)}) collective-permute-start(f32[264,256]{1,0:T(8,128)} %get-tuple-element.52), channel_id=1, source_target_pairs={{0,64},{16,80},{32,96},{48,112},{64,0},{80,16},{96,32},{112,48},{1... | collective-permute-start | bytes 811016 | tf_op jit(solution)/shard_map/ppermute | solution.py:432
  246.5 6.6 %collective-permute-done.15 = f32[264,256]{1,0:T(8,128)S(1)} collective-permute-done((f32[264,256]{1,0:T(8,128)}, f32[264,256]{1,0:T(8,128)S(1)}, u32[]{:S(2)}, u32[]{:S(2)}) %collective-permute-start.15) | collective-permute-done | bytes 270368 | tf_op jit(solution)/shard_map/ppermute | solution.py:432
  257.4 5.5 %collective-permute-done.16 = f32[264,256]{1,0:T(8,128)S(1)} collective-permute-done((f32[264,256]{1,0:T(8,128)S(1)}, f32[264,256]{1,0:T(8,128)S(1)}, u32[]{:S(2)}, u32[]{:S(2)}) %collective-permute-start.16) | collective-permute-done | bytes 270368 | tf_op jit(solution)/shard_map/ppermute | solution.py:433
  262.9 4.8 %collective-permute-start.17 = (f32[264,256]{1,0:T(8,128)S(1)}, f32[264,256]{1,0:T(8,128)S(1)}, u32[]{:S(2)}, u32[]{:S(2)}) collective-permute-start(f32[264,256]{1,0:T(8,128)S(1)} %add.84.mine), channel_id=1, source_target_pairs={{0,256},{16,272},{32,288},{48,304},{64,320},{80,336},{96,352},{112... | collective-permute-start | bytes 811016 | tf_op jit(solution)/shard_map/ppermute | solution.py:438
  267.7 4.5 %collective-permute-done.17.theirs = f32[264,256]{1,0:T(8,128)S(1)} collective-permute-done((f32[264,256]{1,0:T(8,128)S(1)}, f32[264,256]{1,0:T(8,128)S(1)}, u32[]{:S(2)}, u32[]{:S(2)}) %collective-permute-start.17) | collective-permute-done | bytes 270368 | tf_op jit(solution)/shard_map/ppermute | solution.py:438
  273.5 16.3 %root.1 = (f32[8,256]{1,0:T(8,128)}, f32[8,512]{1,0:T(8,128)}, f32[8,256]{1,0:T(8,128)}, f32[8,256]{1,0:T(8,128)}, f32[8,128]{1,0:T(8,128)}) custom-call(s32[4]{0:T(128)} %pad_add_fusion.flags, f32[264,256]{1,0:T(8,128)} %copy-done.5, f32[264,256]{1,0:T(8,128)} %copy-done.17, f32[256,256]{1,0:T(8,128)} %matrix.1, f32[8,256]{1,0:T(8,128)} %broadcast_in_dim.23.right, ...), custom_call_target="tpu_custom_call" | custom-call | tf_op jit(solution)/shard_map/root/pallas_call | solution.py:97
  289.8 4.8 %collective-permute-start.18 = (f32[8,256]{1,0:T(8,128)}, f32[8,256]{1,0:T(8,128)S(1)}, u32[]{:S(2)}, u32[]{:S(2)}) collective-permute-start(f32[8,256]{1,0:T(8,128)} %get-tuple-element.58.own), channel_id=1, source_target_pairs={{10,26},{26,10},{8,24},{24,8},{6,22},{22,6},{4,20},{20,4},{42,58},... | collective-permute-start | bytes 24584 | tf_op jit(solution)/shard_map/ppermute | solution.py:342
  304.9 5.3 %collective-permute-start.21 = (f32[8,256]{1,0:T(8,128)}, f32[8,256]{1,0:T(8,128)S(1)}, u32[]{:S(2)}, u32[]{:S(2)}) collective-permute-start(f32[8,256]{1,0:T(8,128)} %get-tuple-element.61.own), channel_id=1, source_target_pairs={{10,26},{26,10},{8,24},{24,8},{6,22},{22,6},{4,20},{20,4},{42,58},... | collective-permute-start | bytes 24584 | tf_op jit(solution)/shard_map/ppermute | solution.py:342
  (123 shorter events, 90.8 us)
Async XLA Ops:
  1.7 53.2 %collective-permute-start.1 = (f32[256,512]{1,0:T(8,128)S(1)}, f32[256,512]{1,0:T(8,128)S(1)}, u32[]{:S(2)}, u32[]{:S(2)}) collective-permute-start(f32[256,512]{1,0:T(8,128)S(1)} %bitcast_convert_fusion), channel_id=1, source_target_pairs={{0,10},{2,26},{4,8},{6,24},{8,6},{10,22},{12,4},{14,20},{1,42},{3,... | collective-permute-start | bytes 1572872 | tf_op jit(solution)/shard_map/ppermute | solution.py:373
  16.8 27.2 %collective-permute-start = (f32[264,128]{1,0:T(8,128)S(1)}, f32[264,128]{1,0:T(8,128)S(1)}, u32[]{:S(2)}, u32[]{:S(2)}) collective-permute-start(f32[264,128]{1,0:T(8,128)S(1)} %maximum_maximum_fusion), channel_id=1, source_target_pairs={{0,10},{2,26},{4,8},{6,24},{8,6},{10,22},{12,4},{14,20},{1,42},{3,... | collective-permute-start | bytes 405512 | tf_op jit(solution)/shard_map/ppermute | solution.py:372
  59.1 28.1 %collective-permute-start.2 = (f32[264,512]{1,0:T(8,128)}, f32[264,512]{1,0:T(8,128)S(1)}, u32[]{:S(2)}, u32[]{:S(2)}) collective-permute-start(f32[264,512]{1,0:T(8,128)} %get-tuple-element.38.own.own0), channel_id=1, source_target_pairs={{10,26},{26,10},{8,24},{24,8},{6,22},{22,6},{4,20},{20,4},{42,58},... | collective-permute-start | bytes 1622024 | tf_op jit(solution)/shard_map/ppermute | solution.py:342
  67.2 20.1 %collective-permute-start.3 = (f32[264,512]{1,0:T(8,128)}, f32[264,512]{1,0:T(8,128)S(1)}, u32[]{:S(2)}, u32[]{:S(2)}) collective-permute-start(f32[264,512]{1,0:T(8,128)} %get-tuple-element.38.own.own0), channel_id=1, source_target_pairs={{26,8},{8,26},{24,6},{6,24},{22,4},{4,22},{58,40},{40,58},{56,38},... | collective-permute-start | bytes 1622024 | tf_op jit(solution)/shard_map/ppermute | solution.py:343
  79.7 7.5 %collective-permute-start.4 = (f32[136,512]{1,0:T(8,128)}, f32[136,512]{1,0:T(8,128)S(1)}, u32[]{:S(2)}, u32[]{:S(2)}) collective-permute-start(f32[136,512]{1,0:T(8,128)} %get-tuple-element.39), channel_id=1, source_target_pairs={{10,42},{26,58},{8,40},{24,56},{6,38},{22,54},{4,36},{20,52},{42,1... | collective-permute-start | bytes 835592 | tf_op jit(solution)/shard_map/ppermute | solution.py:344
  91.5 15.3 %collective-permute-start.5 = (f32[264,512]{1,0:T(8,128)}, f32[264,512]{1,0:T(8,128)S(1)}, u32[]{:S(2)}, u32[]{:S(2)}) collective-permute-start(f32[264,512]{1,0:T(8,128)} %get-tuple-element.43.own), channel_id=1, source_target_pairs={{10,26},{26,10},{8,24},{24,8},{6,22},{22,6},{4,20},{20,4},{42,58},... | collective-permute-start | bytes 1622024 | tf_op jit(solution)/shard_map/ppermute | solution.py:342
  93.4 13.4 %collective-permute-start.6 = (f32[264,512]{1,0:T(8,128)}, f32[264,512]{1,0:T(8,128)S(1)}, u32[]{:S(2)}, u32[]{:S(2)}) collective-permute-start(f32[264,512]{1,0:T(8,128)} %get-tuple-element.43.own), channel_id=1, source_target_pairs={{26,8},{8,26},{24,6},{6,24},{22,4},{4,22},{58,40},{40,58},{56,38},... | collective-permute-start | bytes 1622024 | tf_op jit(solution)/shard_map/ppermute | solution.py:343
  99.3 7.5 %collective-permute-start.7 = (f32[136,512]{1,0:T(8,128)}, f32[136,512]{1,0:T(8,128)S(1)}, u32[]{:S(2)}, u32[]{:S(2)}) collective-permute-start(f32[136,512]{1,0:T(8,128)} %get-tuple-element.44), channel_id=1, source_target_pairs={{10,42},{26,58},{8,40},{24,56},{6,38},{22,54},{4,36},{20,52},{42,1... | collective-permute-start | bytes 835592 | tf_op jit(solution)/shard_map/ppermute | solution.py:344
  111.6 15.3 %collective-permute-start.8 = (f32[264,512]{1,0:T(8,128)}, f32[264,512]{1,0:T(8,128)S(1)}, u32[]{:S(2)}, u32[]{:S(2)}) collective-permute-start(f32[264,512]{1,0:T(8,128)} %get-tuple-element.45.own2), channel_id=1, source_target_pairs={{10,26},{26,10},{8,24},{24,8},{6,22},{22,6},{4,20},{20,4},{42,58},... | collective-permute-start | bytes 1622024 | tf_op jit(solution)/shard_map/ppermute | solution.py:342
  113.5 13.4 %collective-permute-start.9 = (f32[264,512]{1,0:T(8,128)}, f32[264,512]{1,0:T(8,128)S(1)}, u32[]{:S(2)}, u32[]{:S(2)}) collective-permute-start(f32[264,512]{1,0:T(8,128)} %get-tuple-element.45.own2), channel_id=1, source_target_pairs={{26,8},{8,26},{24,6},{6,24},{22,4},{4,22},{58,40},{40,58},{56,38},... | collective-permute-start | bytes 1622024 | tf_op jit(solution)/shard_map/ppermute | solution.py:343
  118.7 8.2 %collective-permute-start.10 = (f32[136,512]{1,0:T(8,128)}, f32[136,512]{1,0:T(8,128)S(1)}, u32[]{:S(2)}, u32[]{:S(2)}) collective-permute-start(f32[136,512]{1,0:T(8,128)} %get-tuple-element.47), channel_id=1, source_target_pairs={{10,42},{26,58},{8,40},{24,56},{6,38},{22,54},{4,36},{20,52},{42,1... | collective-permute-start | bytes 835592 | tf_op jit(solution)/shard_map/ppermute | solution.py:344
  138.6 8.4 %collective-permute-start.12 = (f32[128,384]{1,0:T(8,128)}, f32[128,384]{1,0:T(8,128)S(1)}, u32[]{:S(2)}, u32[]{:S(2)}) collective-permute-start(f32[128,384]{1,0:T(8,128)} %get-tuple-element.51), channel_id=1, source_target_pairs={{0,32},{16,48},{32,0},{48,16},{64,96},{80,112},{96,64},{112,80},{1... | collective-permute-start | bytes 589832 | tf_op jit(solution)/shard_map/ppermute | solution.py:417
  148.7 23.9 %all-to-all-start = ((f32[16,8,384]{2,1,0:T(8,128)}), f32[16,8,384]{2,1,0:T(8,128)S(1)}, u32[]{:S(2)}, u32[]{:S(2)}) async-start(f32[16,8,384]{2,1,0:T(8,128)} %add_bitcast_fusion), calls=%async_computation | async-start | bytes 393216 | tf_op jit(solution)/shard_map/all_to_all | solution.py:418
  196.5 7.8 %collective-permute-start.13 = (f32[16,8,640]{2,1,0:T(8,128)S(1)}, f32[16,8,640]{2,1,0:T(8,128)S(1)}, u32[]{:S(2)}, u32[]{:S(2)}) collective-permute-start(f32[16,8,640]{2,1,0:T(8,128)S(1)} %all_to_all.10.mine), channel_id=1, source_target_pairs={{0,32},{16,48},{32,0},{48,16},{64,96},{80,112},{96,64},{112,80},{1... | collective-permute-start | bytes 983048 | tf_op jit(solution)/shard_map/ppermute | solution.py:421
  205.0 10.7 %collective-permute-start.14 = (f32[2,16,8,640]{3,2,1,0:T(8,128)S(1)}, f32[2,16,8,640]{3,2,1,0:T(8,128)S(1)}, u32[]{:S(2)}, u32[]{:S(2)}) collective-permute-start(f32[2,16,8,640]{3,2,1,0:T(8,128)S(1)} %pad_maximum_fusion), channel_id=1, source_target_pairs={{0,16},{16,0},{32,48},{48,32},{64,80},{80,64},{96,112},{112,96},{1... | collective-permute-start | bytes 1966088 | tf_op jit(solution)/shard_map/ppermute | solution.py:422
  241.9 11.3 %collective-permute-start.15 = (f32[264,256]{1,0:T(8,128)}, f32[264,256]{1,0:T(8,128)S(1)}, u32[]{:S(2)}, u32[]{:S(2)}) collective-permute-start(f32[264,256]{1,0:T(8,128)} %get-tuple-element.52), channel_id=1, source_target_pairs={{0,64},{16,80},{32,96},{48,112},{64,0},{80,16},{96,32},{112,48},{1... | collective-permute-start | bytes 811016 | tf_op jit(solution)/shard_map/ppermute | solution.py:432
  254.1 8.7 %collective-permute-start.16 = (f32[264,256]{1,0:T(8,128)S(1)}, f32[264,256]{1,0:T(8,128)S(1)}, u32[]{:S(2)}, u32[]{:S(2)}) collective-permute-start(f32[264,256]{1,0:T(8,128)S(1)} %add.83), channel_id=1, source_target_pairs={{0,128},{16,144},{32,160},{48,176},{64,192},{80,208},{96,224},{112... | collective-permute-start | bytes 811016 | tf_op jit(solution)/shard_map/ppermute | solution.py:433
  262.9 9.3 %collective-permute-start.17 = (f32[264,256]{1,0:T(8,128)S(1)}, f32[264,256]{1,0:T(8,128)S(1)}, u32[]{:S(2)}, u32[]{:S(2)}) collective-permute-start(f32[264,256]{1,0:T(8,128)S(1)} %add.84.mine), channel_id=1, source_target_pairs={{0,256},{16,272},{32,288},{48,304},{64,320},{80,336},{96,352},{112... | collective-permute-start | bytes 811016 | tf_op jit(solution)/shard_map/ppermute | solution.py:438
  289.8 12.7 %collective-permute-start.18 = (f32[8,256]{1,0:T(8,128)}, f32[8,256]{1,0:T(8,128)S(1)}, u32[]{:S(2)}, u32[]{:S(2)}) collective-permute-start(f32[8,256]{1,0:T(8,128)} %get-tuple-element.58.own), channel_id=1, source_target_pairs={{10,26},{26,10},{8,24},{24,8},{6,22},{22,6},{4,20},{20,4},{42,58},... | collective-permute-start | bytes 24584 | tf_op jit(solution)/shard_map/ppermute | solution.py:342
  294.6 7.9 %collective-permute-start.19 = (f32[8,256]{1,0:T(8,128)}, f32[8,256]{1,0:T(8,128)S(1)}, u32[]{:S(2)}, u32[]{:S(2)}) collective-permute-start(f32[8,256]{1,0:T(8,128)} %get-tuple-element.58.own), channel_id=1, source_target_pairs={{26,8},{8,26},{24,6},{6,24},{22,4},{4,22},{58,40},{40,58},{56,38},... | collective-permute-start | bytes 24584 | tf_op jit(solution)/shard_map/ppermute | solution.py:343
  297.9 4.6 %collective-permute-start.20 = (f32[8,128]{1,0:T(8,128)}, f32[8,128]{1,0:T(8,128)S(1)}, u32[]{:S(2)}, u32[]{:S(2)}) collective-permute-start(f32[8,128]{1,0:T(8,128)} %get-tuple-element.59), channel_id=1, source_target_pairs={{10,42},{26,58},{8,40},{24,56},{6,38},{22,54},{4,36},{20,52},{42,1... | collective-permute-start | bytes 12296 | tf_op jit(solution)/shard_map/ppermute | solution.py:344
  304.9 11.8 %collective-permute-start.21 = (f32[8,256]{1,0:T(8,128)}, f32[8,256]{1,0:T(8,128)S(1)}, u32[]{:S(2)}, u32[]{:S(2)}) collective-permute-start(f32[8,256]{1,0:T(8,128)} %get-tuple-element.61.own), channel_id=1, source_target_pairs={{10,26},{26,10},{8,24},{24,8},{6,22},{22,6},{4,20},{20,4},{42,58},... | collective-permute-start | bytes 24584 | tf_op jit(solution)/shard_map/ppermute | solution.py:342
  310.2 6.5 %collective-permute-start.22 = (f32[8,256]{1,0:T(8,128)}, f32[8,256]{1,0:T(8,128)S(1)}, u32[]{:S(2)}, u32[]{:S(2)}) collective-permute-start(f32[8,256]{1,0:T(8,128)} %get-tuple-element.61.own), channel_id=1, source_target_pairs={{26,8},{8,26},{24,6},{6,24},{22,4},{4,22},{58,40},{40,58},{56,38},... | collective-permute-start | bytes 24584 | tf_op jit(solution)/shard_map/ppermute | solution.py:343
  319.2 8.2 %collective-permute-start.24 = (f32[8,256]{1,0:T(8,128)}, f32[8,256]{1,0:T(8,128)S(1)}, u32[]{:S(2)}, u32[]{:S(2)}) collective-permute-start(f32[8,256]{1,0:T(8,128)} %finish.1), channel_id=1, source_target_pairs={{10,0},{26,2},{8,4},{24,6},{6,8},{22,10},{4,12},{20,14},{42,1},{58... | collective-permute-start | bytes 24584 | tf_op jit(solution)/shard_map/ppermute | solution.py:456
  (31 other events, 234.0 us)

commit v2 on v1

--- a/solution.py
+++ b/solution.py
@@ -63,18 +63,26 @@
 
 
 def sweep8(matrix, lane, sub):
-    top = matrix[:8]
     columns = [jnp.broadcast_to(matrix[:, k : k + 1], (128, 128)) for k in range(8)]
     small = [c[:8] for c in columns]
-    rows = jnp.where(lane < 8, (sub == lane).astype(F32), top)
-    for k in range(8):
-        scale = 1.0 / small[k][k : k + 1]
-        pivot_row = rows[k : k + 1] * scale
-        factor = jnp.where(sub == k, 0.0, small[k])
-        rows = jnp.where(sub == k, pivot_row, rows - factor * pivot_row)
-        for j in range(k + 1, 8):
-            entry = small[j][k : k + 1] * scale
-            small[j] = jnp.where(sub == k, entry, small[j] - factor * entry)
+    rows = jnp.where(lane < 8, (sub == lane).astype(F32), matrix[:8])
+    for k in range(0, 8, 2):
+        a, b, c = small[k][k : k + 1], small[k][k + 1 : k + 2], small[k + 1][k + 1 : k + 2]
+        scale = 1.0 / (a * c - b * b)
+        a, b, c = a * scale, b * scale, c * scale
+        here, after, pair = sub == k, sub == k + 1, (sub == k) | (sub == k + 1)
+        left = jnp.where(here, -1.0, jnp.where(after, 0.0, small[k]))
+        next_left = jnp.where(after, -1.0, jnp.where(here, 0.0, small[k + 1]))
+
+        def eliminate(panel):
+            one, two = panel[k : k + 1], panel[k + 1 : k + 2]
+            first = c * one - b * two
+            second = a * two - b * one
+            return (jnp.where(pair, 0.0, panel) - left * first) - next_left * second
+
+        for j in range(k + 2, 8):
+            small[j] = eliminate(small[j])
+        rows = eliminate(rows)
     rest = jnp.where(lane < 8, 0.0, matrix[8:])
     for k in range(8):
         rest = rest - columns[k][8:] * rows[k : k + 1]
@@ -104,15 +112,11 @@
     )(*operands)
 
 
-def invert_kernel(pack, inverse, scaled, half_scaled):
-    found = inverses([pack[0:128], pack[128:256]])
-    for t in range(2):
-        across = jnp.broadcast_to(pack[258 + t : 259 + t], (128, 128))
-        down = across.T
-        rows = slice(t * 128, t * 128 + 128)
-        inverse[rows] = found[t]
-        half_scaled[rows] = down * found[t]
-        scaled[rows] = down * found[t] * across
+def invert_kernel(blocks, rows, pack):
+    found = inverses([blocks[0:128], blocks[128:256]])
+    pack[0:128] = found[0]
+    pack[128:256] = found[1]
+    pack[256:264] = rows[...]
 
 
 def put_rows(out, first, second):
@@ -128,14 +132,20 @@
     out[128:129, 0:128] = jnp.where(early, rows[1], rows[0])
 
 
-def start_kernel(flags, pack, inverse, half_scaled, coupling, first, message, to_half):
+def start_kernel(flags, pack, coupling, first, scaled, message, to_half):
     blocks, rows = [], []
     for t in range(2):
         at = slice(t * 128, t * 128 + 128)
-        first[at] = dot(inverse[at], coupling[at])
-        blocks.append(dot(half_scaled[at], coupling[at]))
+        weight = pack[258 + t : 259 + t]
+        across = jnp.broadcast_to(weight, (128, 128))
+        down = across.T
+        inverse = pack[at]
+        scaled[at] = down * inverse * across
+        field = dot(inverse, coupling[at])
+        first[at] = field
+        blocks.append(jnp.concatenate([down] * 4, axis=1) * field)
         message[at] = blocks[t]
-        rows.append(dot(pack[256 + t : 257 + t], half_scaled[at], NT))
+        rows.append(dot(pack[256 + t : 257 + t], inverse) * weight)
     put_rows(message, *rows)
     put_half(flags[0], to_half, blocks, rows)
 
@@ -166,6 +176,37 @@
     put_rows(near, *rows)
     put_rows(message, *new_rows)
     put_half(flags[0], to_half, new, new_rows)
+
+
+def apply_kernel(flags, scaled, near, message, to_half):
+    new, new_rows = [], []
+    for t in range(2):
+        at = slice(t * 128, t * 128 + 128)
+        new.append(dot(scaled[at], near[at]))
+        message[at] = new[t]
+        new_rows.append(dot(near[256:257, at], scaled[at]))
+    put_rows(message, *new_rows)
+    put_half(flags[0], to_half, new, new_rows)
+
+
+def total_kernel(flags, near0, near1, near2, near3, own, core, chip, other, total):
+    blocks, rows = beside(flags[0], own, core, chip, other)
+    for t in range(2):
+        at = slice(t * 128, t * 128 + 128)
+        total[at] = ((near0[at] + near1[at]) + (near2[at] + near3[at])) + blocks[t]
+        rows[t] = rows[t] + ((near0[256:257, at] + near1[256:257, at]) + (near2[256:257, at] + near3[256:257, at]))
+    put_rows(total, *rows)
+
+
+def leaf_kernel(pack, coupling, total, solved, pulled):
+    for t in range(2):
+        at = slice(t * 128, t * 128 + 128)
+        weight = pack[258 + t : 259 + t]
+        down = jnp.broadcast_to(weight, (128, 128)).T
+        source = coupling[at].astype(F32) + jnp.concatenate([down] * 4, axis=1) * total[at]
+        solved[at] = dot(pack[at], source)
+        row = dot(pack[256 + t : 257 + t] + weight * total[256:257, at], pack[at])
+        pulled[0:8, at] = jnp.broadcast_to(row, (8, 128))
 
 
 def ring_columns(ref, b, count):
@@ -265,25 +306,26 @@
             upper[b * 128 : b * 128 + 128, i * 128 : i * 128 + 128] = wide[:, skip : skip + 128]
         part = part + dot(rhs[b], done, TN)
         part_row = part_row + dot(row, rhs[b])
-    root_part[0:256] = part
-    root_part[256:264] = jnp.broadcast_to(part_row, (8, 256))
+    root_part[0:128] = part[0:128, 0:128]
+    root_part[128:256] = part[0:128, 128:256]
+    root_part[256:384] = part[128:256, 128:256]
+    root_part[384:388] = jnp.broadcast_to(part_row[:, 0:128], (4, 128))
+    root_part[388:392] = jnp.broadcast_to(part_row[:, 128:256], (4, 128))
 
 
 def root_kernel(
-    flags, mine, theirs, matrix, right, upper, solved, solved_row, pack, coupling, near0, near1, near2, scaled,
-    step, parent, source, message, to_half,
+    flags, mine, opposite, below, above, matrix, right, upper, solved, solved_row, leaf_solved, pulled, step, parent, move,
 ):
-    total = matrix[...] + (mine[0:256] + theirs[0:256])
-    vector = right[0:1] - (mine[256:257] + theirs[256:257])
-    side = total[0:128, 128:256]
-    (first,) = inverses([total[0:128, 0:128]])
+    part = (mine[...] + opposite[...]) + (below[...] + above[...])
+    side = matrix[0:128, 128:256] + part[128:256]
+    (first,) = inverses([matrix[0:128, 0:128] + part[0:128]])
     pushed = dot(first, side)
-    (second,) = inverses([total[128:256, 128:256] - dot(side, pushed, TN)])
-    head = dot(vector[:, 0:128], first)
-    tail = dot(vector[:, 128:256] - dot(head, side), second)
+    (second,) = inverses([matrix[128:256, 128:256] + part[256:384] - dot(side, pushed, TN)])
+    head = dot(right[0:1, 0:128] - part[384:385], first)
+    tail = dot(right[0:1, 128:256] - part[388:389] - dot(head, side), second)
     head = head - dot(tail, pushed, NT)
     root = jnp.concatenate([head, tail], axis=1)
-    step[...] = jnp.broadcast_to(root, (8, 256))
+    step[...] = root
     pieces = [None] * 4
     for b in range(3, -1, -1):
         at = slice(b * 128, b * 128 + 128)
@@ -291,50 +333,15 @@
         for j in range(b + 1, 4):
             value = value - dot(pieces[j], upper[at, j * 128 : j * 128 + 128], NT)
         pieces[b] = value
+    chosen = jnp.zeros((1, 128), F32)
+    for b in range(4):
+        chosen = chosen + jnp.where(flags[4] == b, pieces[b], 0.0)
+    chosen = pltpu.roll(jnp.broadcast_to(chosen, (8, 128)), flags[5], 1)
+    parent[...] = chosen[0:1, 0:32]
     whole = jnp.concatenate(pieces, axis=1)
-    parent[...] = jnp.broadcast_to(whole, (8, 512))
-    source_rows, message_rows = [], []
-    for t in range(2):
-        at = slice(t * 128, t * 128 + 128)
-        last = near2[256:257, at] - dot(whole, near2[at], NT)
-        early = near0[256:257, at] + near1[256:257, at] - dot(whole, near0[at] + near1[at], NT)
-        weight = pack[258 + t : 259 + t]
-        source_rows.append(pack[256 + t : 257 + t] - dot(whole, coupling[at], NT) + weight * (early + last))
-        message_rows.append(dot(last, scaled[at]))
-    source[...] = jnp.broadcast_to(jnp.concatenate(source_rows, axis=1), (8, 256))
-    message[...] = jnp.broadcast_to(jnp.concatenate(message_rows, axis=1), (8, 256))
-    other = jnp.where(flags[0] == 0, message_rows[1], message_rows[0])
-    to_half[...] = jnp.broadcast_to(other, (8, 128))
-
-
-def beside_rows(half, own, core, chip, other):
-    late = (half == 1).astype(F32)
-    weights = (late, 1.0 - late)
-    rows = []
-    for t in range(2):
-        at = slice(t * 128, t * 128 + 128)
-        back = slice(128 - t * 128, 256 - t * 128)
-        rows.append(own[0:1, back] + core[0:1, at] + chip[0:1, at] + other[0:1] * weights[t])
-    return rows
-
-
-def vector_kernel(flags, pack, scaled, source, own, core, chip, other, new_source, message, to_half):
-    rows = beside_rows(flags[0], own, core, chip, other)
-    new = []
-    for t in range(2):
-        at = slice(t * 128, t * 128 + 128)
-        new_source[0:8, at] = jnp.broadcast_to(source[0:1, at] + pack[258 + t : 259 + t] * rows[t], (8, 128))
-        new.append(dot(rows[t], scaled[at]))
-    message[...] = jnp.broadcast_to(jnp.concatenate(new, axis=1), (8, 256))
-    to_half[...] = jnp.broadcast_to(jnp.where(flags[0] == 0, new[1], new[0]), (8, 128))
-
-
-def finish_kernel(flags, pack, inverse, source, own, core, chip, other, out):
-    rows = beside_rows(flags[0], own, core, chip, other)
-    for t in range(2):
-        at = slice(t * 128, t * 128 + 128)
-        full = source[0:1, at] + pack[258 + t : 259 + t] * rows[t]
-        out[0:8, at] = jnp.broadcast_to(dot(full, inverse[at]), (8, 128))
+    for t in range(2):
+        at = slice(t * 128, t * 128 + 128)
+        move[t : t + 1] = pulled[0:1, at] - dot(whole, leaf_solved[at], NT)
 
 
 def neighbours(message, to_half):
@@ -357,20 +364,17 @@
     core = scen % 2
     column = (scen // 2) % 2
     half = column ^ (quarter % 2)
-    flags = jnp.stack([half, core, column, scen % 4]).astype(jnp.int32)
+    turn = (128 - (strip % 4) * 32) % 128
+    flags = jnp.stack([half, core, column, scen % 4, strip // 4, turn]).astype(jnp.int32)
 
     weight = conductance[0] * (1.0 + compressor[0].astype(F32)[..., None]) * 0.5
-    pack = jnp.concatenate(
-        [
-            blocks[0].reshape(256, 128),
-            leaf_rhs[0].reshape(2, 128),
-            weight.reshape(2, 128),
-            jnp.zeros((4, 128), F32),
-        ],
-        axis=0,
-    )
-    pack = lax.ppermute(pack, AXES, MOVE_OUT)
-    field = lax.ppermute(coupling[0].reshape(256, 512).astype(F32), AXES, MOVE_OUT)
+    own_coupling = coupling[0].reshape(256, 512)
+    rows = jnp.concatenate(
+        [leaf_rhs[0].reshape(2, 128), weight.reshape(2, 128), jnp.zeros((4, 128), F32)], axis=0
+    )
+    field = lax.ppermute(own_coupling.astype(F32), AXES, MOVE_OUT)
+    (own_pack,) = call(invert_kernel, "invert", [(264, 128)], blocks[0].reshape(256, 128), rows)
+    pack = lax.ppermute(own_pack, AXES, MOVE_OUT)
 
     label = parent_of[0]
     sibling = scen % 4
@@ -386,11 +390,8 @@
     right = lax.dynamic_update_slice(jnp.zeros((512,), F32), right, (strip * 32,)).reshape(4, 128)
     right = jnp.concatenate([right, jnp.zeros((4, 128), F32)], axis=0)
 
-    inverse, scaled, half_scaled = call(invert_kernel, "invert", [(256, 128)] * 3, pack)
-    shapes = [(256, 512), (264, 512), (136, 512)]
-    first, own0, half0 = call(
-        start_kernel, "start", shapes, flags, pack, inverse, half_scaled, field, scalars=1
-    )
+    shapes = [(256, 512), (256, 128), (264, 512), (136, 512)]
+    first, scaled, own0, half0 = call(start_kernel, "start", shapes, flags, pack, field, scalars=1)
     shapes = [(264, 512), (264, 512), (136, 512)]
     near0, own1, half1 = call(
         sweep_kernel, "sweep", shapes, flags, scaled, own0, *neighbours(own0, half0), scalars=1
@@ -410,52 +411,45 @@
         scalars=1,
         scratch=[pltpu.VMEM((2, 2, 128, 384), F32), pltpu.VMEM((256, 512), F32), pltpu.VMEM((256, 512), F32)],
     )
-
-    keep, send = call(
-        halve_kernel, "halve", [(128, 384)] * 2, flags, keep, lax.ppermute(send, "scen", flip(1)), scalars=1
-    )
+    own3, half3 = call(apply_kernel, "apply", shapes[1:], flags, scaled, near2, scalars=1)
+    around3 = neighbours(own3, half3)
+    theirs, _ = lax.optimization_barrier((lax.ppermute(send, "scen", flip(1)), own3))
+    keep, send = call(halve_kernel, "halve", [(128, 384)] * 2, flags, keep, theirs, scalars=1)
     quarter_sum = keep + lax.ppermute(send, "scen", flip(2))
     shares = lax.all_to_all(quarter_sum.reshape(16, 8, 384), Z_AXES, 0, 0)
+    near3, own4, half4 = call(sweep_kernel, "sweep", shapes, flags, scaled, own3, *around3, scalars=1)
+    around4 = neighbours(own4, half4)
+    shares, _ = lax.optimization_barrier((shares, own4))
     share = jnp.concatenate([jnp.sum(shares, axis=0) + matrix_rows, link_rows], axis=1)
     mine = lax.all_to_all(jnp.broadcast_to(share[None], (16, 8, 640)), Z_AXES, 0, 0)
+    (total,) = call(
+        total_kernel, "total", [(264, 512)], flags, near0, near1, near2, near3, own4, *around4, scalars=1
+    )
+    mine, total = lax.optimization_barrier((mine, total))
     across_x = lax.ppermute(mine, "scen", flip(2))
     across_core = lax.ppermute(jnp.stack([mine, across_x]), "scen", flip(1))
+
+    total = lax.ppermute(total, AXES, MOVE_BACK)
+    leaf_solved, pulled = call(leaf_kernel, "leaf", [(256, 512), (8, 256)], own_pack, own_coupling, total)
 
     part, upper, solved, solved_row = call(
         parent_kernel,
         "parent",
-        [(264, 256), (384, 512), (512, 256), (8, 512)],
+        [(392, 128), (384, 512), (512, 256), (8, 512)],
         flags, mine, across_x, across_core,
         scalars=1,
         scratch=[pltpu.VMEM((16, 4, 8, 640), F32)],
     )
     part = part + lax.ppermute(part, "scen", flip(4))
-    part = part + lax.ppermute(part, "scen", flip(8))
-    step, parent, source, message, to_half = call(
+    others = [lax.ppermute(part, "scen", [(i, (i + by) % 32) for i in range(32)]) for by in (16, 8, 24)]
+    step, parent, move = call(
         root_kernel,
         "root",
-        [(8, 256), (8, 512), (8, 256), (8, 256), (8, 128)],
-        flags, part, lax.ppermute(part, "scen", flip(16)), root_mat,
-        jnp.broadcast_to(root_rhs[None], (8, 256)), upper, solved, solved_row, pack, field, near0, near1, near2, scaled,
+        [(1, 256), (1, 32), (2, 128)],
+        flags, part, *others, root_mat, root_rhs.reshape(1, 256), upper, solved, solved_row, leaf_solved, pulled,
         scalars=1,
     )
-    source, message, to_half = call(
-        vector_kernel,
-        "vector",
-        [(8, 256), (8, 256), (8, 128)],
-        flags, pack, scaled, source, message, *neighbours(message, to_half),
-        scalars=1,
-    )
-    (move,) = call(
-        finish_kernel,
-        "finish",
-        [(8, 256)],
-        flags, pack, inverse, source, message, *neighbours(message, to_half),
-        scalars=1,
-    )
-    move = lax.ppermute(move, AXES, MOVE_BACK)
-    parent_at_leaf = lax.dynamic_slice(parent, (0, strip * 32), (1, 32))
-    return move[0].reshape(1, 2, 1, 128), parent_at_leaf, step[0]
+    return move.reshape(1, 2, 1, 128), parent, step.reshape(256)
 
 
 def solution(mesh):

time: 334 us -> 302 us (0.904); the launches traced: 328 us -> 300 us
  blocking collectives: 23.8 us -> 0 us
  waiting for transfers between devices: 84.7 us -> 64 us
  starting transfers between devices: 121 us -> 132 us
  Pallas kernels: 75.4 us -> 81.2 us
    all_to_all x1 -> x0, blocking collectives: 23.8 us -> none  [body(): lax.all_to_all(jnp.broadcast_to(share[None], (16, 8, 640)), Z_AXES, 0, 0)]
    ppermute x5 -> x6, waiting for transfers between devices: 35.9 us -> 15.1 us  [the longest x1 14 us: body(): pack = lax.ppermute(own_pack, AXES, MOVE_OUT)]
    all_to_all x1, waiting for transfers between devices: 13.1 us -> 0.01 us  [body(): shares = lax.all_to_all(quarter_sum.reshape(16, 8, 384), Z_AXES, 0, 0)]
    ppermute x5, waiting for transfers between devices: 15.2 us -> 26 us  [neighbours(): lax.ppermute(to_half, AXES, TO_HALF)]
    ppermute x5 -> x6, starting transfers between devices: 27.6 us -> 36.4 us  [the longest x1 13.4 us: body(): field = lax.ppermute(own_coupling.astype(F32), AXES, MOVE_OUT)]
    all_to_all x0 -> x1, starting transfers between devices: none -> 8.6 us  [body(): lax.all_to_all(jnp.broadcast_to(share[None], (16, 8, 640)), Z_AXES, 0, 0)]
    ppermute x1, starting transfers between devices: 9.18 us -> 1.91 us  [body(): across_core = lax.ppermute(jnp.stack([mine, across_x]), 'scen', flip(1))]
    pallas_call x11 -> x13, Pallas kernels: 75.4 us -> 81.2 us  [call(): pl.pallas_call(kernel, name=name, out_shape=[jax.ShapeDtypeStruct(s, F32)...]
  transfers between devices with their start and end apart: 26 -> 28, of which waited for: 15 -> 12; matrix products, arithmetic and copies ran while one was open for 2% -> 1% of each run, Pallas kernels for 4% -> 17%
where the time goes in v2:
time: 302 us; the launch traced here: 300 us
  starting transfers between devices  132 us (44%)
  Pallas kernels  81.2 us (27%)
  waiting for transfers between devices  64 us (21%)
  local copies, waits for them, and re-layouts  15.5 us (5%)
  other arithmetic  5.31 us (2%)
    pallas_call x13, Pallas kernels, call(): pl.pallas_call(kernel, name=name, out_shape=[jax.ShapeDtypeStruct(s, F32)...  81.2 us
    ppermute x5, starting transfers between devices, neighbours(): lax.ppermute(message, AXES, TO_CHIP)  32.6 us
    ppermute x5, waiting for transfers between devices, neighbours(): lax.ppermute(to_half, AXES, TO_HALF)  26 us
    ppermute x5, starting transfers between devices, neighbours(): lax.ppermute(message, AXES, TO_CORE)  18.5 us
    ppermute x1, waiting for transfers between devices, body(): pack = lax.ppermute(own_pack, AXES, MOVE_OUT)  14 us
    ppermute x1, starting transfers between devices, body(): field = lax.ppermute(own_coupling.astype(F32), AXES, MOVE_OUT)  13.4 us
    unnamed x70, local copies, waits for them, and re-layouts  12.8 us
    ppermute x3, starting transfers between devices, body(): lax.ppermute(part, 'scen', [(i, (i + by) % 32) for i in range(32)])  11.3 us
  transfers between devices with their start and end apart: 28, of which 12 were waited for; matrix products, arithmetic and copies ran while one was open for 1% of the time, Pallas kernels for 17%

profile of v2, /device:TPU:1, one launch (start us, length us, event | category | flops | bytes accessed | tf_op | source)
XLA Modules:
  0.0 300.1 jit_solution(15418268919849500080)
XLA Ops:
  1.7 13.4 %collective-permute-start.1 = (f32[256,512]{1,0:T(8,128)S(1)}, f32[256,512]{1,0:T(8,128)S(1)}, u32[]{:S(2)}, u32[]{:S(2)}) collective-permute-start(f32[256,512]{1,0:T(8,128)S(1)} %bitcast_convert_fusion), channel_id=1, source_target_pairs={{0,10},{2,26},{4,8},{6,24},{8,6},{10,22},{12,4},{14,20},{1,42},{3,... | collective-permute-start | bytes 1572872 | tf_op jit(solution)/shard_map/ppermute | solution.py:375
  17.3 10.1 %invert.1.pack = f32[264,128]{1,0:T(8,128)} custom-call(f32[256,128]{1,0:T(8,128)} %bitcast.38, f32[8,128]{1,0:T(8,128)} %maximum_maximum_fusion.rows), custom_call_target="tpu_custom_call" | custom-call | tf_op jit(solution)/shard_map/invert/pallas_call | solution.py:105
  30.1 14.0 %collective-permute-done.pack = f32[264,128]{1,0:T(8,128)S(1)} collective-permute-done((f32[264,128]{1,0:T(8,128)}, f32[264,128]{1,0:T(8,128)S(1)}, u32[]{:S(2)}, u32[]{:S(2)}) %collective-permute-start) | collective-permute-done | bytes 135200 | tf_op jit(solution)/shard_map/ppermute | solution.py:377
  48.4 8.0 %collective-permute-start.2 = (f32[264,512]{1,0:T(8,128)}, f32[264,512]{1,0:T(8,128)S(1)}, u32[]{:S(2)}, u32[]{:S(2)}) collective-permute-start(f32[264,512]{1,0:T(8,128)} %get-tuple-element.39.own.own0), channel_id=1, source_target_pairs={{10,26},{26,10},{8,24},{24,8},{6,22},{22,6},{4,20},{20,4},{42,58},... | collective-permute-start | bytes 1622024 | tf_op jit(solution)/shard_map/ppermute | solution.py:349
  56.5 12.5 %collective-permute-start.3 = (f32[264,512]{1,0:T(8,128)}, f32[264,512]{1,0:T(8,128)S(1)}, u32[]{:S(2)}, u32[]{:S(2)}) collective-permute-start(f32[264,512]{1,0:T(8,128)} %get-tuple-element.39.own.own0), channel_id=1, source_target_pairs={{26,8},{8,26},{24,6},{6,24},{22,4},{4,22},{58,40},{40,58},{56,38},... | collective-permute-start | bytes 1622024 | tf_op jit(solution)/shard_map/ppermute | solution.py:350
  70.9 5.6 %collective-permute-done.4.other = f32[136,512]{1,0:T(8,128)S(1)} collective-permute-done((f32[136,512]{1,0:T(8,128)}, f32[136,512]{1,0:T(8,128)S(1)}, u32[]{:S(2)}, u32[]{:S(2)}) %collective-permute-start.4) | collective-permute-done | bytes 278560 | tf_op jit(solution)/shard_map/ppermute | solution.py:351
  82.7 5.8 %collective-permute-start.6 = (f32[264,512]{1,0:T(8,128)}, f32[264,512]{1,0:T(8,128)S(1)}, u32[]{:S(2)}, u32[]{:S(2)}) collective-permute-start(f32[264,512]{1,0:T(8,128)} %get-tuple-element.45.own), channel_id=1, source_target_pairs={{26,8},{8,26},{24,6},{6,24},{22,4},{4,22},{58,40},{40,58},{56,38},... | collective-permute-start | bytes 1622024 | tf_op jit(solution)/shard_map/ppermute | solution.py:350
  90.4 5.6 %collective-permute-done.7.other = f32[136,512]{1,0:T(8,128)S(1)} collective-permute-done((f32[136,512]{1,0:T(8,128)}, f32[136,512]{1,0:T(8,128)S(1)}, u32[]{:S(2)}, u32[]{:S(2)}) %collective-permute-start.7) | collective-permute-done | bytes 278560 | tf_op jit(solution)/shard_map/ppermute | solution.py:351
  102.8 5.0 %collective-permute-start.9 = (f32[264,512]{1,0:T(8,128)}, f32[264,512]{1,0:T(8,128)S(1)}, u32[]{:S(2)}, u32[]{:S(2)}) collective-permute-start(f32[264,512]{1,0:T(8,128)} %get-tuple-element.47.own2), channel_id=1, source_target_pairs={{26,8},{8,26},{24,6},{6,24},{22,4},{4,22},{58,40},{40,58},{56,38},... | collective-permute-start | bytes 1622024 | tf_op jit(solution)/shard_map/ppermute | solution.py:350
  131.9 4.9 %collective-permute-done.12 = f32[128,384]{1,0:T(8,128)S(1)} collective-permute-done((f32[128,384]{1,0:T(8,128)}, f32[128,384]{1,0:T(8,128)S(1)}, u32[]{:S(2)}, u32[]{:S(2)}) %collective-permute-start.12) | collective-permute-done | bytes 196640 | tf_op jit(solution)/shard_map/ppermute | solution.py:418
  138.5 11.1 %all-to-all-start = ((f32[16,8,384]{2,1,0:T(8,128)}), f32[16,8,384]{2,1,0:T(8,128)S(1)}, u32[]{:S(2)}, u32[]{:S(2)}) async-start(f32[16,8,384]{2,1,0:T(8,128)} %add_bitcast_fusion), calls=%async_computation | async-start | bytes 393216 | tf_op jit(solution)/shard_map/all_to_all | solution.py:419
  152.7 4.7 %collective-permute-start.14 = (f32[264,512]{1,0:T(8,128)S(1)}, f32[264,512]{1,0:T(8,128)S(1)}, u32[]{:S(2)}, u32[]{:S(2)}) collective-permute-start(f32[264,512]{1,0:T(8,128)S(1)} %copy-done.12), channel_id=1, source_target_pairs={{26,8},{8,26},{24,6},{6,24},{22,4},{4,22},{58,40},{40,58},{56,38},... | collective-permute-start | bytes 1622024 | tf_op jit(solution)/shard_map/ppermute | solution.py:350
  160.9 6.9 %collective-permute-done.15.other = f32[136,512]{1,0:T(8,128)S(1)} collective-permute-done((f32[136,512]{1,0:T(8,128)S(1)}, f32[136,512]{1,0:T(8,128)S(1)}, u32[]{:S(2)}, u32[]{:S(2)}) %collective-permute-start.15) | collective-permute-done | bytes 278560 | tf_op jit(solution)/shard_map/ppermute | solution.py:351
  173.4 8.6 %all-to-all-start.1 = ((f32[16,8,640]{2,1,0:T(8,128)}), f32[16,8,640]{2,1,0:T(8,128)S(1)}, u32[]{:S(2)}, u32[]{:S(2)}) async-start(f32[16,8,640]{2,1,0:T(8,128)} %broadcast_in_dim.16), calls=%async_computation.1 | async-start | bytes 655360 | tf_op jit(solution)/shard_map/all_to_all | solution.py:424
  185.6 4.7 %collective-permute-start.17 = (f32[264,512]{1,0:T(8,128)S(1)}, f32[264,512]{1,0:T(8,128)S(1)}, u32[]{:S(2)}, u32[]{:S(2)}) collective-permute-start(f32[264,512]{1,0:T(8,128)S(1)} %copy-done.9), channel_id=1, source_target_pairs={{26,8},{8,26},{24,6},{6,24},{22,4},{4,22},{58,40},{40,58},{56,38},... | collective-permute-start | bytes 1622024 | tf_op jit(solution)/shard_map/ppermute | solution.py:350
  192.9 7.6 %collective-permute-done.18.other = f32[136,512]{1,0:T(8,128)S(1)} collective-permute-done((f32[136,512]{1,0:T(8,128)S(1)}, f32[136,512]{1,0:T(8,128)S(1)}, u32[]{:S(2)}, u32[]{:S(2)}) %collective-permute-start.18) | collective-permute-done | bytes 278560 | tf_op jit(solution)/shard_map/ppermute | solution.py:351
  200.6 5.3 %collective-permute-done.17.chip = f32[264,512]{1,0:T(8,128)S(1)} collective-permute-done((f32[264,512]{1,0:T(8,128)S(1)}, f32[264,512]{1,0:T(8,128)S(1)}, u32[]{:S(2)}, u32[]{:S(2)}) %collective-permute-start.17) | collective-permute-done | bytes 540704 | tf_op jit(solution)/shard_map/ppermute | solution.py:350
  212.5 7.8 %collective-permute-done.19.across_x = f32[16,8,640]{2,1,0:T(8,128)S(1)} collective-permute-done((f32[16,8,640]{2,1,0:T(8,128)S(1)}, f32[16,8,640]{2,1,0:T(8,128)S(1)}, u32[]{:S(2)}, u32[]{:S(2)}) %collective-permute-start.19) | collective-permute-done | bytes 327712 | tf_op jit(solution)/shard_map/ppermute | solution.py:429
  223.0 9.8 %collective-permute-start.25 = (f32[264,512]{1,0:T(8,128)S(1)}, f32[264,512]{1,0:T(8,128)S(1)}, u32[]{:S(2)}, u32[]{:S(2)}) collective-permute-start(f32[264,512]{1,0:T(8,128)S(1)} %copy-done.6), channel_id=1, source_target_pairs={{10,0},{26,2},{8,4},{24,6},{6,8},{22,10},{4,12},{20,14},{42,1},{58... | collective-permute-start | bytes 1622024 | tf_op jit(solution)/shard_map/ppermute | solution.py:432
  233.6 25.3 %parent.1 = (f32[392,128]{1,0:T(8,128)}, f32[384,512]{1,0:T(8,128)}, f32[512,256]{1,0:T(8,128)}, f32[8,512]{1,0:T(8,128)}) custom-call(s32[6]{0:T(128)} %stack.36.flags, f32[16,8,640]{2,1,0:T(8,128)} %copy-done.1, f32[16,8,640]{2,1,0:T(8,128)} %copy-done.3, f32[2,16,8,640]{3,2,1,0:T(8,128)} %copy-done.5), custom_call_target="tpu_custom_call" | custom-call | tf_op jit(solution)/shard_map/parent/pallas_call | solution.py:105
  262.9 4.6 %collective-permute-done.21 = f32[392,128]{1,0:T(8,128)S(1)} collective-permute-done((f32[392,128]{1,0:T(8,128)}, f32[392,128]{1,0:T(8,128)S(1)}, u32[]{:S(2)}, u32[]{:S(2)}) %collective-permute-start.21) | collective-permute-done | bytes 200736 | tf_op jit(solution)/shard_map/ppermute | solution.py:443
  268.5 4.8 %collective-permute-start.22 = (f32[392,128]{1,0:T(8,128)S(1)}, f32[392,128]{1,0:T(8,128)S(1)}, u32[]{:S(2)}, u32[]{:S(2)}) collective-permute-start(f32[392,128]{1,0:T(8,128)S(1)} %add.87.mine), channel_id=1, source_target_pairs={{0,256},{16,272},{32,288},{48,304},{64,320},{80,336},{96,352},{112... | collective-permute-start | bytes 602120 | tf_op jit(solution)/shard_map/ppermute | solution.py:444
  275.6 4.2 %collective-permute-start.24 = (f32[392,128]{1,0:T(8,128)S(1)}, f32[392,128]{1,0:T(8,128)S(1)}, u32[]{:S(2)}, u32[]{:S(2)}) collective-permute-start(f32[392,128]{1,0:T(8,128)S(1)} %add.87.mine), channel_id=1, source_target_pairs={{0,384},{16,400},{32,416},{48,432},{64,448},{80,464},{96,480},{112... | collective-permute-start | bytes 602120 | tf_op jit(solution)/shard_map/ppermute | solution.py:444
  285.3 14.8 %root.1 = (f32[1,256]{1,0:T(1,128)}, f32[1,32]{1,0:T(1,128)}, f32[2,128]{1,0:T(2,128)}) custom-call(s32[6]{0:T(128)} %stack.36.flags, f32[392,128]{1,0:T(8,128)} %copy-done.4, f32[392,128]{1,0:T(8,128)} %copy-done.27, f32[392,128]{1,0:T(8,128)} %copy-done.28, f32[392,128]{1,0:T(8,128)} %copy-done.29, f32[256,256]{1,0:T(8,128)} %matrix.1, f32[1,256]{1,0:T(1,128)} %bitcast.40, ...), custom_call_target="tpu_custom_call" | custom-call | tf_op jit(solution)/shard_map/root/pallas_call | solution.py:105
  (135 shorter events, 92.9 us)
Async XLA Ops:
  1.7 42.3 %collective-permute-start.1 = (f32[256,512]{1,0:T(8,128)S(1)}, f32[256,512]{1,0:T(8,128)S(1)}, u32[]{:S(2)}, u32[]{:S(2)}) collective-permute-start(f32[256,512]{1,0:T(8,128)S(1)} %bitcast_convert_fusion), channel_id=1, source_target_pairs={{0,10},{2,26},{4,8},{6,24},{8,6},{10,22},{12,4},{14,20},{1,42},{3,... | collective-permute-start | bytes 1572872 | tf_op jit(solution)/shard_map/ppermute | solution.py:375
  27.4 16.7 %collective-permute-start = (f32[264,128]{1,0:T(8,128)}, f32[264,128]{1,0:T(8,128)S(1)}, u32[]{:S(2)}, u32[]{:S(2)}) collective-permute-start(f32[264,128]{1,0:T(8,128)} %invert.1.pack), channel_id=1, source_target_pairs={{0,10},{2,26},{4,8},{6,24},{8,6},{10,22},{12,4},{14,20},{1,42},{3,... | collective-permute-start | bytes 405512 | tf_op jit(solution)/shard_map/ppermute | solution.py:377
  48.4 28.1 %collective-permute-start.2 = (f32[264,512]{1,0:T(8,128)}, f32[264,512]{1,0:T(8,128)S(1)}, u32[]{:S(2)}, u32[]{:S(2)}) collective-permute-start(f32[264,512]{1,0:T(8,128)} %get-tuple-element.39.own.own0), channel_id=1, source_target_pairs={{10,26},{26,10},{8,24},{24,8},{6,22},{22,6},{4,20},{20,4},{42,58},... | collective-permute-start | bytes 1622024 | tf_op jit(solution)/shard_map/ppermute | solution.py:349
  56.5 20.1 %collective-permute-start.3 = (f32[264,512]{1,0:T(8,128)}, f32[264,512]{1,0:T(8,128)S(1)}, u32[]{:S(2)}, u32[]{:S(2)}) collective-permute-start(f32[264,512]{1,0:T(8,128)} %get-tuple-element.39.own.own0), channel_id=1, source_target_pairs={{26,8},{8,26},{24,6},{6,24},{22,4},{4,22},{58,40},{40,58},{56,38},... | collective-permute-start | bytes 1622024 | tf_op jit(solution)/shard_map/ppermute | solution.py:350
  80.8 15.3 %collective-permute-start.5 = (f32[264,512]{1,0:T(8,128)}, f32[264,512]{1,0:T(8,128)S(1)}, u32[]{:S(2)}, u32[]{:S(2)}) collective-permute-start(f32[264,512]{1,0:T(8,128)} %get-tuple-element.45.own), channel_id=1, source_target_pairs={{10,26},{26,10},{8,24},{24,8},{6,22},{22,6},{4,20},{20,4},{42,58},... | collective-permute-start | bytes 1622024 | tf_op jit(solution)/shard_map/ppermute | solution.py:349
  82.7 13.4 %collective-permute-start.6 = (f32[264,512]{1,0:T(8,128)}, f32[264,512]{1,0:T(8,128)S(1)}, u32[]{:S(2)}, u32[]{:S(2)}) collective-permute-start(f32[264,512]{1,0:T(8,128)} %get-tuple-element.45.own), channel_id=1, source_target_pairs={{26,8},{8,26},{24,6},{6,24},{22,4},{4,22},{58,40},{40,58},{56,38},... | collective-permute-start | bytes 1622024 | tf_op jit(solution)/shard_map/ppermute | solution.py:350
  100.9 15.3 %collective-permute-start.8 = (f32[264,512]{1,0:T(8,128)}, f32[264,512]{1,0:T(8,128)S(1)}, u32[]{:S(2)}, u32[]{:S(2)}) collective-permute-start(f32[264,512]{1,0:T(8,128)} %get-tuple-element.47.own2), channel_id=1, source_target_pairs={{10,26},{26,10},{8,24},{24,8},{6,22},{22,6},{4,20},{20,4},{42,58},... | collective-permute-start | bytes 1622024 | tf_op jit(solution)/shard_map/ppermute | solution.py:349
  102.8 13.4 %collective-permute-start.9 = (f32[264,512]{1,0:T(8,128)}, f32[264,512]{1,0:T(8,128)S(1)}, u32[]{:S(2)}, u32[]{:S(2)}) collective-permute-start(f32[264,512]{1,0:T(8,128)} %get-tuple-element.47.own2), channel_id=1, source_target_pairs={{26,8},{8,26},{24,6},{6,24},{22,4},{4,22},{58,40},{40,58},{56,38},... | collective-permute-start | bytes 1622024 | tf_op jit(solution)/shard_map/ppermute | solution.py:350
  107.9 8.3 %collective-permute-start.10 = (f32[136,512]{1,0:T(8,128)}, f32[136,512]{1,0:T(8,128)S(1)}, u32[]{:S(2)}, u32[]{:S(2)}) collective-permute-start(f32[136,512]{1,0:T(8,128)} %get-tuple-element.49), channel_id=1, source_target_pairs={{10,42},{26,58},{8,40},{24,56},{6,38},{22,54},{4,36},{20,52},{42,1... | collective-permute-start | bytes 835592 | tf_op jit(solution)/shard_map/ppermute | solution.py:351
  138.5 34.1 %all-to-all-start = ((f32[16,8,384]{2,1,0:T(8,128)}), f32[16,8,384]{2,1,0:T(8,128)S(1)}, u32[]{:S(2)}, u32[]{:S(2)}) async-start(f32[16,8,384]{2,1,0:T(8,128)} %add_bitcast_fusion), calls=%async_computation | async-start | bytes 393216 | tf_op jit(solution)/shard_map/all_to_all | solution.py:419
  149.7 18.1 %collective-permute-start.13 = (f32[264,512]{1,0:T(8,128)S(1)}, f32[264,512]{1,0:T(8,128)S(1)}, u32[]{:S(2)}, u32[]{:S(2)}) collective-permute-start(f32[264,512]{1,0:T(8,128)S(1)} %copy-done.12), channel_id=1, source_target_pairs={{10,26},{26,10},{8,24},{24,8},{6,22},{22,6},{4,20},{20,4},{42,58},... | collective-permute-start | bytes 1622024 | tf_op jit(solution)/shard_map/ppermute | solution.py:349
  152.7 15.1 %collective-permute-start.14 = (f32[264,512]{1,0:T(8,128)S(1)}, f32[264,512]{1,0:T(8,128)S(1)}, u32[]{:S(2)}, u32[]{:S(2)}) collective-permute-start(f32[264,512]{1,0:T(8,128)S(1)} %copy-done.12), channel_id=1, source_target_pairs={{26,8},{8,26},{24,6},{6,24},{22,4},{4,22},{58,40},{40,58},{56,38},... | collective-permute-start | bytes 1622024 | tf_op jit(solution)/shard_map/ppermute | solution.py:350
  157.4 10.3 %collective-permute-start.15 = (f32[136,512]{1,0:T(8,128)S(1)}, f32[136,512]{1,0:T(8,128)S(1)}, u32[]{:S(2)}, u32[]{:S(2)}) collective-permute-start(f32[136,512]{1,0:T(8,128)S(1)} %copy-done.32), channel_id=1, source_target_pairs={{10,42},{26,58},{8,40},{24,56},{6,38},{22,54},{4,36},{20,52},{42,1... | collective-permute-start | bytes 835592 | tf_op jit(solution)/shard_map/ppermute | solution.py:351
  173.4 36.4 %all-to-all-start.1 = ((f32[16,8,640]{2,1,0:T(8,128)}), f32[16,8,640]{2,1,0:T(8,128)S(1)}, u32[]{:S(2)}, u32[]{:S(2)}) async-start(f32[16,8,640]{2,1,0:T(8,128)} %broadcast_in_dim.16), calls=%async_computation.1 | async-start | bytes 655360 | tf_op jit(solution)/shard_map/all_to_all | solution.py:424
  182.0 18.5 %collective-permute-start.16 = (f32[264,512]{1,0:T(8,128)S(1)}, f32[264,512]{1,0:T(8,128)S(1)}, u32[]{:S(2)}, u32[]{:S(2)}) collective-permute-start(f32[264,512]{1,0:T(8,128)S(1)} %copy-done.9), channel_id=1, source_target_pairs={{10,26},{26,10},{8,24},{24,8},{6,22},{22,6},{4,20},{20,4},{42,58},... | collective-permute-start | bytes 1622024 | tf_op jit(solution)/shard_map/ppermute | solution.py:349
  185.6 20.3 %collective-permute-start.17 = (f32[264,512]{1,0:T(8,128)S(1)}, f32[264,512]{1,0:T(8,128)S(1)}, u32[]{:S(2)}, u32[]{:S(2)}) collective-permute-start(f32[264,512]{1,0:T(8,128)S(1)} %copy-done.9), channel_id=1, source_target_pairs={{26,8},{8,26},{24,6},{6,24},{22,4},{4,22},{58,40},{40,58},{56,38},... | collective-permute-start | bytes 1622024 | tf_op jit(solution)/shard_map/ppermute | solution.py:350
  190.2 10.3 %collective-permute-start.18 = (f32[136,512]{1,0:T(8,128)S(1)}, f32[136,512]{1,0:T(8,128)S(1)}, u32[]{:S(2)}, u32[]{:S(2)}) collective-permute-start(f32[136,512]{1,0:T(8,128)S(1)} %copy-done.33), channel_id=1, source_target_pairs={{10,42},{26,58},{8,40},{24,56},{6,38},{22,54},{4,36},{20,52},{42,1... | collective-permute-start | bytes 835592 | tf_op jit(solution)/shard_map/ppermute | solution.py:351
  209.8 10.5 %collective-permute-start.19 = (f32[16,8,640]{2,1,0:T(8,128)S(1)}, f32[16,8,640]{2,1,0:T(8,128)S(1)}, u32[]{:S(2)}, u32[]{:S(2)}) collective-permute-start(f32[16,8,640]{2,1,0:T(8,128)S(1)} %all-to-all-done.1.mine), channel_id=1, source_target_pairs={{0,32},{16,48},{32,0},{48,16},{64,96},{80,112},{96,64},{112,80},{1... | collective-permute-start | bytes 983048 | tf_op jit(solution)/shard_map/ppermute | solution.py:429
  221.1 11.7 %collective-permute-start.20 = (f32[2,16,8,640]{3,2,1,0:T(8,128)S(1)}, f32[2,16,8,640]{3,2,1,0:T(8,128)S(1)}, u32[]{:S(2)}, u32[]{:S(2)}) collective-permute-start(f32[2,16,8,640]{3,2,1,0:T(8,128)S(1)} %pad_maximum_fusion), channel_id=1, source_target_pairs={{0,16},{16,0},{32,48},{48,32},{64,80},{80,64},{96,112},{112,96},{1... | collective-permute-start | bytes 1966088 | tf_op jit(solution)/shard_map/ppermute | solution.py:430
  223.0 56.8 %collective-permute-start.25 = (f32[264,512]{1,0:T(8,128)S(1)}, f32[264,512]{1,0:T(8,128)S(1)}, u32[]{:S(2)}, u32[]{:S(2)}) collective-permute-start(f32[264,512]{1,0:T(8,128)S(1)} %copy-done.6), channel_id=1, source_target_pairs={{10,0},{26,2},{8,4},{24,6},{6,8},{22,10},{4,12},{20,14},{42,1},{58... | collective-permute-start | bytes 1622024 | tf_op jit(solution)/shard_map/ppermute | solution.py:432
  258.9 8.6 %collective-permute-start.21 = (f32[392,128]{1,0:T(8,128)}, f32[392,128]{1,0:T(8,128)S(1)}, u32[]{:S(2)}, u32[]{:S(2)}) collective-permute-start(f32[392,128]{1,0:T(8,128)} %get-tuple-element.63), channel_id=1, source_target_pairs={{0,64},{16,80},{32,96},{48,112},{64,0},{80,16},{96,32},{112,48},{1... | collective-permute-start | bytes 602120 | tf_op jit(solution)/shard_map/ppermute | solution.py:443
  268.5 15.0 %collective-permute-start.22 = (f32[392,128]{1,0:T(8,128)S(1)}, f32[392,128]{1,0:T(8,128)S(1)}, u32[]{:S(2)}, u32[]{:S(2)}) collective-permute-start(f32[392,128]{1,0:T(8,128)S(1)} %add.87.mine), channel_id=1, source_target_pairs={{0,256},{16,272},{32,288},{48,304},{64,320},{80,336},{96,352},{112... | collective-permute-start | bytes 602120 | tf_op jit(solution)/shard_map/ppermute | solution.py:444
  273.3 10.1 %collective-permute-start.23 = (f32[392,128]{1,0:T(8,128)S(1)}, f32[392,128]{1,0:T(8,128)S(1)}, u32[]{:S(2)}, u32[]{:S(2)}) collective-permute-start(f32[392,128]{1,0:T(8,128)S(1)} %add.87.mine), channel_id=1, source_target_pairs={{0,128},{16,144},{32,160},{48,176},{64,192},{80,208},{96,224},{112... | collective-permute-start | bytes 602120 | tf_op jit(solution)/shard_map/ppermute | solution.py:444
  275.6 9.0 %collective-permute-start.24 = (f32[392,128]{1,0:T(8,128)S(1)}, f32[392,128]{1,0:T(8,128)S(1)}, u32[]{:S(2)}, u32[]{:S(2)}) collective-permute-start(f32[392,128]{1,0:T(8,128)S(1)} %add.87.mine), channel_id=1, source_target_pairs={{0,384},{16,400},{32,416},{48,432},{64,448},{80,464},{96,480},{112... | collective-permute-start | bytes 602120 | tf_op jit(solution)/shard_map/ppermute | solution.py:444
  (39 other events, 327.7 us)

commit v3 on v2

--- a/solution.py
+++ b/solution.py
@@ -13,7 +13,6 @@
 HIGH = lax.Precision.HIGHEST
 
 QUARTER = (0, 2, 1, 3)
-LEAF_OF_QUARTER = (0, 2, 1, 3)
 Z_SHIFT = 2
 
 
@@ -50,6 +49,13 @@
 ]
 
 
+SAME_CORE = [
+    [((group * 4 + column * 2 + core) * 8 + space) * 2 + tm for column in range(2) for space in range(8) for tm in range(2)]
+    for group in range(8)
+    for core in range(2)
+]
+
+
 def flip(bit):
     return [(i, i ^ bit) for i in range(32)]
 
@@ -62,49 +68,65 @@
 TN = ((0,), (0,))
 
 
-def sweep8(matrix, lane, sub):
-    columns = [jnp.broadcast_to(matrix[:, k : k + 1], (128, 128)) for k in range(8)]
-    small = [c[:8] for c in columns]
-    rows = jnp.where(lane < 8, (sub == lane).astype(F32), matrix[:8])
-    for k in range(0, 8, 2):
-        a, b, c = small[k][k : k + 1], small[k][k + 1 : k + 2], small[k + 1][k + 1 : k + 2]
-        scale = 1.0 / (a * c - b * b)
-        a, b, c = a * scale, b * scale, c * scale
-        here, after, pair = sub == k, sub == k + 1, (sub == k) | (sub == k + 1)
-        left = jnp.where(here, -1.0, jnp.where(after, 0.0, small[k]))
-        next_left = jnp.where(after, -1.0, jnp.where(here, 0.0, small[k + 1]))
-
-        def eliminate(panel):
-            one, two = panel[k : k + 1], panel[k + 1 : k + 2]
-            first = c * one - b * two
-            second = a * two - b * one
-            return (jnp.where(pair, 0.0, panel) - left * first) - next_left * second
-
-        for j in range(k + 2, 8):
-            small[j] = eliminate(small[j])
-        rows = eliminate(rows)
-    rest = jnp.where(lane < 8, 0.0, matrix[8:])
-    for k in range(8):
-        rest = rest - columns[k][8:] * rows[k : k + 1]
-    return jnp.concatenate([rest, rows], axis=0)
+def split(x):
+    high = x.astype(jnp.bfloat16)
+    return high, (x - high.astype(F32)).astype(jnp.bfloat16)
+
+
+def dot3(a, b, dims=((1,), (0,))):
+    (k,), (m,) = dims
+    a_high, a_low = split(a)
+    b_high, b_low = split(b)
+    plain = functools.partial(
+        lax.dot_general, dimension_numbers=(dims, ((), ())), preferred_element_type=F32
+    )
+    if a.shape[k] < 256:
+        first = plain(jnp.concatenate([a_high, a_low], axis=k), jnp.concatenate([b_high, b_high], axis=m))
+    else:
+        first = plain(a_high, b_high) + plain(a_low, b_high)
+    return first + plain(a_high, b_low)
+
+
+def eliminate(matrix, start, lane, sub):
+    stop = start + 16
+    inside = (lane >= start) & (lane < stop)
+    panel = matrix[start:stop]
+    small = [jnp.broadcast_to(panel[:, start + k : start + k + 1], (16, 128)) for k in range(16)]
+    rows = jnp.where(inside, (sub == lane - start).astype(F32), panel)
+    left = jnp.where(inside, matrix, 0.0)
+    for k in range(16):
+        scale = 1.0 / small[k][k : k + 1]
+        factor = jnp.where(sub == k, -1.0, small[k])
+
+        def step(block):
+            return jnp.where(sub == k, 0.0, block) - factor * (block[k : k + 1] * scale)
+
+        for j in range(k + 1, 16):
+            small[j] = step(small[j])
+        rows = step(rows)
+    spread = [jnp.zeros((n, 128), F32) for n in (start, 112 - start) if n]
+    spread.insert(1 if start else 0, rows)
+    rest = jnp.where(inside, 0.0, matrix) - dot(left, jnp.concatenate(spread, axis=0))
+    kept = [rest[stop:]] if stop < 128 else []
+    return jnp.concatenate(([rest[:start]] if start else []) + [rows] + kept, axis=0)
 
 
 def inverses(matrices):
     lane = lax.broadcasted_iota(jnp.int32, (1, 128), 1)
-    sub = lax.broadcasted_iota(jnp.int32, (8, 1), 0)
+    sub = lax.broadcasted_iota(jnp.int32, (16, 1), 0)
 
     def step(_, carry):
-        return tuple(pltpu.roll(sweep8(m, lane, sub), 120, 1) for m in carry)
-
-    return lax.fori_loop(0, 16, step, tuple(matrices))
-
-
-def call(kernel, name, shapes, *operands, scratch=(), scalars=0):
+        out = [eliminate(eliminate(m, 0, lane, sub), 16, lane, sub) for m in carry]
+        return tuple(pltpu.roll(jnp.concatenate([m[32:], m[:32]], axis=0), 96, 1) for m in out)
+
+    return lax.fori_loop(0, 4, step, tuple(matrices))
+
+
+def call(kernel, shapes, *operands, scratch=(), scalars=0):
     smem = pl.BlockSpec(memory_space=pltpu.SMEM)
     vmem = pl.BlockSpec(memory_space=pltpu.VMEM)
     return pl.pallas_call(
         kernel,
-        name=name,
         out_shape=[jax.ShapeDtypeStruct(s, F32) for s in shapes],
         in_specs=[smem] * scalars + [vmem] * (len(operands) - scalars),
         out_specs=[vmem] * len(shapes),
@@ -112,11 +134,20 @@
     )(*operands)
 
 
-def invert_kernel(blocks, rows, pack):
+def triangles():
+    row = lax.broadcasted_iota(jnp.int32, (128, 128), 0)
+    column = lax.broadcasted_iota(jnp.int32, (128, 128), 1)
+    return row, column
+
+
+def invert_kernel(blocks, rows, inverse, pack):
     found = inverses([blocks[0:128], blocks[128:256]])
-    pack[0:128] = found[0]
-    pack[128:256] = found[1]
-    pack[256:264] = rows[...]
+    inverse[0:128] = found[0]
+    inverse[128:256] = found[1]
+    row, column = triangles()
+    pack[0:128] = jnp.where(row >= column, found[0], found[1])
+    pack[128:136] = rows[...]
+    pack[132:133] = jnp.sum(jnp.where(row == column, found[1], 0.0), axis=0, keepdims=True)
 
 
 def put_rows(out, first, second):
@@ -133,19 +164,27 @@
 
 
 def start_kernel(flags, pack, coupling, first, scaled, message, to_half):
+    row, column = triangles()
+    packed = pack[0:128]
+    turned = packed.T
+    diagonal = jnp.broadcast_to(pack[132:133], (128, 128))
+    inverses_here = [
+        jnp.where(row >= column, packed, turned),
+        jnp.where(row < column, packed, jnp.where(row > column, turned, diagonal)),
+    ]
     blocks, rows = [], []
     for t in range(2):
         at = slice(t * 128, t * 128 + 128)
-        weight = pack[258 + t : 259 + t]
+        weight = pack[130 + t : 131 + t]
         across = jnp.broadcast_to(weight, (128, 128))
         down = across.T
-        inverse = pack[at]
+        inverse = inverses_here[t]
         scaled[at] = down * inverse * across
-        field = dot(inverse, coupling[at])
+        field = dot3(inverse, coupling[at])
         first[at] = field
         blocks.append(jnp.concatenate([down] * 4, axis=1) * field)
         message[at] = blocks[t]
-        rows.append(dot(pack[256 + t : 257 + t], inverse) * weight)
+        rows.append(dot(pack[128 + t : 129 + t], inverse) * weight)
     put_rows(message, *rows)
     put_half(flags[0], to_half, blocks, rows)
 
@@ -170,7 +209,7 @@
     for t in range(2):
         at = slice(t * 128, t * 128 + 128)
         near[at] = blocks[t]
-        new.append(dot(scaled[at], blocks[t]))
+        new.append(dot3(scaled[at], blocks[t]))
         message[at] = new[t]
         new_rows.append(dot(rows[t], scaled[at]))
     put_rows(near, *rows)
@@ -182,7 +221,7 @@
     new, new_rows = [], []
     for t in range(2):
         at = slice(t * 128, t * 128 + 128)
-        new.append(dot(scaled[at], near[at]))
+        new.append(dot3(scaled[at], near[at]))
         message[at] = new[t]
         new_rows.append(dot(near[256:257, at], scaled[at]))
     put_rows(message, *new_rows)
@@ -198,14 +237,14 @@
     put_rows(total, *rows)
 
 
-def leaf_kernel(pack, coupling, total, solved, pulled):
-    for t in range(2):
-        at = slice(t * 128, t * 128 + 128)
-        weight = pack[258 + t : 259 + t]
+def leaf_kernel(inverse, rows, coupling, total, solved, pulled):
+    for t in range(2):
+        at = slice(t * 128, t * 128 + 128)
+        weight = rows[2 + t : 3 + t]
         down = jnp.broadcast_to(weight, (128, 128)).T
         source = coupling[at].astype(F32) + jnp.concatenate([down] * 4, axis=1) * total[at]
-        solved[at] = dot(pack[at], source)
-        row = dot(pack[256 + t : 257 + t] + weight * total[256:257, at], pack[at])
+        solved[at] = dot3(inverse[at], source)
+        row = dot(rows[t : t + 1] + weight * total[256:257, at], inverse[at])
         pulled[0:8, at] = jnp.broadcast_to(row, (8, 128))
 
 
@@ -218,15 +257,15 @@
     for b in range(4):
         count = 3 if b < 2 else 2
         at = slice(b * 128, b * 128 + 128)
-        part = dot(coupling[0:256, at], ring_columns(first, b, count), TN)
-        part = part + dot(own[0:256, at], ring_columns(near, b, count), TN)
+        part = dot3(coupling[0:256, at], ring_columns(first, b, count), TN)
+        part = part + dot3(own[0:256, at], ring_columns(near, b, count), TN)
         gram[at, 0 : count * 128] = part
         if count == 2:
             gram[at, 256:384] = jnp.zeros((128, 128), F32)
     row = jnp.zeros((1, 512), F32)
     for t in range(2):
         at = slice(t * 128, t * 128 + 128)
-        row = row + dot(pack[256 + t : 257 + t], first[at])
+        row = row + dot(pack[128 + t : 129 + t], first[at])
         row = row + dot(near[256:257, at], own[at])
     gather[0:8] = jnp.broadcast_to(row, (8, 512))
 
@@ -246,7 +285,7 @@
     for b in range(4):
         count = 3 if b < 2 else 2
         at = slice(b * 128, b * 128 + 128)
-        part = gram[at, 0 : count * 128] + dot(both[0:256, at], ring_columns(fields, b, count), TN)
+        part = gram[at, 0 : count * 128] + dot3(both[0:256, at], ring_columns(fields, b, count), TN)
         for m in range(4):
             for j in range(4):
                 source = part[m * 32 + j * 8 : m * 32 + j * 8 + 8]
@@ -261,17 +300,14 @@
     send[...] = total[1 - flags[1]]
 
 
-def halve_kernel(flags, mine, theirs, keep, send):
-    keep[...] = mine[flags[2]] + theirs[flags[2]]
-    send[...] = mine[1 - flags[2]] + theirs[1 - flags[2]]
-
-
-def parent_kernel(flags, mine, across_x, across_core, root_part, upper, solved, solved_row, held):
-    leaf = flags[3]
+def parent_kernel(
+    flags, mine, across_x, across_core, across_both, root_part, upper, solved, solved_row, held
+):
+    leaf = flags[2]
     held[:, leaf] = mine[...]
     held[:, leaf ^ 2] = across_x[...]
-    held[:, leaf ^ 1] = across_core[0]
-    held[:, leaf ^ 3] = across_core[1]
+    held[:, leaf ^ 1] = across_core[...]
+    held[:, leaf ^ 3] = across_both[...]
 
     def block(b, m):
         return held[4 * b : 4 * b + 4, :, :, m * 128 : m * 128 + 128].reshape(128, 128)
@@ -335,8 +371,8 @@
         pieces[b] = value
     chosen = jnp.zeros((1, 128), F32)
     for b in range(4):
-        chosen = chosen + jnp.where(flags[4] == b, pieces[b], 0.0)
-    chosen = pltpu.roll(jnp.broadcast_to(chosen, (8, 128)), flags[5], 1)
+        chosen = chosen + jnp.where(flags[3] == b, pieces[b], 0.0)
+    chosen = pltpu.roll(jnp.broadcast_to(chosen, (8, 128)), flags[4], 1)
     parent[...] = chosen[0:1, 0:32]
     whole = jnp.concatenate(pieces, axis=1)
     for t in range(2):
@@ -345,11 +381,9 @@
 
 
 def neighbours(message, to_half):
-    return (
-        lax.ppermute(message, AXES, TO_CORE),
-        lax.ppermute(message, AXES, TO_CHIP),
-        lax.ppermute(to_half, AXES, TO_HALF),
-    )
+    chip = lax.ppermute(message, AXES, TO_CHIP)
+    other = lax.ppermute(to_half, AXES, TO_HALF)
+    return lax.ppermute(message, AXES, TO_CORE), chip, other
 
 
 def body(
@@ -365,7 +399,7 @@
     column = (scen // 2) % 2
     half = column ^ (quarter % 2)
     turn = (128 - (strip % 4) * 32) % 128
-    flags = jnp.stack([half, core, column, scen % 4, strip // 4, turn]).astype(jnp.int32)
+    flags = jnp.stack([half, core, scen % 4, strip // 4, turn]).astype(jnp.int32)
 
     weight = conductance[0] * (1.0 + compressor[0].astype(F32)[..., None]) * 0.5
     own_coupling = coupling[0].reshape(256, 512)
@@ -373,7 +407,7 @@
         [leaf_rhs[0].reshape(2, 128), weight.reshape(2, 128), jnp.zeros((4, 128), F32)], axis=0
     )
     field = lax.ppermute(own_coupling.astype(F32), AXES, MOVE_OUT)
-    (own_pack,) = call(invert_kernel, "invert", [(264, 128)], blocks[0].reshape(256, 128), rows)
+    own_inverse, own_pack = call(invert_kernel, [(256, 128), (136, 128)], blocks[0].reshape(256, 128), rows)
     pack = lax.ppermute(own_pack, AXES, MOVE_OUT)
 
     label = parent_of[0]
@@ -391,52 +425,42 @@
     right = jnp.concatenate([right, jnp.zeros((4, 128), F32)], axis=0)
 
     shapes = [(256, 512), (256, 128), (264, 512), (136, 512)]
-    first, scaled, own0, half0 = call(start_kernel, "start", shapes, flags, pack, field, scalars=1)
+    first, scaled, own0, half0 = call(start_kernel, shapes, flags, pack, field, scalars=1)
     shapes = [(264, 512), (264, 512), (136, 512)]
-    near0, own1, half1 = call(
-        sweep_kernel, "sweep", shapes, flags, scaled, own0, *neighbours(own0, half0), scalars=1
-    )
+    near0, own1, half1 = call(sweep_kernel, shapes, flags, scaled, own0, *neighbours(own0, half0), scalars=1)
     around1 = neighbours(own1, half1)
-    gram, gather = call(
-        gram_early_kernel, "gram_early", [(512, 384), (8, 512)], pack, field, first, own0, near0
-    )
-    near1, own2, half2 = call(
-        sweep_kernel, "sweep", shapes, flags, scaled, own1, *around1, scalars=1
-    )
+    gram, gather = call(gram_early_kernel, [(512, 384), (8, 512)], pack, field, first, own0, near0)
+    near1, own2, half2 = call(sweep_kernel, shapes, flags, scaled, own1, *around1, scalars=1)
     near2, keep, send = call(
         gram_late_kernel,
-        "gram_late",
         [(264, 512), (2, 128, 384), (2, 128, 384)],
         flags, gram, gather, right, own0, own2, near1, *neighbours(own2, half2),
         scalars=1,
         scratch=[pltpu.VMEM((2, 2, 128, 384), F32), pltpu.VMEM((256, 512), F32), pltpu.VMEM((256, 512), F32)],
     )
-    own3, half3 = call(apply_kernel, "apply", shapes[1:], flags, scaled, near2, scalars=1)
+    own3, half3 = call(apply_kernel, shapes[1:], flags, scaled, near2, scalars=1)
     around3 = neighbours(own3, half3)
     theirs, _ = lax.optimization_barrier((lax.ppermute(send, "scen", flip(1)), own3))
-    keep, send = call(halve_kernel, "halve", [(128, 384)] * 2, flags, keep, theirs, scalars=1)
-    quarter_sum = keep + lax.ppermute(send, "scen", flip(2))
-    shares = lax.all_to_all(quarter_sum.reshape(16, 8, 384), Z_AXES, 0, 0)
-    near3, own4, half4 = call(sweep_kernel, "sweep", shapes, flags, scaled, own3, *around3, scalars=1)
+    half_sum = (keep + theirs).reshape(32, 8, 384)
+    shares = lax.all_to_all(half_sum, AXES, 0, 0, axis_index_groups=SAME_CORE)
+    near3, own4, half4 = call(sweep_kernel, shapes, flags, scaled, own3, *around3, scalars=1)
     around4 = neighbours(own4, half4)
     shares, _ = lax.optimization_barrier((shares, own4))
     share = jnp.concatenate([jnp.sum(shares, axis=0) + matrix_rows, link_rows], axis=1)
     mine = lax.all_to_all(jnp.broadcast_to(share[None], (16, 8, 640)), Z_AXES, 0, 0)
-    (total,) = call(
-        total_kernel, "total", [(264, 512)], flags, near0, near1, near2, near3, own4, *around4, scalars=1
-    )
+    (total,) = call(total_kernel, [(264, 512)], flags, near0, near1, near2, near3, own4, *around4, scalars=1)
     mine, total = lax.optimization_barrier((mine, total))
     across_x = lax.ppermute(mine, "scen", flip(2))
-    across_core = lax.ppermute(jnp.stack([mine, across_x]), "scen", flip(1))
+    across_core = lax.ppermute(mine, "scen", flip(1))
+    across_both = lax.ppermute(across_x, "scen", flip(1))
 
     total = lax.ppermute(total, AXES, MOVE_BACK)
-    leaf_solved, pulled = call(leaf_kernel, "leaf", [(256, 512), (8, 256)], own_pack, own_coupling, total)
+    leaf_solved, pulled = call(leaf_kernel, [(256, 512), (8, 256)], own_inverse, rows, own_coupling, total)
 
     part, upper, solved, solved_row = call(
         parent_kernel,
-        "parent",
         [(392, 128), (384, 512), (512, 256), (8, 512)],
-        flags, mine, across_x, across_core,
+        flags, mine, across_x, across_core, across_both,
         scalars=1,
         scratch=[pltpu.VMEM((16, 4, 8, 640), F32)],
     )
@@ -444,7 +468,6 @@
     others = [lax.ppermute(part, "scen", [(i, (i + by) % 32) for i in range(32)]) for by in (16, 8, 24)]
     step, parent, move = call(
         root_kernel,
-        "root",
         [(1, 256), (1, 32), (2, 128)],
         flags, part, *others, root_mat, root_rhs.reshape(1, 256), upper, solved, solved_row, leaf_solved, pulled,
         scalars=1,

time: 302 us -> 289 us (0.957)
  Pallas kernels: 81.2 us -> 69.8 us
    pallas_call x13 -> x12, Pallas kernels: 81.2 us -> 69.8 us  [call(): pl.pallas_call(kernel, out_shape=[jax.ShapeDtypeStruct(s, F32) for s in s...]
    ppermute x17, waiting for transfers between devices: 36.4 us -> 41 us  [the longest x5 27.2 us: neighbours(): other = lax.ppermute(to_half, AXES, TO_HALF)]
    ppermute x17, starting transfers between devices: 67.4 us -> 63.9 us  [the longest x5 31.8 us: neighbours(): chip = lax.ppermute(message, AXES, TO_CHIP)]
  transfers between devices with their start and end apart: 28 -> 28, of which waited for: 12 -> 11; matrix products, arithmetic and copies ran while one was open for 1% -> 2% of each run, Pallas kernels for 17% -> 15%
where the time goes in v3:
time: 289 us; the launch traced here: 288 us
  starting transfers between devices  131 us (45%)
  Pallas kernels  69.8 us (24%)
  waiting for transfers between devices  66.8 us (23%)
  local copies, waits for them, and re-layouts  14 us (5%)
  other arithmetic  4.41 us (2%)
    pallas_call x12, Pallas kernels, call(): pl.pallas_call(kernel, out_shape=[jax.ShapeDtypeStruct(s, F32) for s in s...  69.8 us
    ppermute x5, starting transfers between devices, neighbours(): chip = lax.ppermute(message, AXES, TO_CHIP)  31.8 us
    ppermute x5, waiting for transfers between devices, neighbours(): other = lax.ppermute(to_half, AXES, TO_HALF)  27.2 us
    ppermute x5, starting transfers between devices, neighbours(): return (lax.ppermute(message, AXES, TO_CORE), chip, other)  16.2 us
    ppermute x1, waiting for transfers between devices, body(): pack = lax.ppermute(own_pack, AXES, MOVE_OUT)  14.5 us
    ppermute x5, waiting for transfers between devices, neighbours(): chip = lax.ppermute(message, AXES, TO_CHIP)  13.8 us
    ppermute x1, starting transfers between devices, body(): field = lax.ppermute(own_coupling.astype(F32), AXES, MOVE_OUT)  13.4 us
    ppermute x5, starting transfers between devices, neighbours(): other = lax.ppermute(to_half, AXES, TO_HALF)  12 us
  transfers between devices with their start and end apart: 28, of which 11 were waited for; matrix products, arithmetic and copies ran while one was open for 2% of the time, Pallas kernels for 15%

profile of v3, /device:TPU:1, one launch (start us, length us, event | category | flops | bytes accessed | tf_op | source)
XLA Modules:
  0.0 287.6 jit_solution(15909550546289364096)
XLA Ops:
  1.7 13.4 %collective-permute-start.1 = (f32[256,512]{1,0:T(8,128)S(1)}, f32[256,512]{1,0:T(8,128)S(1)}, u32[]{:S(2)}, u32[]{:S(2)}) collective-permute-start(f32[256,512]{1,0:T(8,128)S(1)} %bitcast_convert_fusion), channel_id=1, source_target_pairs={{0,10},{2,26},{4,8},{6,24},{8,6},{10,22},{12,4},{14,20},{1,42},{3,... | collective-permute-start | bytes 1572872 | tf_op jit(solution)/shard_map/ppermute | solution.py:409
  17.3 6.8 %shard_map.130 = (f32[256,128]{1,0:T(8,128)}, f32[136,128]{1,0:T(8,128)}) custom-call(f32[256,128]{1,0:T(8,128)} %bitcast.32, f32[8,128]{1,0:T(8,128)} %maximum_maximum_fusion.rows), custom_call_target="tpu_custom_call" | custom-call | tf_op jit(solution)/shard_map/pallas_call | solution.py:128
  26.8 14.5 %collective-permute-done.pack = f32[136,128]{1,0:T(8,128)S(1)} collective-permute-done((f32[136,128]{1,0:T(8,128)}, f32[136,128]{1,0:T(8,128)S(1)}, u32[]{:S(2)}, u32[]{:S(2)}) %collective-permute-start) | collective-permute-done | bytes 69664 | tf_op jit(solution)/shard_map/ppermute | solution.py:411
  45.3 7.3 %collective-permute-start.2 = (f32[264,512]{1,0:T(8,128)}, f32[264,512]{1,0:T(8,128)S(1)}, u32[]{:S(2)}, u32[]{:S(2)}) collective-permute-start(f32[264,512]{1,0:T(8,128)} %get-tuple-element.40.own.own0), channel_id=1, source_target_pairs={{10,26},{26,10},{8,24},{24,8},{6,22},{22,6},{4,20},{20,4},{42,58},... | collective-permute-start | bytes 1622024 | tf_op jit(solution)/shard_map/ppermute | solution.py:386
  52.7 11.8 %collective-permute-start.3 = (f32[264,512]{1,0:T(8,128)}, f32[264,512]{1,0:T(8,128)S(1)}, u32[]{:S(2)}, u32[]{:S(2)}) collective-permute-start(f32[264,512]{1,0:T(8,128)} %get-tuple-element.40.own.own0), channel_id=1, source_target_pairs={{26,8},{8,26},{24,6},{6,24},{22,4},{4,22},{58,40},{40,58},{56,38},... | collective-permute-start | bytes 1622024 | tf_op jit(solution)/shard_map/ppermute | solution.py:384
  66.4 5.6 %collective-permute-done.4.other = f32[136,512]{1,0:T(8,128)S(1)} collective-permute-done((f32[136,512]{1,0:T(8,128)}, f32[136,512]{1,0:T(8,128)S(1)}, u32[]{:S(2)}, u32[]{:S(2)}) %collective-permute-start.4) | collective-permute-done | bytes 278560 | tf_op jit(solution)/shard_map/ppermute | solution.py:385
  77.9 5.8 %collective-permute-start.6 = (f32[264,512]{1,0:T(8,128)}, f32[264,512]{1,0:T(8,128)S(1)}, u32[]{:S(2)}, u32[]{:S(2)}) collective-permute-start(f32[264,512]{1,0:T(8,128)} %get-tuple-element.46.own), channel_id=1, source_target_pairs={{26,8},{8,26},{24,6},{6,24},{22,4},{4,22},{58,40},{40,58},{56,38},... | collective-permute-start | bytes 1622024 | tf_op jit(solution)/shard_map/ppermute | solution.py:384
  85.6 5.6 %collective-permute-done.7.other = f32[136,512]{1,0:T(8,128)S(1)} collective-permute-done((f32[136,512]{1,0:T(8,128)}, f32[136,512]{1,0:T(8,128)S(1)}, u32[]{:S(2)}, u32[]{:S(2)}) %collective-permute-start.7) | collective-permute-done | bytes 278560 | tf_op jit(solution)/shard_map/ppermute | solution.py:385
  97.8 5.0 %collective-permute-start.9 = (f32[264,512]{1,0:T(8,128)}, f32[264,512]{1,0:T(8,128)S(1)}, u32[]{:S(2)}, u32[]{:S(2)}) collective-permute-start(f32[264,512]{1,0:T(8,128)} %get-tuple-element.48.own2), channel_id=1, source_target_pairs={{26,8},{8,26},{24,6},{6,24},{22,4},{4,22},{58,40},{40,58},{56,38},... | collective-permute-start | bytes 1622024 | tf_op jit(solution)/shard_map/ppermute | solution.py:384
  121.4 11.4 %all-to-all-start = ((f32[32,8,384]{2,1,0:T(8,128)}), f32[32,8,384]{2,1,0:T(8,128)S(1)}, u32[]{:S(2)}, u32[]{:S(2)}) async-start(f32[32,8,384]{2,1,0:T(8,128)} %bitcast.13), calls=%async_computation | async-start | bytes 786432 | tf_op jit(solution)/shard_map/all_to_all | solution.py:445
  135.1 4.5 %collective-permute-start.13 = (f32[264,512]{1,0:T(8,128)S(1)}, f32[264,512]{1,0:T(8,128)S(1)}, u32[]{:S(2)}, u32[]{:S(2)}) collective-permute-start(f32[264,512]{1,0:T(8,128)S(1)} %copy-done.9), channel_id=1, source_target_pairs={{26,8},{8,26},{24,6},{6,24},{22,4},{4,22},{58,40},{40,58},{56,38},... | collective-permute-start | bytes 1622024 | tf_op jit(solution)/shard_map/ppermute | solution.py:384
  143.5 7.8 %collective-permute-done.14.other = f32[136,512]{1,0:T(8,128)S(1)} collective-permute-done((f32[136,512]{1,0:T(8,128)S(1)}, f32[136,512]{1,0:T(8,128)S(1)}, u32[]{:S(2)}, u32[]{:S(2)}) %collective-permute-start.14) | collective-permute-done | bytes 278560 | tf_op jit(solution)/shard_map/ppermute | solution.py:385
  151.3 7.8 %collective-permute-done.13.chip = f32[264,512]{1,0:T(8,128)S(1)} collective-permute-done((f32[264,512]{1,0:T(8,128)S(1)}, f32[264,512]{1,0:T(8,128)S(1)}, u32[]{:S(2)}, u32[]{:S(2)}) %collective-permute-start.13) | collective-permute-done | bytes 540704 | tf_op jit(solution)/shard_map/ppermute | solution.py:384
  163.7 9.1 %all-to-all-start.1 = ((f32[16,8,640]{2,1,0:T(8,128)}), f32[16,8,640]{2,1,0:T(8,128)S(1)}, u32[]{:S(2)}, u32[]{:S(2)}) async-start(f32[16,8,640]{2,1,0:T(8,128)} %broadcast_in_dim.16), calls=%async_computation.1 | async-start | bytes 655360 | tf_op jit(solution)/shard_map/all_to_all | solution.py:450
  175.7 4.7 %collective-permute-start.16 = (f32[264,512]{1,0:T(8,128)S(1)}, f32[264,512]{1,0:T(8,128)S(1)}, u32[]{:S(2)}, u32[]{:S(2)}) collective-permute-start(f32[264,512]{1,0:T(8,128)S(1)} %copy-done.6), channel_id=1, source_target_pairs={{26,8},{8,26},{24,6},{6,24},{22,4},{4,22},{58,40},{40,58},{56,38},... | collective-permute-start | bytes 1622024 | tf_op jit(solution)/shard_map/ppermute | solution.py:384
  183.5 7.2 %collective-permute-done.17.other = f32[136,512]{1,0:T(8,128)S(1)} collective-permute-done((f32[136,512]{1,0:T(8,128)S(1)}, f32[136,512]{1,0:T(8,128)S(1)}, u32[]{:S(2)}, u32[]{:S(2)}) %collective-permute-start.17) | collective-permute-done | bytes 278560 | tf_op jit(solution)/shard_map/ppermute | solution.py:385
  190.7 6.0 %collective-permute-done.16.chip = f32[264,512]{1,0:T(8,128)S(1)} collective-permute-done((f32[264,512]{1,0:T(8,128)S(1)}, f32[264,512]{1,0:T(8,128)S(1)}, u32[]{:S(2)}, u32[]{:S(2)}) %collective-permute-start.16) | collective-permute-done | bytes 540704 | tf_op jit(solution)/shard_map/ppermute | solution.py:384
  205.7 5.5 %collective-permute-done.18.across_x = f32[16,8,640]{2,1,0:T(8,128)S(1)} collective-permute-done((f32[16,8,640]{2,1,0:T(8,128)S(1)}, f32[16,8,640]{2,1,0:T(8,128)S(1)}, u32[]{:S(2)}, u32[]{:S(2)}) %collective-permute-start.18) | collective-permute-done | bytes 327712 | tf_op jit(solution)/shard_map/ppermute | solution.py:453
  213.1 10.2 %collective-permute-start.25 = (f32[264,512]{1,0:T(8,128)}, f32[264,512]{1,0:T(8,128)S(1)}, u32[]{:S(2)}, u32[]{:S(2)}) collective-permute-start(f32[264,512]{1,0:T(8,128)} %shard_map.138), channel_id=1, source_target_pairs={{10,0},{26,2},{8,4},{24,6},{6,8},{22,10},{4,12},{20,14},{42,1},{58... | collective-permute-start | bytes 1622024 | tf_op jit(solution)/shard_map/ppermute | solution.py:457
  224.7 22.9 %shard_map.139 = (f32[392,128]{1,0:T(8,128)}, f32[384,512]{1,0:T(8,128)}, f32[512,256]{1,0:T(8,128)}, f32[8,512]{1,0:T(8,128)}) custom-call(s32[5]{0:T(128)} %stack.23.flags, f32[16,8,640]{2,1,0:T(8,128)} %copy-done.2, f32[16,8,640]{2,1,0:T(8,128)} %copy-done.18, f32[16,8,640]{2,1,0:T(8,128)} %copy-done.19, f32[16,8,640]{2,1,0:T(8,128)} %copy-done.20), custom_call_target="tpu_custom_call" | custom-call | tf_op jit(solution)/shard_map/pallas_call | solution.py:128
  251.7 4.4 %collective-permute-done.21 = f32[392,128]{1,0:T(8,128)S(1)} collective-permute-done((f32[392,128]{1,0:T(8,128)}, f32[392,128]{1,0:T(8,128)S(1)}, u32[]{:S(2)}, u32[]{:S(2)}) %collective-permute-start.21) | collective-permute-done | bytes 200736 | tf_op jit(solution)/shard_map/ppermute | solution.py:467
  257.1 4.8 %collective-permute-start.22 = (f32[392,128]{1,0:T(8,128)S(1)}, f32[392,128]{1,0:T(8,128)S(1)}, u32[]{:S(2)}, u32[]{:S(2)}) collective-permute-start(f32[392,128]{1,0:T(8,128)S(1)} %add.87.mine), channel_id=1, source_target_pairs={{0,256},{16,272},{32,288},{48,304},{64,320},{80,336},{96,352},{112... | collective-permute-start | bytes 602120 | tf_op jit(solution)/shard_map/ppermute | solution.py:468
  264.3 4.2 %collective-permute-start.24 = (f32[392,128]{1,0:T(8,128)S(1)}, f32[392,128]{1,0:T(8,128)S(1)}, u32[]{:S(2)}, u32[]{:S(2)}) collective-permute-start(f32[392,128]{1,0:T(8,128)S(1)} %add.87.mine), channel_id=1, source_target_pairs={{0,384},{16,400},{32,416},{48,432},{64,448},{80,464},{96,480},{112... | collective-permute-start | bytes 602120 | tf_op jit(solution)/shard_map/ppermute | solution.py:468
  273.9 13.7 %shard_map.141 = (f32[1,256]{1,0:T(1,128)}, f32[1,32]{1,0:T(1,128)}, f32[2,128]{1,0:T(2,128)}) custom-call(s32[5]{0:T(128)} %stack.23.flags, f32[392,128]{1,0:T(8,128)} %copy-done.3, f32[392,128]{1,0:T(8,128)} %copy-done.27, f32[392,128]{1,0:T(8,128)} %copy-done.28, f32[392,128]{1,0:T(8,128)} %copy-done.29, f32[256,256]{1,0:T(8,128)} %matrix.1, ...), custom_call_target="tpu_custom_call" | custom-call | tf_op jit(solution)/shard_map/pallas_call | solution.py:128
  (133 shorter events, 85.6 us)
Async XLA Ops:
  1.7 39.5 %collective-permute-start.1 = (f32[256,512]{1,0:T(8,128)S(1)}, f32[256,512]{1,0:T(8,128)S(1)}, u32[]{:S(2)}, u32[]{:S(2)}) collective-permute-start(f32[256,512]{1,0:T(8,128)S(1)} %bitcast_convert_fusion), channel_id=1, source_target_pairs={{0,10},{2,26},{4,8},{6,24},{8,6},{10,22},{12,4},{14,20},{1,42},{3,... | collective-permute-start | bytes 1572872 | tf_op jit(solution)/shard_map/ppermute | solution.py:409
  24.1 17.1 %collective-permute-start = (f32[136,128]{1,0:T(8,128)}, f32[136,128]{1,0:T(8,128)S(1)}, u32[]{:S(2)}, u32[]{:S(2)}) collective-permute-start(f32[136,128]{1,0:T(8,128)} %get-tuple-element.38), channel_id=1, source_target_pairs={{0,10},{2,26},{4,8},{6,24},{8,6},{10,22},{12,4},{14,20},{1,42},{3,... | collective-permute-start | bytes 208904 | tf_op jit(solution)/shard_map/ppermute | solution.py:411
  45.3 26.7 %collective-permute-start.2 = (f32[264,512]{1,0:T(8,128)}, f32[264,512]{1,0:T(8,128)S(1)}, u32[]{:S(2)}, u32[]{:S(2)}) collective-permute-start(f32[264,512]{1,0:T(8,128)} %get-tuple-element.40.own.own0), channel_id=1, source_target_pairs={{10,26},{26,10},{8,24},{24,8},{6,22},{22,6},{4,20},{20,4},{42,58},... | collective-permute-start | bytes 1622024 | tf_op jit(solution)/shard_map/ppermute | solution.py:386
  52.7 19.4 %collective-permute-start.3 = (f32[264,512]{1,0:T(8,128)}, f32[264,512]{1,0:T(8,128)S(1)}, u32[]{:S(2)}, u32[]{:S(2)}) collective-permute-start(f32[264,512]{1,0:T(8,128)} %get-tuple-element.40.own.own0), channel_id=1, source_target_pairs={{26,8},{8,26},{24,6},{6,24},{22,4},{4,22},{58,40},{40,58},{56,38},... | collective-permute-start | bytes 1622024 | tf_op jit(solution)/shard_map/ppermute | solution.py:384
  76.0 15.3 %collective-permute-start.5 = (f32[264,512]{1,0:T(8,128)}, f32[264,512]{1,0:T(8,128)S(1)}, u32[]{:S(2)}, u32[]{:S(2)}) collective-permute-start(f32[264,512]{1,0:T(8,128)} %get-tuple-element.46.own), channel_id=1, source_target_pairs={{10,26},{26,10},{8,24},{24,8},{6,22},{22,6},{4,20},{20,4},{42,58},... | collective-permute-start | bytes 1622024 | tf_op jit(solution)/shard_map/ppermute | solution.py:386
  77.9 13.4 %collective-permute-start.6 = (f32[264,512]{1,0:T(8,128)}, f32[264,512]{1,0:T(8,128)S(1)}, u32[]{:S(2)}, u32[]{:S(2)}) collective-permute-start(f32[264,512]{1,0:T(8,128)} %get-tuple-element.46.own), channel_id=1, source_target_pairs={{26,8},{8,26},{24,6},{6,24},{22,4},{4,22},{58,40},{40,58},{56,38},... | collective-permute-start | bytes 1622024 | tf_op jit(solution)/shard_map/ppermute | solution.py:384
  95.9 15.3 %collective-permute-start.8 = (f32[264,512]{1,0:T(8,128)}, f32[264,512]{1,0:T(8,128)S(1)}, u32[]{:S(2)}, u32[]{:S(2)}) collective-permute-start(f32[264,512]{1,0:T(8,128)} %get-tuple-element.48.own2), channel_id=1, source_target_pairs={{10,26},{26,10},{8,24},{24,8},{6,22},{22,6},{4,20},{20,4},{42,58},... | collective-permute-start | bytes 1622024 | tf_op jit(solution)/shard_map/ppermute | solution.py:386
  97.8 13.4 %collective-permute-start.9 = (f32[264,512]{1,0:T(8,128)}, f32[264,512]{1,0:T(8,128)S(1)}, u32[]{:S(2)}, u32[]{:S(2)}) collective-permute-start(f32[264,512]{1,0:T(8,128)} %get-tuple-element.48.own2), channel_id=1, source_target_pairs={{26,8},{8,26},{24,6},{6,24},{22,4},{4,22},{58,40},{40,58},{56,38},... | collective-permute-start | bytes 1622024 | tf_op jit(solution)/shard_map/ppermute | solution.py:384
  121.4 41.4 %all-to-all-start = ((f32[32,8,384]{2,1,0:T(8,128)}), f32[32,8,384]{2,1,0:T(8,128)S(1)}, u32[]{:S(2)}, u32[]{:S(2)}) async-start(f32[32,8,384]{2,1,0:T(8,128)} %bitcast.13), calls=%async_computation | async-start | bytes 786432 | tf_op jit(solution)/shard_map/all_to_all | solution.py:445
  132.9 18.5 %collective-permute-start.12 = (f32[264,512]{1,0:T(8,128)S(1)}, f32[264,512]{1,0:T(8,128)S(1)}, u32[]{:S(2)}, u32[]{:S(2)}) collective-permute-start(f32[264,512]{1,0:T(8,128)S(1)} %copy-done.9), channel_id=1, source_target_pairs={{10,26},{26,10},{8,24},{24,8},{6,22},{22,6},{4,20},{20,4},{42,58},... | collective-permute-start | bytes 1622024 | tf_op jit(solution)/shard_map/ppermute | solution.py:386
  135.1 24.1 %collective-permute-start.13 = (f32[264,512]{1,0:T(8,128)S(1)}, f32[264,512]{1,0:T(8,128)S(1)}, u32[]{:S(2)}, u32[]{:S(2)}) collective-permute-start(f32[264,512]{1,0:T(8,128)S(1)} %copy-done.9), channel_id=1, source_target_pairs={{26,8},{8,26},{24,6},{6,24},{22,4},{4,22},{58,40},{40,58},{56,38},... | collective-permute-start | bytes 1622024 | tf_op jit(solution)/shard_map/ppermute | solution.py:384
  139.6 11.7 %collective-permute-start.14 = (f32[136,512]{1,0:T(8,128)S(1)}, f32[136,512]{1,0:T(8,128)S(1)}, u32[]{:S(2)}, u32[]{:S(2)}) collective-permute-start(f32[136,512]{1,0:T(8,128)S(1)} %copy-done.32), channel_id=1, source_target_pairs={{10,42},{26,58},{8,40},{24,56},{6,38},{22,54},{4,36},{20,52},{42,1... | collective-permute-start | bytes 835592 | tf_op jit(solution)/shard_map/ppermute | solution.py:385
  163.7 36.9 %all-to-all-start.1 = ((f32[16,8,640]{2,1,0:T(8,128)}), f32[16,8,640]{2,1,0:T(8,128)S(1)}, u32[]{:S(2)}, u32[]{:S(2)}) async-start(f32[16,8,640]{2,1,0:T(8,128)} %broadcast_in_dim.16), calls=%async_computation.1 | async-start | bytes 655360 | tf_op jit(solution)/shard_map/all_to_all | solution.py:450
  172.8 17.9 %collective-permute-start.15 = (f32[264,512]{1,0:T(8,128)S(1)}, f32[264,512]{1,0:T(8,128)S(1)}, u32[]{:S(2)}, u32[]{:S(2)}) collective-permute-start(f32[264,512]{1,0:T(8,128)S(1)} %copy-done.6), channel_id=1, source_target_pairs={{10,26},{26,10},{8,24},{24,8},{6,22},{22,6},{4,20},{20,4},{42,58},... | collective-permute-start | bytes 1622024 | tf_op jit(solution)/shard_map/ppermute | solution.py:386
  175.7 21.0 %collective-permute-start.16 = (f32[264,512]{1,0:T(8,128)S(1)}, f32[264,512]{1,0:T(8,128)S(1)}, u32[]{:S(2)}, u32[]{:S(2)}) collective-permute-start(f32[264,512]{1,0:T(8,128)S(1)} %copy-done.6), channel_id=1, source_target_pairs={{26,8},{8,26},{24,6},{6,24},{22,4},{4,22},{58,40},{40,58},{56,38},... | collective-permute-start | bytes 1622024 | tf_op jit(solution)/shard_map/ppermute | solution.py:384
  180.4 10.3 %collective-permute-start.17 = (f32[136,512]{1,0:T(8,128)S(1)}, f32[136,512]{1,0:T(8,128)S(1)}, u32[]{:S(2)}, u32[]{:S(2)}) collective-permute-start(f32[136,512]{1,0:T(8,128)S(1)} %copy-done.33), channel_id=1, source_target_pairs={{10,42},{26,58},{8,40},{24,56},{6,38},{22,54},{4,36},{20,52},{42,1... | collective-permute-start | bytes 835592 | tf_op jit(solution)/shard_map/ppermute | solution.py:385
  200.6 10.5 %collective-permute-start.18 = (f32[16,8,640]{2,1,0:T(8,128)S(1)}, f32[16,8,640]{2,1,0:T(8,128)S(1)}, u32[]{:S(2)}, u32[]{:S(2)}) collective-permute-start(f32[16,8,640]{2,1,0:T(8,128)S(1)} %all-to-all-done.1.mine), channel_id=1, source_target_pairs={{0,32},{16,48},{32,0},{48,16},{64,96},{80,112},{96,64},{112,80},{1... | collective-permute-start | bytes 983048 | tf_op jit(solution)/shard_map/ppermute | solution.py:453
  203.7 19.5 %collective-permute-start.19 = (f32[16,8,640]{2,1,0:T(8,128)S(1)}, f32[16,8,640]{2,1,0:T(8,128)S(1)}, u32[]{:S(2)}, u32[]{:S(2)}) collective-permute-start(f32[16,8,640]{2,1,0:T(8,128)S(1)} %all-to-all-done.1.mine), channel_id=1, source_target_pairs={{0,16},{16,0},{32,48},{48,32},{64,80},{80,64},{96,112},{112,96},{1... | collective-permute-start | bytes 983048 | tf_op jit(solution)/shard_map/ppermute | solution.py:454
  211.1 12.1 %collective-permute-start.20 = (f32[16,8,640]{2,1,0:T(8,128)S(1)}, f32[16,8,640]{2,1,0:T(8,128)S(1)}, u32[]{:S(2)}, u32[]{:S(2)}) collective-permute-start(f32[16,8,640]{2,1,0:T(8,128)S(1)} %collective-permute-done.18.across_x), channel_id=1, source_target_pairs={{0,16},{16,0},{32,48},{48,32},{64,80},{80,64},{96,112},{112,96},{1... | collective-permute-start | bytes 983048 | tf_op jit(solution)/shard_map/ppermute | solution.py:455
  213.1 55.4 %collective-permute-start.25 = (f32[264,512]{1,0:T(8,128)}, f32[264,512]{1,0:T(8,128)S(1)}, u32[]{:S(2)}, u32[]{:S(2)}) collective-permute-start(f32[264,512]{1,0:T(8,128)} %shard_map.138), channel_id=1, source_target_pairs={{10,0},{26,2},{8,4},{24,6},{6,8},{22,10},{4,12},{20,14},{42,1},{58... | collective-permute-start | bytes 1622024 | tf_op jit(solution)/shard_map/ppermute | solution.py:457
  247.6 8.6 %collective-permute-start.21 = (f32[392,128]{1,0:T(8,128)}, f32[392,128]{1,0:T(8,128)S(1)}, u32[]{:S(2)}, u32[]{:S(2)}) collective-permute-start(f32[392,128]{1,0:T(8,128)} %get-tuple-element.62), channel_id=1, source_target_pairs={{0,64},{16,80},{32,96},{48,112},{64,0},{80,16},{96,32},{112,48},{1... | collective-permute-start | bytes 602120 | tf_op jit(solution)/shard_map/ppermute | solution.py:467
  257.1 14.7 %collective-permute-start.22 = (f32[392,128]{1,0:T(8,128)S(1)}, f32[392,128]{1,0:T(8,128)S(1)}, u32[]{:S(2)}, u32[]{:S(2)}) collective-permute-start(f32[392,128]{1,0:T(8,128)S(1)} %add.87.mine), channel_id=1, source_target_pairs={{0,256},{16,272},{32,288},{48,304},{64,320},{80,336},{96,352},{112... | collective-permute-start | bytes 602120 | tf_op jit(solution)/shard_map/ppermute | solution.py:468
  261.9 9.8 %collective-permute-start.23 = (f32[392,128]{1,0:T(8,128)S(1)}, f32[392,128]{1,0:T(8,128)S(1)}, u32[]{:S(2)}, u32[]{:S(2)}) collective-permute-start(f32[392,128]{1,0:T(8,128)S(1)} %add.87.mine), channel_id=1, source_target_pairs={{0,128},{16,144},{32,160},{48,176},{64,192},{80,208},{96,224},{112... | collective-permute-start | bytes 602120 | tf_op jit(solution)/shard_map/ppermute | solution.py:468
  264.3 9.0 %collective-permute-start.24 = (f32[392,128]{1,0:T(8,128)S(1)}, f32[392,128]{1,0:T(8,128)S(1)}, u32[]{:S(2)}, u32[]{:S(2)}) collective-permute-start(f32[392,128]{1,0:T(8,128)S(1)} %add.87.mine), channel_id=1, source_target_pairs={{0,384},{16,400},{32,416},{48,432},{64,448},{80,464},{96,480},{112... | collective-permute-start | bytes 602120 | tf_op jit(solution)/shard_map/ppermute | solution.py:468
  (39 other events, 342.2 us)

commit v4 on v3

--- a/solution.py
+++ b/solution.py
@@ -447,7 +447,8 @@
     around4 = neighbours(own4, half4)
     shares, _ = lax.optimization_barrier((shares, own4))
     share = jnp.concatenate([jnp.sum(shares, axis=0) + matrix_rows, link_rows], axis=1)
-    mine = lax.all_to_all(jnp.broadcast_to(share[None], (16, 8, 640)), Z_AXES, 0, 0)
+    share = jnp.broadcast_to(share[None], (16, 8, 640))
+    mine = lax.all_to_all(share, Z_AXES, 0, 0)
     (total,) = call(total_kernel, [(264, 512)], flags, near0, near1, near2, near3, own4, *around4, scalars=1)
     mine, total = lax.optimization_barrier((mine, total))
     across_x = lax.ppermute(mine, "scen", flip(2))
@@ -464,7 +465,8 @@
         scalars=1,
         scratch=[pltpu.VMEM((16, 4, 8, 640), F32)],
     )
-    part = part + lax.ppermute(part, "scen", flip(4))
+    across, leaf_solved = lax.optimization_barrier((lax.ppermute(part, "scen", flip(4)), leaf_solved))
+    part = part + across
     others = [lax.ppermute(part, "scen", [(i, (i + by) % 32) for i in range(32)]) for by in (16, 8, 24)]
     step, parent, move = call(
         root_kernel,

time: 289 us -> 283 us (0.979); the launches traced: 288 us -> 279 us
  waiting for transfers between devices: 66.8 us -> 61.4 us
    ppermute x1, waiting for transfers between devices: 5.46 us -> 0.01 us  [body(): across_x = lax.ppermute(mine, 'scen', flip(2))]
    unnamed x70 -> x72, local copies, waits for them, and re-layouts: 11.2 us -> 10.6 us
  transfers between devices with their start and end apart: 28 -> 28, of which waited for: 11 -> 12; matrix products, arithmetic and copies ran while one was open for 2% -> 1% of each run, Pallas kernels for 15% -> 16%
where the time goes in v4:
time: 283 us; the launch traced here: 279 us
  starting transfers between devices  129 us (46%)
  Pallas kernels  69.8 us (25%)
  waiting for transfers between devices  61.4 us (22%)
  local copies, waits for them, and re-layouts  13.3 us (5%)
  other arithmetic  3.48 us (1%)
    pallas_call x12, Pallas kernels, call(): pl.pallas_call(kernel, out_shape=[jax.ShapeDtypeStruct(s, F32) for s in s...  69.8 us
    ppermute x5, starting transfers between devices, neighbours(): chip = lax.ppermute(message, AXES, TO_CHIP)  31.8 us
    ppermute x5, waiting for transfers between devices, neighbours(): other = lax.ppermute(to_half, AXES, TO_HALF)  27.2 us
    ppermute x5, starting transfers between devices, neighbours(): return (lax.ppermute(message, AXES, TO_CORE), chip, other)  16.2 us
    ppermute x1, waiting for transfers between devices, body(): pack = lax.ppermute(own_pack, AXES, MOVE_OUT)  14.5 us
    ppermute x5, waiting for transfers between devices, neighbours(): chip = lax.ppermute(message, AXES, TO_CHIP)  13.8 us
    ppermute x1, starting transfers between devices, body(): field = lax.ppermute(own_coupling.astype(F32), AXES, MOVE_OUT)  13.4 us
    ppermute x5, starting transfers between devices, neighbours(): other = lax.ppermute(to_half, AXES, TO_HALF)  12 us
  transfers between devices with their start and end apart: 28, of which 12 were waited for; matrix products, arithmetic and copies ran while one was open for 1% of the time, Pallas kernels for 16%

profile of v4, /device:TPU:1, one launch (start us, length us, event | category | flops | bytes accessed | tf_op | source)
XLA Modules:
  0.0 278.6 jit_solution(9800461619482226353)
XLA Ops:
  1.7 13.4 %collective-permute-start.1 = (f32[256,512]{1,0:T(8,128)S(1)}, f32[256,512]{1,0:T(8,128)S(1)}, u32[]{:S(2)}, u32[]{:S(2)}) collective-permute-start(f32[256,512]{1,0:T(8,128)S(1)} %bitcast_convert_fusion), channel_id=1, source_target_pairs={{0,10},{2,26},{4,8},{6,24},{8,6},{10,22},{12,4},{14,20},{1,42},{3,... | collective-permute-start | bytes 1572872 | tf_op jit(solution)/shard_map/ppermute | solution.py:409
  17.3 6.8 %shard_map.130 = (f32[256,128]{1,0:T(8,128)}, f32[136,128]{1,0:T(8,128)}) custom-call(f32[256,128]{1,0:T(8,128)} %bitcast.32, f32[8,128]{1,0:T(8,128)} %maximum_maximum_fusion.rows), custom_call_target="tpu_custom_call" | custom-call | tf_op jit(solution)/shard_map/pallas_call | solution.py:128
  26.8 14.5 %collective-permute-done.pack = f32[136,128]{1,0:T(8,128)S(1)} collective-permute-done((f32[136,128]{1,0:T(8,128)}, f32[136,128]{1,0:T(8,128)S(1)}, u32[]{:S(2)}, u32[]{:S(2)}) %collective-permute-start) | collective-permute-done | bytes 69664 | tf_op jit(solution)/shard_map/ppermute | solution.py:411
  45.3 7.3 %collective-permute-start.2 = (f32[264,512]{1,0:T(8,128)}, f32[264,512]{1,0:T(8,128)S(1)}, u32[]{:S(2)}, u32[]{:S(2)}) collective-permute-start(f32[264,512]{1,0:T(8,128)} %get-tuple-element.42.own.own0), channel_id=1, source_target_pairs={{10,26},{26,10},{8,24},{24,8},{6,22},{22,6},{4,20},{20,4},{42,58},... | collective-permute-start | bytes 1622024 | tf_op jit(solution)/shard_map/ppermute | solution.py:386
  52.7 11.8 %collective-permute-start.3 = (f32[264,512]{1,0:T(8,128)}, f32[264,512]{1,0:T(8,128)S(1)}, u32[]{:S(2)}, u32[]{:S(2)}) collective-permute-start(f32[264,512]{1,0:T(8,128)} %get-tuple-element.42.own.own0), channel_id=1, source_target_pairs={{26,8},{8,26},{24,6},{6,24},{22,4},{4,22},{58,40},{40,58},{56,38},... | collective-permute-start | bytes 1622024 | tf_op jit(solution)/shard_map/ppermute | solution.py:384
  66.4 5.6 %collective-permute-done.4.other = f32[136,512]{1,0:T(8,128)S(1)} collective-permute-done((f32[136,512]{1,0:T(8,128)}, f32[136,512]{1,0:T(8,128)S(1)}, u32[]{:S(2)}, u32[]{:S(2)}) %collective-permute-start.4) | collective-permute-done | bytes 278560 | tf_op jit(solution)/shard_map/ppermute | solution.py:385
  77.9 5.8 %collective-permute-start.6 = (f32[264,512]{1,0:T(8,128)}, f32[264,512]{1,0:T(8,128)S(1)}, u32[]{:S(2)}, u32[]{:S(2)}) collective-permute-start(f32[264,512]{1,0:T(8,128)} %get-tuple-element.48.own), channel_id=1, source_target_pairs={{26,8},{8,26},{24,6},{6,24},{22,4},{4,22},{58,40},{40,58},{56,38},... | collective-permute-start | bytes 1622024 | tf_op jit(solution)/shard_map/ppermute | solution.py:384
  85.6 5.6 %collective-permute-done.7.other = f32[136,512]{1,0:T(8,128)S(1)} collective-permute-done((f32[136,512]{1,0:T(8,128)}, f32[136,512]{1,0:T(8,128)S(1)}, u32[]{:S(2)}, u32[]{:S(2)}) %collective-permute-start.7) | collective-permute-done | bytes 278560 | tf_op jit(solution)/shard_map/ppermute | solution.py:385
  97.8 5.0 %collective-permute-start.9 = (f32[264,512]{1,0:T(8,128)}, f32[264,512]{1,0:T(8,128)S(1)}, u32[]{:S(2)}, u32[]{:S(2)}) collective-permute-start(f32[264,512]{1,0:T(8,128)} %get-tuple-element.50.own2), channel_id=1, source_target_pairs={{26,8},{8,26},{24,6},{6,24},{22,4},{4,22},{58,40},{40,58},{56,38},... | collective-permute-start | bytes 1622024 | tf_op jit(solution)/shard_map/ppermute | solution.py:384
  112.3 3.8 %shard_map.135 = (f32[264,512]{1,0:T(8,128)}, f32[2,128,384]{2,1,0:T(8,128)}, f32[2,128,384]{2,1,0:T(8,128)}) custom-call(s32[5]{0:T(128)} %stack.23.flags, f32[512,384]{1,0:T(8,128)} %get-tuple-element.46.gram, f32[8,512]{1,0:T(8,128)} %get-tuple-element.47.gather, f32[8,128]{1,0:T(8,128)} %concatenate.13.right, f32[264,512]{1,0:T(8,128)} %get-tuple-element.42.own.own0, ...), custom_call_target="tpu_custom_call" | custom-call | tf_op jit(solution)/shard_map/pallas_call | solution.py:128
  121.3 11.5 %all-to-all-start = ((f32[32,8,384]{2,1,0:T(8,128)}), f32[32,8,384]{2,1,0:T(8,128)S(1)}, u32[]{:S(2)}, u32[]{:S(2)}) async-start(f32[32,8,384]{2,1,0:T(8,128)} %bitcast.13), calls=%async_computation | async-start | bytes 786432 | tf_op jit(solution)/shard_map/all_to_all | solution.py:445
  135.0 4.5 %collective-permute-start.13 = (f32[264,512]{1,0:T(8,128)S(1)}, f32[264,512]{1,0:T(8,128)S(1)}, u32[]{:S(2)}, u32[]{:S(2)}) collective-permute-start(f32[264,512]{1,0:T(8,128)S(1)} %copy-done.9), channel_id=1, source_target_pairs={{26,8},{8,26},{24,6},{6,24},{22,4},{4,22},{58,40},{40,58},{56,38},... | collective-permute-start | bytes 1622024 | tf_op jit(solution)/shard_map/ppermute | solution.py:384
  143.5 7.8 %collective-permute-done.14.other = f32[136,512]{1,0:T(8,128)S(1)} collective-permute-done((f32[136,512]{1,0:T(8,128)S(1)}, f32[136,512]{1,0:T(8,128)S(1)}, u32[]{:S(2)}, u32[]{:S(2)}) %collective-permute-start.14) | collective-permute-done | bytes 278560 | tf_op jit(solution)/shard_map/ppermute | solution.py:385
  151.3 7.8 %collective-permute-done.13.chip = f32[264,512]{1,0:T(8,128)S(1)} collective-permute-done((f32[264,512]{1,0:T(8,128)S(1)}, f32[264,512]{1,0:T(8,128)S(1)}, u32[]{:S(2)}, u32[]{:S(2)}) %collective-permute-start.13) | collective-permute-done | bytes 540704 | tf_op jit(solution)/shard_map/ppermute | solution.py:384
  163.6 9.1 %all-to-all-start.1 = ((f32[16,8,640]{2,1,0:T(8,128)}), f32[16,8,640]{2,1,0:T(8,128)S(1)}, u32[]{:S(2)}, u32[]{:S(2)}) async-start(f32[16,8,640]{2,1,0:T(8,128)} %broadcast_in_dim.16), calls=%async_computation.1 | async-start | bytes 655360 | tf_op jit(solution)/shard_map/all_to_all | solution.py:451
  175.7 4.7 %collective-permute-start.16 = (f32[264,512]{1,0:T(8,128)S(1)}, f32[264,512]{1,0:T(8,128)S(1)}, u32[]{:S(2)}, u32[]{:S(2)}) collective-permute-start(f32[264,512]{1,0:T(8,128)S(1)} %copy-done.6), channel_id=1, source_target_pairs={{26,8},{8,26},{24,6},{6,24},{22,4},{4,22},{58,40},{40,58},{56,38},... | collective-permute-start | bytes 1622024 | tf_op jit(solution)/shard_map/ppermute | solution.py:384
  183.5 7.2 %collective-permute-done.17.other = f32[136,512]{1,0:T(8,128)S(1)} collective-permute-done((f32[136,512]{1,0:T(8,128)S(1)}, f32[136,512]{1,0:T(8,128)S(1)}, u32[]{:S(2)}, u32[]{:S(2)}) %collective-permute-start.17) | collective-permute-done | bytes 278560 | tf_op jit(solution)/shard_map/ppermute | solution.py:385
  190.7 6.0 %collective-permute-done.16.chip = f32[264,512]{1,0:T(8,128)S(1)} collective-permute-done((f32[264,512]{1,0:T(8,128)S(1)}, f32[264,512]{1,0:T(8,128)S(1)}, u32[]{:S(2)}, u32[]{:S(2)}) %collective-permute-start.16) | collective-permute-done | bytes 540704 | tf_op jit(solution)/shard_map/ppermute | solution.py:384
  203.7 7.5 %collective-permute-start.22 = (f32[264,512]{1,0:T(8,128)}, f32[264,512]{1,0:T(8,128)S(1)}, u32[]{:S(2)}, u32[]{:S(2)}) collective-permute-start(f32[264,512]{1,0:T(8,128)} %shard_map.138), channel_id=1, source_target_pairs={{10,0},{26,2},{8,4},{24,6},{6,8},{22,10},{4,12},{20,14},{42,1},{58... | collective-permute-start | bytes 1622024 | tf_op jit(solution)/shard_map/ppermute | solution.py:458
  217.6 22.9 %shard_map.139 = (f32[392,128]{1,0:T(8,128)}, f32[384,512]{1,0:T(8,128)}, f32[512,256]{1,0:T(8,128)}, f32[8,512]{1,0:T(8,128)}) custom-call(s32[5]{0:T(128)} %stack.23.flags, f32[16,8,640]{2,1,0:T(8,128)} %copy-done.2, f32[16,8,640]{2,1,0:T(8,128)} %copy-done.18, f32[16,8,640]{2,1,0:T(8,128)} %copy-done.19, f32[16,8,640]{2,1,0:T(8,128)} %copy-done.20), custom_call_target="tpu_custom_call" | custom-call | tf_op jit(solution)/shard_map/pallas_call | solution.py:128
  240.4 4.2 %collective-permute-start.21 = (f32[392,128]{1,0:T(8,128)}, f32[392,128]{1,0:T(8,128)S(1)}, u32[]{:S(2)}, u32[]{:S(2)}) collective-permute-start(f32[392,128]{1,0:T(8,128)} %get-tuple-element.64), channel_id=1, source_target_pairs={{0,64},{16,80},{32,96},{48,112},{64,0},{80,16},{96,32},{112,48},{1... | collective-permute-start | bytes 602120 | tf_op jit(solution)/shard_map/ppermute | solution.py:468
  250.3 4.8 %collective-permute-start.23 = (f32[392,128]{1,0:T(8,128)S(1)}, f32[392,128]{1,0:T(8,128)S(1)}, u32[]{:S(2)}, u32[]{:S(2)}) collective-permute-start(f32[392,128]{1,0:T(8,128)S(1)} %add.87.mine), channel_id=1, source_target_pairs={{0,256},{16,272},{32,288},{48,304},{64,320},{80,336},{96,352},{112... | collective-permute-start | bytes 602120 | tf_op jit(solution)/shard_map/ppermute | solution.py:470
  257.4 4.2 %collective-permute-start.25 = (f32[392,128]{1,0:T(8,128)S(1)}, f32[392,128]{1,0:T(8,128)S(1)}, u32[]{:S(2)}, u32[]{:S(2)}) collective-permute-start(f32[392,128]{1,0:T(8,128)S(1)} %add.87.mine), channel_id=1, source_target_pairs={{0,384},{16,400},{32,416},{48,432},{64,448},{80,464},{96,480},{112... | collective-permute-start | bytes 602120 | tf_op jit(solution)/shard_map/ppermute | solution.py:470
  264.9 13.7 %shard_map.141 = (f32[1,256]{1,0:T(1,128)}, f32[1,32]{1,0:T(1,128)}, f32[2,128]{1,0:T(2,128)}) custom-call(s32[5]{0:T(128)} %stack.23.flags, f32[392,128]{1,0:T(8,128)} %copy-done.3, f32[392,128]{1,0:T(8,128)} %copy-done.27, f32[392,128]{1,0:T(8,128)} %copy-done.28, f32[392,128]{1,0:T(8,128)} %copy-done.29, f32[256,256]{1,0:T(8,128)} %matrix.1, ...), custom_call_target="tpu_custom_call" | custom-call | tf_op jit(solution)/shard_map/pallas_call | solution.py:128
  (135 shorter events, 81.2 us)
Async XLA Ops:
  1.7 39.5 %collective-permute-start.1 = (f32[256,512]{1,0:T(8,128)S(1)}, f32[256,512]{1,0:T(8,128)S(1)}, u32[]{:S(2)}, u32[]{:S(2)}) collective-permute-start(f32[256,512]{1,0:T(8,128)S(1)} %bitcast_convert_fusion), channel_id=1, source_target_pairs={{0,10},{2,26},{4,8},{6,24},{8,6},{10,22},{12,4},{14,20},{1,42},{3,... | collective-permute-start | bytes 1572872 | tf_op jit(solution)/shard_map/ppermute | solution.py:409
  24.1 17.1 %collective-permute-start = (f32[136,128]{1,0:T(8,128)}, f32[136,128]{1,0:T(8,128)S(1)}, u32[]{:S(2)}, u32[]{:S(2)}) collective-permute-start(f32[136,128]{1,0:T(8,128)} %get-tuple-element.40), channel_id=1, source_target_pairs={{0,10},{2,26},{4,8},{6,24},{8,6},{10,22},{12,4},{14,20},{1,42},{3,... | collective-permute-start | bytes 208904 | tf_op jit(solution)/shard_map/ppermute | solution.py:411
  45.3 26.7 %collective-permute-start.2 = (f32[264,512]{1,0:T(8,128)}, f32[264,512]{1,0:T(8,128)S(1)}, u32[]{:S(2)}, u32[]{:S(2)}) collective-permute-start(f32[264,512]{1,0:T(8,128)} %get-tuple-element.42.own.own0), channel_id=1, source_target_pairs={{10,26},{26,10},{8,24},{24,8},{6,22},{22,6},{4,20},{20,4},{42,58},... | collective-permute-start | bytes 1622024 | tf_op jit(solution)/shard_map/ppermute | solution.py:386
  52.7 19.4 %collective-permute-start.3 = (f32[264,512]{1,0:T(8,128)}, f32[264,512]{1,0:T(8,128)S(1)}, u32[]{:S(2)}, u32[]{:S(2)}) collective-permute-start(f32[264,512]{1,0:T(8,128)} %get-tuple-element.42.own.own0), channel_id=1, source_target_pairs={{26,8},{8,26},{24,6},{6,24},{22,4},{4,22},{58,40},{40,58},{56,38},... | collective-permute-start | bytes 1622024 | tf_op jit(solution)/shard_map/ppermute | solution.py:384
  64.5 7.6 %collective-permute-start.4 = (f32[136,512]{1,0:T(8,128)}, f32[136,512]{1,0:T(8,128)S(1)}, u32[]{:S(2)}, u32[]{:S(2)}) collective-permute-start(f32[136,512]{1,0:T(8,128)} %get-tuple-element.44), channel_id=1, source_target_pairs={{10,42},{26,58},{8,40},{24,56},{6,38},{22,54},{4,36},{20,52},{42,1... | collective-permute-start | bytes 835592 | tf_op jit(solution)/shard_map/ppermute | solution.py:385
  76.0 15.3 %collective-permute-start.5 = (f32[264,512]{1,0:T(8,128)}, f32[264,512]{1,0:T(8,128)S(1)}, u32[]{:S(2)}, u32[]{:S(2)}) collective-permute-start(f32[264,512]{1,0:T(8,128)} %get-tuple-element.48.own), channel_id=1, source_target_pairs={{10,26},{26,10},{8,24},{24,8},{6,22},{22,6},{4,20},{20,4},{42,58},... | collective-permute-start | bytes 1622024 | tf_op jit(solution)/shard_map/ppermute | solution.py:386
  77.9 13.4 %collective-permute-start.6 = (f32[264,512]{1,0:T(8,128)}, f32[264,512]{1,0:T(8,128)S(1)}, u32[]{:S(2)}, u32[]{:S(2)}) collective-permute-start(f32[264,512]{1,0:T(8,128)} %get-tuple-element.48.own), channel_id=1, source_target_pairs={{26,8},{8,26},{24,6},{6,24},{22,4},{4,22},{58,40},{40,58},{56,38},... | collective-permute-start | bytes 1622024 | tf_op jit(solution)/shard_map/ppermute | solution.py:384
  83.7 7.6 %collective-permute-start.7 = (f32[136,512]{1,0:T(8,128)}, f32[136,512]{1,0:T(8,128)S(1)}, u32[]{:S(2)}, u32[]{:S(2)}) collective-permute-start(f32[136,512]{1,0:T(8,128)} %get-tuple-element.49), channel_id=1, source_target_pairs={{10,42},{26,58},{8,40},{24,56},{6,38},{22,54},{4,36},{20,52},{42,1... | collective-permute-start | bytes 835592 | tf_op jit(solution)/shard_map/ppermute | solution.py:385
  95.9 15.3 %collective-permute-start.8 = (f32[264,512]{1,0:T(8,128)}, f32[264,512]{1,0:T(8,128)S(1)}, u32[]{:S(2)}, u32[]{:S(2)}) collective-permute-start(f32[264,512]{1,0:T(8,128)} %get-tuple-element.50.own2), channel_id=1, source_target_pairs={{10,26},{26,10},{8,24},{24,8},{6,22},{22,6},{4,20},{20,4},{42,58},... | collective-permute-start | bytes 1622024 | tf_op jit(solution)/shard_map/ppermute | solution.py:386
  97.8 13.4 %collective-permute-start.9 = (f32[264,512]{1,0:T(8,128)}, f32[264,512]{1,0:T(8,128)S(1)}, u32[]{:S(2)}, u32[]{:S(2)}) collective-permute-start(f32[264,512]{1,0:T(8,128)} %get-tuple-element.50.own2), channel_id=1, source_target_pairs={{26,8},{8,26},{24,6},{6,24},{22,4},{4,22},{58,40},{40,58},{56,38},... | collective-permute-start | bytes 1622024 | tf_op jit(solution)/shard_map/ppermute | solution.py:384
  102.8 8.3 %collective-permute-start.10 = (f32[136,512]{1,0:T(8,128)}, f32[136,512]{1,0:T(8,128)S(1)}, u32[]{:S(2)}, u32[]{:S(2)}) collective-permute-start(f32[136,512]{1,0:T(8,128)} %get-tuple-element.52), channel_id=1, source_target_pairs={{10,42},{26,58},{8,40},{24,56},{6,38},{22,54},{4,36},{20,52},{42,1... | collective-permute-start | bytes 835592 | tf_op jit(solution)/shard_map/ppermute | solution.py:385
  121.3 41.4 %all-to-all-start = ((f32[32,8,384]{2,1,0:T(8,128)}), f32[32,8,384]{2,1,0:T(8,128)S(1)}, u32[]{:S(2)}, u32[]{:S(2)}) async-start(f32[32,8,384]{2,1,0:T(8,128)} %bitcast.13), calls=%async_computation | async-start | bytes 786432 | tf_op jit(solution)/shard_map/all_to_all | solution.py:445
  132.8 18.5 %collective-permute-start.12 = (f32[264,512]{1,0:T(8,128)S(1)}, f32[264,512]{1,0:T(8,128)S(1)}, u32[]{:S(2)}, u32[]{:S(2)}) collective-permute-start(f32[264,512]{1,0:T(8,128)S(1)} %copy-done.9), channel_id=1, source_target_pairs={{10,26},{26,10},{8,24},{24,8},{6,22},{22,6},{4,20},{20,4},{42,58},... | collective-permute-start | bytes 1622024 | tf_op jit(solution)/shard_map/ppermute | solution.py:386
  135.0 24.1 %collective-permute-start.13 = (f32[264,512]{1,0:T(8,128)S(1)}, f32[264,512]{1,0:T(8,128)S(1)}, u32[]{:S(2)}, u32[]{:S(2)}) collective-permute-start(f32[264,512]{1,0:T(8,128)S(1)} %copy-done.9), channel_id=1, source_target_pairs={{26,8},{8,26},{24,6},{6,24},{22,4},{4,22},{58,40},{40,58},{56,38},... | collective-permute-start | bytes 1622024 | tf_op jit(solution)/shard_map/ppermute | solution.py:384
  139.6 11.7 %collective-permute-start.14 = (f32[136,512]{1,0:T(8,128)S(1)}, f32[136,512]{1,0:T(8,128)S(1)}, u32[]{:S(2)}, u32[]{:S(2)}) collective-permute-start(f32[136,512]{1,0:T(8,128)S(1)} %copy-done.33), channel_id=1, source_target_pairs={{10,42},{26,58},{8,40},{24,56},{6,38},{22,54},{4,36},{20,52},{42,1... | collective-permute-start | bytes 835592 | tf_op jit(solution)/shard_map/ppermute | solution.py:385
  163.6 36.9 %all-to-all-start.1 = ((f32[16,8,640]{2,1,0:T(8,128)}), f32[16,8,640]{2,1,0:T(8,128)S(1)}, u32[]{:S(2)}, u32[]{:S(2)}) async-start(f32[16,8,640]{2,1,0:T(8,128)} %broadcast_in_dim.16), calls=%async_computation.1 | async-start | bytes 655360 | tf_op jit(solution)/shard_map/all_to_all | solution.py:451
  172.8 17.9 %collective-permute-start.15 = (f32[264,512]{1,0:T(8,128)S(1)}, f32[264,512]{1,0:T(8,128)S(1)}, u32[]{:S(2)}, u32[]{:S(2)}) collective-permute-start(f32[264,512]{1,0:T(8,128)S(1)} %copy-done.6), channel_id=1, source_target_pairs={{10,26},{26,10},{8,24},{24,8},{6,22},{22,6},{4,20},{20,4},{42,58},... | collective-permute-start | bytes 1622024 | tf_op jit(solution)/shard_map/ppermute | solution.py:386
  175.7 21.0 %collective-permute-start.16 = (f32[264,512]{1,0:T(8,128)S(1)}, f32[264,512]{1,0:T(8,128)S(1)}, u32[]{:S(2)}, u32[]{:S(2)}) collective-permute-start(f32[264,512]{1,0:T(8,128)S(1)} %copy-done.6), channel_id=1, source_target_pairs={{26,8},{8,26},{24,6},{6,24},{22,4},{4,22},{58,40},{40,58},{56,38},... | collective-permute-start | bytes 1622024 | tf_op jit(solution)/shard_map/ppermute | solution.py:384
  180.3 10.3 %collective-permute-start.17 = (f32[136,512]{1,0:T(8,128)S(1)}, f32[136,512]{1,0:T(8,128)S(1)}, u32[]{:S(2)}, u32[]{:S(2)}) collective-permute-start(f32[136,512]{1,0:T(8,128)S(1)} %copy-done.34), channel_id=1, source_target_pairs={{10,42},{26,58},{8,40},{24,56},{6,38},{22,54},{4,36},{20,52},{42,1... | collective-permute-start | bytes 835592 | tf_op jit(solution)/shard_map/ppermute | solution.py:385
  200.6 12.6 %collective-permute-start.18 = (f32[16,8,640]{2,1,0:T(8,128)S(1)}, f32[16,8,640]{2,1,0:T(8,128)S(1)}, u32[]{:S(2)}, u32[]{:S(2)}) collective-permute-start(f32[16,8,640]{2,1,0:T(8,128)S(1)} %all-to-all-done.1.mine), channel_id=1, source_target_pairs={{0,32},{16,48},{32,0},{48,16},{64,96},{80,112},{96,64},{112,80},{1... | collective-permute-start | bytes 983048 | tf_op jit(solution)/shard_map/ppermute | solution.py:454
  203.7 40.9 %collective-permute-start.22 = (f32[264,512]{1,0:T(8,128)}, f32[264,512]{1,0:T(8,128)S(1)}, u32[]{:S(2)}, u32[]{:S(2)}) collective-permute-start(f32[264,512]{1,0:T(8,128)} %shard_map.138), channel_id=1, source_target_pairs={{10,0},{26,2},{8,4},{24,6},{6,8},{22,10},{4,12},{20,14},{42,1},{58... | collective-permute-start | bytes 1622024 | tf_op jit(solution)/shard_map/ppermute | solution.py:458
  240.4 9.8 %collective-permute-start.21 = (f32[392,128]{1,0:T(8,128)}, f32[392,128]{1,0:T(8,128)S(1)}, u32[]{:S(2)}, u32[]{:S(2)}) collective-permute-start(f32[392,128]{1,0:T(8,128)} %get-tuple-element.64), channel_id=1, source_target_pairs={{0,64},{16,80},{32,96},{48,112},{64,0},{80,16},{96,32},{112,48},{1... | collective-permute-start | bytes 602120 | tf_op jit(solution)/shard_map/ppermute | solution.py:468
  250.3 11.3 %collective-permute-start.23 = (f32[392,128]{1,0:T(8,128)S(1)}, f32[392,128]{1,0:T(8,128)S(1)}, u32[]{:S(2)}, u32[]{:S(2)}) collective-permute-start(f32[392,128]{1,0:T(8,128)S(1)} %add.87.mine), channel_id=1, source_target_pairs={{0,256},{16,272},{32,288},{48,304},{64,320},{80,336},{96,352},{112... | collective-permute-start | bytes 602120 | tf_op jit(solution)/shard_map/ppermute | solution.py:470
  255.1 8.4 %collective-permute-start.24 = (f32[392,128]{1,0:T(8,128)S(1)}, f32[392,128]{1,0:T(8,128)S(1)}, u32[]{:S(2)}, u32[]{:S(2)}) collective-permute-start(f32[392,128]{1,0:T(8,128)S(1)} %add.87.mine), channel_id=1, source_target_pairs={{0,128},{16,144},{32,160},{48,176},{64,192},{80,208},{96,224},{112... | collective-permute-start | bytes 602120 | tf_op jit(solution)/shard_map/ppermute | solution.py:470
  (40 other events, 323.7 us)

commit v5 on v4

--- a/solution.py
+++ b/solution.py
@@ -24,8 +24,8 @@
     return linear(group * 4 + leaf, half * 8 + cell)
 
 
-def away(group, leaf, half, cell):
-    column = half ^ (leaf // 2)
+def away(group, leaf, half, cell, side=0):
+    column = half ^ (leaf // 2) ^ side
     z = (4 * QUARTER[leaf] + 3 - cell // 2 + Z_SHIFT) % 16
     return linear(group * 4 + column * 2 + cell % 2, z)
 
@@ -39,6 +39,7 @@
 
 
 MOVE_OUT = [(home(*at), away(*at)) for at in every_cell()]
+MOVE_SIDE = [(home(*at), away(*at, 1)) for at in every_cell()]
 MOVE_BACK = [(there, here) for here, there in MOVE_OUT]
 TO_CORE = [(away(g, l, h, c), away(g, l, h, c ^ 1)) for g, l, h, c in every_cell()]
 TO_HALF = [(away(g, l, h, c), away(g, l, h ^ 1, c)) for g, l, h, c in every_cell()]
@@ -163,7 +164,7 @@
     out[128:129, 0:128] = jnp.where(early, rows[1], rows[0])
 
 
-def start_kernel(flags, pack, coupling, first, scaled, message, to_half):
+def start_kernel(flags, pack, early, later, scaled, message, to_half):
     row, column = triangles()
     packed = pack[0:128]
     turned = packed.T
@@ -180,8 +181,7 @@
         down = across.T
         inverse = inverses_here[t]
         scaled[at] = down * inverse * across
-        field = dot3(inverse, coupling[at])
-        first[at] = field
+        field = dot3(inverse, (early, later)[t][...])
         blocks.append(jnp.concatenate([down] * 4, axis=1) * field)
         message[at] = blocks[t]
         rows.append(dot(pack[128 + t : 129 + t], inverse) * weight)
@@ -253,25 +253,45 @@
     return jnp.concatenate(parts, axis=1)
 
 
-def gram_early_kernel(pack, coupling, first, own, near, gram, gather):
+def gram_home_kernel(inverse, rows, coupling, right, gram, gather, first):
+    row = -jnp.concatenate([right[i : i + 1] for i in range(4)], axis=1)
+    for t in range(2):
+        at = slice(t * 128, t * 128 + 128)
+        first[at] = dot3(inverse[at], coupling[at].astype(F32))
+        row = row + dot(rows[t : t + 1], first[at])
+    gather[0:8] = jnp.broadcast_to(row, (8, 512))
+    high, low = split(first[...])
     for b in range(4):
         count = 3 if b < 2 else 2
         at = slice(b * 128, b * 128 + 128)
-        part = dot3(coupling[0:256, at], ring_columns(first, b, count), TN)
-        part = part + dot3(own[0:256, at], ring_columns(near, b, count), TN)
+        left = coupling[0:256, at]
+        part = None
+        for piece in (high, low):
+            wide = ring_columns(piece, b, count)
+            term = lax.dot_general(left, wide, ((TN), ((), ())), preferred_element_type=F32)
+            part = term if part is None else part + term
         gram[at, 0 : count * 128] = part
         if count == 2:
             gram[at, 256:384] = jnp.zeros((128, 128), F32)
-    row = jnp.zeros((1, 512), F32)
-    for t in range(2):
-        at = slice(t * 128, t * 128 + 128)
-        row = row + dot(pack[128 + t : 129 + t], first[at])
+
+
+def gram_early_kernel(known, known_gather, own, near, gram, gather):
+    for b in range(4):
+        count = 3 if b < 2 else 2
+        at = slice(b * 128, b * 128 + 128)
+        part = dot3(own[0:256, at], ring_columns(near, b, count), TN)
+        gram[at, 0 : count * 128] = known[at, 0 : count * 128] + part
+        if count == 2:
+            gram[at, 256:384] = jnp.zeros((128, 128), F32)
+    row = known_gather[0:1]
+    for t in range(2):
+        at = slice(t * 128, t * 128 + 128)
         row = row + dot(near[256:257, at], own[at])
     gather[0:8] = jnp.broadcast_to(row, (8, 512))
 
 
 def gram_late_kernel(
-    flags, gram, gather, right, own0, own2, near1, own2_core, chip, other, near2, keep, send, total, both, fields
+    flags, gram, gather, own0, own2, near1, own2_core, chip, other, near2, keep, send, total, both, fields
 ):
     blocks, rows = beside(flags[0], own2, own2_core, chip, other)
     both[...] = own0[0:256] + own2[0:256]
@@ -294,7 +314,7 @@
                     extra = jnp.zeros((8, 128), F32)
                     if b == 2 and m == 0 and j == 0:
                         four = jnp.concatenate([row[:, i * 128 : i * 128 + 128] for i in range(4)], axis=0)
-                        extra = jnp.concatenate([four - right[0:4], jnp.zeros((4, 128), F32)], axis=0)
+                        extra = jnp.concatenate([four, jnp.zeros((4, 128), F32)], axis=0)
                     total[j % 2, j // 2, b * 32 + m * 8 : b * 32 + m * 8 + 8, 256:384] = extra
     keep[...] = total[flags[1]]
     send[...] = total[1 - flags[1]]
@@ -406,7 +426,8 @@
     rows = jnp.concatenate(
         [leaf_rhs[0].reshape(2, 128), weight.reshape(2, 128), jnp.zeros((4, 128), F32)], axis=0
     )
-    field = lax.ppermute(own_coupling.astype(F32), AXES, MOVE_OUT)
+    later = lax.ppermute(own_coupling[128:256].astype(F32), AXES, MOVE_SIDE)
+    early = lax.ppermute(own_coupling[0:128].astype(F32), AXES, MOVE_OUT)
     own_inverse, own_pack = call(invert_kernel, [(256, 128), (136, 128)], blocks[0].reshape(256, 128), rows)
     pack = lax.ppermute(own_pack, AXES, MOVE_OUT)
 
@@ -424,17 +445,23 @@
     right = lax.dynamic_update_slice(jnp.zeros((512,), F32), right, (strip * 32,)).reshape(4, 128)
     right = jnp.concatenate([right, jnp.zeros((4, 128), F32)], axis=0)
 
-    shapes = [(256, 512), (256, 128), (264, 512), (136, 512)]
-    first, scaled, own0, half0 = call(start_kernel, shapes, flags, pack, field, scalars=1)
+    gram, gather = call(
+        gram_home_kernel, [(512, 384), (8, 512)], own_inverse, rows, own_coupling, right,
+        scratch=[pltpu.VMEM((256, 512), F32)],
+    )
+    later, gram = lax.optimization_barrier((later, gram))
+    later = lax.ppermute(later, "scen", flip(2))
+    shapes = [(256, 128), (264, 512), (136, 512)]
+    scaled, own0, half0 = call(start_kernel, shapes, flags, pack, early, later, scalars=1)
     shapes = [(264, 512), (264, 512), (136, 512)]
     near0, own1, half1 = call(sweep_kernel, shapes, flags, scaled, own0, *neighbours(own0, half0), scalars=1)
     around1 = neighbours(own1, half1)
-    gram, gather = call(gram_early_kernel, [(512, 384), (8, 512)], pack, field, first, own0, near0)
+    gram, gather = call(gram_early_kernel, [(512, 384), (8, 512)], gram, gather, own0, near0)
     near1, own2, half2 = call(sweep_kernel, shapes, flags, scaled, own1, *around1, scalars=1)
     near2, keep, send = call(
         gram_late_kernel,
         [(264, 512), (2, 128, 384), (2, 128, 384)],
-        flags, gram, gather, right, own0, own2, near1, *neighbours(own2, half2),
+        flags, gram, gather, own0, own2, near1, *neighbours(own2, half2),
         scalars=1,
         scratch=[pltpu.VMEM((2, 2, 128, 384), F32), pltpu.VMEM((256, 512), F32), pltpu.VMEM((256, 512), F32)],
     )

time: 283 us -> 290 us (1.025)
  starting transfers between devices: 129 us -> 135 us
    ppermute x5, starting transfers between devices: 31.8 us -> 15.9 us  [neighbours(): chip = lax.ppermute(message, AXES, TO_CHIP)]
    ppermute x1, waiting for transfers between devices: 14.5 us -> 1.89 us  [body(): pack = lax.ppermute(own_pack, AXES, MOVE_OUT)]
    ppermute x5, starting transfers between devices: 12 us -> 20.4 us  [neighbours(): other = lax.ppermute(to_half, AXES, TO_HALF)]
    ppermute x1, starting transfers between devices: 1.91 us -> 9.38 us  [body(): pack = lax.ppermute(own_pack, AXES, MOVE_OUT)]
    ppermute x5, waiting for transfers between devices: 27.2 us -> 33.9 us  [neighbours(): other = lax.ppermute(to_half, AXES, TO_HALF)]
    ppermute x1 -> x3, starting transfers between devices: 13.4 us -> 18.1 us  [the longest x1 14.3 us: body(): later = lax.ppermute(own_coupling[128:256].astype(F32), AXES, MOVE_SIDE)]
    ppermute x1 -> x3, waiting for transfers between devices: 0.01 us -> 4.17 us  [the longest x1 4.16 us: body(): later = lax.ppermute(own_coupling[128:256].astype(F32), AXES, MOVE_SIDE)]
    ppermute x5, starting transfers between devices: 16.2 us -> 19.6 us  [neighbours(): return (lax.ppermute(message, AXES, TO_CORE), chip, other)]
  transfers between devices with their start and end apart: 28 -> 30, of which waited for: 12 -> 13; matrix products, arithmetic and copies ran while one was open for 1% -> 1% of each run, Pallas kernels for 16% -> 16%
where the time goes in v5:
time: 290 us; the launch traced here: 286 us
  starting transfers between devices  135 us (47%)
  Pallas kernels  72.1 us (25%)
  waiting for transfers between devices  59.5 us (21%)
  local copies, waits for them, and re-layouts  13.9 us (5%)
  other arithmetic  3.46 us (1%)
    pallas_call x13, Pallas kernels, call(): pl.pallas_call(kernel, out_shape=[jax.ShapeDtypeStruct(s, F32) for s in s...  72.1 us
    ppermute x5, waiting for transfers between devices, neighbours(): other = lax.ppermute(to_half, AXES, TO_HALF)  33.9 us
    ppermute x5, starting transfers between devices, neighbours(): other = lax.ppermute(to_half, AXES, TO_HALF)  20.4 us
    ppermute x5, starting transfers between devices, neighbours(): return (lax.ppermute(message, AXES, TO_CORE), chip, other)  19.6 us
    ppermute x5, starting transfers between devices, neighbours(): chip = lax.ppermute(message, AXES, TO_CHIP)  15.9 us
    ppermute x1, starting transfers between devices, body(): later = lax.ppermute(own_coupling[128:256].astype(F32), AXES, MOVE_SIDE)  14.3 us
    ppermute x5, waiting for transfers between devices, neighbours(): chip = lax.ppermute(message, AXES, TO_CHIP)  13.8 us
    ppermute x3, starting transfers between devices, body(): lax.ppermute(part, 'scen', [(i, (i + by) % 32) for i in range(32)])  11.3 us
  transfers between devices with their start and end apart: 30, of which 13 were waited for; matrix products, arithmetic and copies ran while one was open for 1% of the time, Pallas kernels for 16%

profile of v5, /device:TPU:1, one launch (start us, length us, event | category | flops | bytes accessed | tf_op | source)
XLA Modules:
  0.0 285.7 jit_solution(18369387247685103128)
XLA Ops:
  1.7 14.3 %collective-permute-start = (f32[128,512]{1,0:T(8,128)S(1)}, f32[128,512]{1,0:T(8,128)S(1)}, u32[]{:S(2)}, u32[]{:S(2)}) collective-permute-start(f32[128,512]{1,0:T(8,128)S(1)} %get-tuple-element.87), channel_id=1, source_target_pairs={{0,42},{2,58},{4,40},{6,56},{8,38},{10,54},{12,36},{14,52},{1,10},... | collective-permute-start | bytes 786440 | tf_op jit(solution)/shard_map/ppermute | solution.py:429
  22.8 6.8 %shard_map.130 = (f32[256,128]{1,0:T(8,128)}, f32[136,128]{1,0:T(8,128)}) custom-call(f32[256,128]{1,0:T(8,128)} %bitcast.38, f32[8,128]{1,0:T(8,128)} %maximum_maximum_fusion.rows), custom_call_target="tpu_custom_call" | custom-call | tf_op jit(solution)/shard_map/pallas_call | solution.py:129
  32.7 4.2 %collective-permute-done = f32[128,512]{1,0:T(8,128)S(1)} collective-permute-done((f32[128,512]{1,0:T(8,128)S(1)}, f32[128,512]{1,0:T(8,128)S(1)}, u32[]{:S(2)}, u32[]{:S(2)}) %collective-permute-start) | collective-permute-done | bytes 262176 | tf_op jit(solution)/shard_map/ppermute | solution.py:429
  38.8 9.4 %collective-permute-start.1 = (f32[136,128]{1,0:T(8,128)S(1)}, f32[136,128]{1,0:T(8,128)S(1)}, u32[]{:S(2)}, u32[]{:S(2)}) collective-permute-start(f32[136,128]{1,0:T(8,128)S(1)} %copy-done.36), channel_id=1, source_target_pairs={{0,10},{2,26},{4,8},{6,24},{8,6},{10,22},{12,4},{14,20},{1,42},{3,... | collective-permute-start | bytes 208904 | tf_op jit(solution)/shard_map/ppermute | solution.py:432
  54.7 9.6 %collective-permute-start.4 = (f32[264,512]{1,0:T(8,128)}, f32[264,512]{1,0:T(8,128)S(1)}, u32[]{:S(2)}, u32[]{:S(2)}) collective-permute-start(f32[264,512]{1,0:T(8,128)} %get-tuple-element.49.own.own0), channel_id=1, source_target_pairs={{10,26},{26,10},{8,24},{24,8},{6,22},{22,6},{4,20},{20,4},{42,58},... | collective-permute-start | bytes 1622024 | tf_op jit(solution)/shard_map/ppermute | solution.py:406
  67.1 7.3 %collective-permute-start.6 = (f32[136,512]{1,0:T(8,128)}, f32[136,512]{1,0:T(8,128)S(1)}, u32[]{:S(2)}, u32[]{:S(2)}) collective-permute-start(f32[136,512]{1,0:T(8,128)} %get-tuple-element.51), channel_id=1, source_target_pairs={{10,42},{26,58},{8,40},{24,56},{6,38},{22,54},{4,36},{20,52},{42,1... | collective-permute-start | bytes 835592 | tf_op jit(solution)/shard_map/ppermute | solution.py:405
  74.5 7.3 %collective-permute-done.6.other = f32[136,512]{1,0:T(8,128)S(1)} collective-permute-done((f32[136,512]{1,0:T(8,128)}, f32[136,512]{1,0:T(8,128)S(1)}, u32[]{:S(2)}, u32[]{:S(2)}) %collective-permute-start.6) | collective-permute-done | bytes 278560 | tf_op jit(solution)/shard_map/ppermute | solution.py:405
  93.7 7.2 %collective-permute-done.9.other = f32[136,512]{1,0:T(8,128)S(1)} collective-permute-done((f32[136,512]{1,0:T(8,128)}, f32[136,512]{1,0:T(8,128)S(1)}, u32[]{:S(2)}, u32[]{:S(2)}) %collective-permute-start.9) | collective-permute-done | bytes 278560 | tf_op jit(solution)/shard_map/ppermute | solution.py:405
  116.1 4.4 %collective-permute-done.12.other = f32[136,512]{1,0:T(8,128)S(1)} collective-permute-done((f32[136,512]{1,0:T(8,128)}, f32[136,512]{1,0:T(8,128)S(1)}, u32[]{:S(2)}, u32[]{:S(2)}) %collective-permute-start.12) | collective-permute-done | bytes 278560 | tf_op jit(solution)/shard_map/ppermute | solution.py:405
  121.5 3.8 %shard_map.136 = (f32[264,512]{1,0:T(8,128)}, f32[2,128,384]{2,1,0:T(8,128)}, f32[2,128,384]{2,1,0:T(8,128)}) custom-call(s32[5]{0:T(128)} %stack.23.flags, f32[512,384]{1,0:T(8,128)} %get-tuple-element.53.gram, f32[8,512]{1,0:T(8,128)} %get-tuple-element.54.gather, f32[264,512]{1,0:T(8,128)} %get-tuple-element.49.own.own0, ...), custom_call_target="tpu_custom_call" | custom-call | tf_op jit(solution)/shard_map/pallas_call | solution.py:129
  131.3 8.5 %all-to-all-start = ((f32[32,8,384]{2,1,0:T(8,128)}), f32[32,8,384]{2,1,0:T(8,128)S(1)}, u32[]{:S(2)}, u32[]{:S(2)}) async-start(f32[32,8,384]{2,1,0:T(8,128)} %bitcast.15), calls=%async_computation | async-start | bytes 786432 | tf_op jit(solution)/shard_map/all_to_all | solution.py:472
  142.0 4.5 %collective-permute-start.15 = (f32[264,512]{1,0:T(8,128)S(1)}, f32[264,512]{1,0:T(8,128)S(1)}, u32[]{:S(2)}, u32[]{:S(2)}) collective-permute-start(f32[264,512]{1,0:T(8,128)S(1)} %copy-done.6), channel_id=1, source_target_pairs={{26,8},{8,26},{24,6},{6,24},{22,4},{4,22},{58,40},{40,58},{56,38},... | collective-permute-start | bytes 1622024 | tf_op jit(solution)/shard_map/ppermute | solution.py:404
  150.5 7.8 %collective-permute-done.16.other = f32[136,512]{1,0:T(8,128)S(1)} collective-permute-done((f32[136,512]{1,0:T(8,128)S(1)}, f32[136,512]{1,0:T(8,128)S(1)}, u32[]{:S(2)}, u32[]{:S(2)}) %collective-permute-start.16) | collective-permute-done | bytes 278560 | tf_op jit(solution)/shard_map/ppermute | solution.py:405
  158.3 7.8 %collective-permute-done.15.chip = f32[264,512]{1,0:T(8,128)S(1)} collective-permute-done((f32[264,512]{1,0:T(8,128)S(1)}, f32[264,512]{1,0:T(8,128)S(1)}, u32[]{:S(2)}, u32[]{:S(2)}) %collective-permute-start.15) | collective-permute-done | bytes 540704 | tf_op jit(solution)/shard_map/ppermute | solution.py:404
  170.6 9.1 %all-to-all-start.1 = ((f32[16,8,640]{2,1,0:T(8,128)}), f32[16,8,640]{2,1,0:T(8,128)S(1)}, u32[]{:S(2)}, u32[]{:S(2)}) async-start(f32[16,8,640]{2,1,0:T(8,128)} %broadcast_in_dim.16), calls=%async_computation.1 | async-start | bytes 655360 | tf_op jit(solution)/shard_map/all_to_all | solution.py:478
  182.7 4.7 %collective-permute-start.18 = (f32[264,512]{1,0:T(8,128)S(1)}, f32[264,512]{1,0:T(8,128)S(1)}, u32[]{:S(2)}, u32[]{:S(2)}) collective-permute-start(f32[264,512]{1,0:T(8,128)S(1)} %copy-done.3), channel_id=1, source_target_pairs={{26,8},{8,26},{24,6},{6,24},{22,4},{4,22},{58,40},{40,58},{56,38},... | collective-permute-start | bytes 1622024 | tf_op jit(solution)/shard_map/ppermute | solution.py:404
  190.5 7.2 %collective-permute-done.19.other = f32[136,512]{1,0:T(8,128)S(1)} collective-permute-done((f32[136,512]{1,0:T(8,128)S(1)}, f32[136,512]{1,0:T(8,128)S(1)}, u32[]{:S(2)}, u32[]{:S(2)}) %collective-permute-start.19) | collective-permute-done | bytes 278560 | tf_op jit(solution)/shard_map/ppermute | solution.py:405
  197.7 6.0 %collective-permute-done.18.chip = f32[264,512]{1,0:T(8,128)S(1)} collective-permute-done((f32[264,512]{1,0:T(8,128)S(1)}, f32[264,512]{1,0:T(8,128)S(1)}, u32[]{:S(2)}, u32[]{:S(2)}) %collective-permute-start.18) | collective-permute-done | bytes 540704 | tf_op jit(solution)/shard_map/ppermute | solution.py:404
  210.7 7.5 %collective-permute-start.24 = (f32[264,512]{1,0:T(8,128)}, f32[264,512]{1,0:T(8,128)S(1)}, u32[]{:S(2)}, u32[]{:S(2)}) collective-permute-start(f32[264,512]{1,0:T(8,128)} %shard_map.139), channel_id=1, source_target_pairs={{10,0},{26,2},{8,4},{24,6},{6,8},{22,10},{4,12},{20,14},{42,1},{58... | collective-permute-start | bytes 1622024 | tf_op jit(solution)/shard_map/ppermute | solution.py:485
  224.6 22.8 %shard_map.140 = (f32[392,128]{1,0:T(8,128)}, f32[384,512]{1,0:T(8,128)}, f32[512,256]{1,0:T(8,128)}, f32[8,512]{1,0:T(8,128)}) custom-call(s32[5]{0:T(128)} %stack.23.flags, f32[16,8,640]{2,1,0:T(8,128)} %copy-done.1, f32[16,8,640]{2,1,0:T(8,128)} %copy-done.17, f32[16,8,640]{2,1,0:T(8,128)} %copy-done.18, f32[16,8,640]{2,1,0:T(8,128)} %copy-done.19), custom_call_target="tpu_custom_call" | custom-call | tf_op jit(solution)/shard_map/pallas_call | solution.py:129
  247.4 4.5 %collective-permute-start.23 = (f32[392,128]{1,0:T(8,128)}, f32[392,128]{1,0:T(8,128)S(1)}, u32[]{:S(2)}, u32[]{:S(2)}) collective-permute-start(f32[392,128]{1,0:T(8,128)} %get-tuple-element.71), channel_id=1, source_target_pairs={{0,64},{16,80},{32,96},{48,112},{64,0},{80,16},{96,32},{112,48},{1... | collective-permute-start | bytes 602120 | tf_op jit(solution)/shard_map/ppermute | solution.py:495
  257.4 4.8 %collective-permute-start.25 = (f32[392,128]{1,0:T(8,128)S(1)}, f32[392,128]{1,0:T(8,128)S(1)}, u32[]{:S(2)}, u32[]{:S(2)}) collective-permute-start(f32[392,128]{1,0:T(8,128)S(1)} %add.87.mine), channel_id=1, source_target_pairs={{0,256},{16,272},{32,288},{48,304},{64,320},{80,336},{96,352},{112... | collective-permute-start | bytes 602120 | tf_op jit(solution)/shard_map/ppermute | solution.py:497
  264.5 4.2 %collective-permute-start.27 = (f32[392,128]{1,0:T(8,128)S(1)}, f32[392,128]{1,0:T(8,128)S(1)}, u32[]{:S(2)}, u32[]{:S(2)}) collective-permute-start(f32[392,128]{1,0:T(8,128)S(1)} %add.87.mine), channel_id=1, source_target_pairs={{0,384},{16,400},{32,416},{48,432},{64,448},{80,464},{96,480},{112... | collective-permute-start | bytes 602120 | tf_op jit(solution)/shard_map/ppermute | solution.py:497
  272.0 13.7 %shard_map.142 = (f32[1,256]{1,0:T(1,128)}, f32[1,32]{1,0:T(1,128)}, f32[2,128]{1,0:T(2,128)}) custom-call(s32[5]{0:T(128)} %stack.23.flags, f32[392,128]{1,0:T(8,128)} %copy-done.2, f32[392,128]{1,0:T(8,128)} %copy-done.27, f32[392,128]{1,0:T(8,128)} %copy-done.28, f32[392,128]{1,0:T(8,128)} %copy-done.29, f32[256,256]{1,0:T(8,128)} %matrix.1, ...), custom_call_target="tpu_custom_call" | custom-call | tf_op jit(solution)/shard_map/pallas_call | solution.py:129
  (144 shorter events, 96.4 us)
Async XLA Ops:
  1.7 35.1 %collective-permute-start = (f32[128,512]{1,0:T(8,128)S(1)}, f32[128,512]{1,0:T(8,128)S(1)}, u32[]{:S(2)}, u32[]{:S(2)}) collective-permute-start(f32[128,512]{1,0:T(8,128)S(1)} %get-tuple-element.87), channel_id=1, source_target_pairs={{0,42},{2,58},{4,40},{6,56},{8,38},{10,54},{12,36},{14,52},{1,10},... | collective-permute-start | bytes 786440 | tf_op jit(solution)/shard_map/ppermute | solution.py:429
  16.1 34.8 %collective-permute-start.2 = (f32[128,512]{1,0:T(8,128)S(1)}, f32[128,512]{1,0:T(8,128)S(1)}, u32[]{:S(2)}, u32[]{:S(2)}) collective-permute-start(f32[128,512]{1,0:T(8,128)S(1)} %get-tuple-element.86), channel_id=1, source_target_pairs={{0,10},{2,26},{4,8},{6,24},{8,6},{10,22},{12,4},{14,20},{1,42},{3,... | collective-permute-start | bytes 786440 | tf_op jit(solution)/shard_map/ppermute | solution.py:430
  36.8 14.0 %collective-permute-start.3 = (f32[128,512]{1,0:T(8,128)S(1)}, f32[128,512]{1,0:T(8,128)S(1)}, u32[]{:S(2)}, u32[]{:S(2)}) collective-permute-start(f32[128,512]{1,0:T(8,128)S(1)} %collective-permute-done), channel_id=1, source_target_pairs={{0,32},{16,48},{32,0},{48,16},{64,96},{80,112},{96,64},{112,80},{1... | collective-permute-start | bytes 786440 | tf_op jit(solution)/shard_map/ppermute | solution.py:453
  38.8 12.1 %collective-permute-start.1 = (f32[136,128]{1,0:T(8,128)S(1)}, f32[136,128]{1,0:T(8,128)S(1)}, u32[]{:S(2)}, u32[]{:S(2)}) collective-permute-start(f32[136,128]{1,0:T(8,128)S(1)} %copy-done.36), channel_id=1, source_target_pairs={{0,10},{2,26},{4,8},{6,24},{8,6},{10,22},{12,4},{14,20},{1,42},{3,... | collective-permute-start | bytes 208904 | tf_op jit(solution)/shard_map/ppermute | solution.py:432
  54.7 27.1 %collective-permute-start.4 = (f32[264,512]{1,0:T(8,128)}, f32[264,512]{1,0:T(8,128)S(1)}, u32[]{:S(2)}, u32[]{:S(2)}) collective-permute-start(f32[264,512]{1,0:T(8,128)} %get-tuple-element.49.own.own0), channel_id=1, source_target_pairs={{10,26},{26,10},{8,24},{24,8},{6,22},{22,6},{4,20},{20,4},{42,58},... | collective-permute-start | bytes 1622024 | tf_op jit(solution)/shard_map/ppermute | solution.py:406
  64.3 17.4 %collective-permute-start.5 = (f32[264,512]{1,0:T(8,128)}, f32[264,512]{1,0:T(8,128)S(1)}, u32[]{:S(2)}, u32[]{:S(2)}) collective-permute-start(f32[264,512]{1,0:T(8,128)} %get-tuple-element.49.own.own0), channel_id=1, source_target_pairs={{26,8},{8,26},{24,6},{6,24},{22,4},{4,22},{58,40},{40,58},{56,38},... | collective-permute-start | bytes 1622024 | tf_op jit(solution)/shard_map/ppermute | solution.py:404
  67.1 14.7 %collective-permute-start.6 = (f32[136,512]{1,0:T(8,128)}, f32[136,512]{1,0:T(8,128)S(1)}, u32[]{:S(2)}, u32[]{:S(2)}) collective-permute-start(f32[136,512]{1,0:T(8,128)} %get-tuple-element.51), channel_id=1, source_target_pairs={{10,42},{26,58},{8,40},{24,56},{6,38},{22,54},{4,36},{20,52},{42,1... | collective-permute-start | bytes 835592 | tf_op jit(solution)/shard_map/ppermute | solution.py:405
  85.7 15.2 %collective-permute-start.7 = (f32[264,512]{1,0:T(8,128)}, f32[264,512]{1,0:T(8,128)S(1)}, u32[]{:S(2)}, u32[]{:S(2)}) collective-permute-start(f32[264,512]{1,0:T(8,128)} %get-tuple-element.55.own), channel_id=1, source_target_pairs={{10,26},{26,10},{8,24},{24,8},{6,22},{22,6},{4,20},{20,4},{42,58},... | collective-permute-start | bytes 1622024 | tf_op jit(solution)/shard_map/ppermute | solution.py:406
  88.1 12.8 %collective-permute-start.8 = (f32[264,512]{1,0:T(8,128)}, f32[264,512]{1,0:T(8,128)S(1)}, u32[]{:S(2)}, u32[]{:S(2)}) collective-permute-start(f32[264,512]{1,0:T(8,128)} %get-tuple-element.55.own), channel_id=1, source_target_pairs={{26,8},{8,26},{24,6},{6,24},{22,4},{4,22},{58,40},{40,58},{56,38},... | collective-permute-start | bytes 1622024 | tf_op jit(solution)/shard_map/ppermute | solution.py:404
  90.0 10.9 %collective-permute-start.9 = (f32[136,512]{1,0:T(8,128)}, f32[136,512]{1,0:T(8,128)S(1)}, u32[]{:S(2)}, u32[]{:S(2)}) collective-permute-start(f32[136,512]{1,0:T(8,128)} %get-tuple-element.56), channel_id=1, source_target_pairs={{10,42},{26,58},{8,40},{24,56},{6,38},{22,54},{4,36},{20,52},{42,1... | collective-permute-start | bytes 835592 | tf_op jit(solution)/shard_map/ppermute | solution.py:405
  105.5 15.0 %collective-permute-start.10 = (f32[264,512]{1,0:T(8,128)}, f32[264,512]{1,0:T(8,128)S(1)}, u32[]{:S(2)}, u32[]{:S(2)}) collective-permute-start(f32[264,512]{1,0:T(8,128)} %get-tuple-element.57.own2), channel_id=1, source_target_pairs={{10,26},{26,10},{8,24},{24,8},{6,22},{22,6},{4,20},{20,4},{42,58},... | collective-permute-start | bytes 1622024 | tf_op jit(solution)/shard_map/ppermute | solution.py:406
  107.9 12.5 %collective-permute-start.11 = (f32[264,512]{1,0:T(8,128)}, f32[264,512]{1,0:T(8,128)S(1)}, u32[]{:S(2)}, u32[]{:S(2)}) collective-permute-start(f32[264,512]{1,0:T(8,128)} %get-tuple-element.57.own2), channel_id=1, source_target_pairs={{26,8},{8,26},{24,6},{6,24},{22,4},{4,22},{58,40},{40,58},{56,38},... | collective-permute-start | bytes 1622024 | tf_op jit(solution)/shard_map/ppermute | solution.py:404
  110.0 10.4 %collective-permute-start.12 = (f32[136,512]{1,0:T(8,128)}, f32[136,512]{1,0:T(8,128)S(1)}, u32[]{:S(2)}, u32[]{:S(2)}) collective-permute-start(f32[136,512]{1,0:T(8,128)} %get-tuple-element.59), channel_id=1, source_target_pairs={{10,42},{26,58},{8,40},{24,56},{6,38},{22,54},{4,36},{20,52},{42,1... | collective-permute-start | bytes 835592 | tf_op jit(solution)/shard_map/ppermute | solution.py:405
  131.3 38.5 %all-to-all-start = ((f32[32,8,384]{2,1,0:T(8,128)}), f32[32,8,384]{2,1,0:T(8,128)S(1)}, u32[]{:S(2)}, u32[]{:S(2)}) async-start(f32[32,8,384]{2,1,0:T(8,128)} %bitcast.15), calls=%async_computation | async-start | bytes 786432 | tf_op jit(solution)/shard_map/all_to_all | solution.py:472
  139.8 18.5 %collective-permute-start.14 = (f32[264,512]{1,0:T(8,128)S(1)}, f32[264,512]{1,0:T(8,128)S(1)}, u32[]{:S(2)}, u32[]{:S(2)}) collective-permute-start(f32[264,512]{1,0:T(8,128)S(1)} %copy-done.6), channel_id=1, source_target_pairs={{10,26},{26,10},{8,24},{24,8},{6,22},{22,6},{4,20},{20,4},{42,58},... | collective-permute-start | bytes 1622024 | tf_op jit(solution)/shard_map/ppermute | solution.py:406
  142.0 24.1 %collective-permute-start.15 = (f32[264,512]{1,0:T(8,128)S(1)}, f32[264,512]{1,0:T(8,128)S(1)}, u32[]{:S(2)}, u32[]{:S(2)}) collective-permute-start(f32[264,512]{1,0:T(8,128)S(1)} %copy-done.6), channel_id=1, source_target_pairs={{26,8},{8,26},{24,6},{6,24},{22,4},{4,22},{58,40},{40,58},{56,38},... | collective-permute-start | bytes 1622024 | tf_op jit(solution)/shard_map/ppermute | solution.py:404
  146.6 11.7 %collective-permute-start.16 = (f32[136,512]{1,0:T(8,128)S(1)}, f32[136,512]{1,0:T(8,128)S(1)}, u32[]{:S(2)}, u32[]{:S(2)}) collective-permute-start(f32[136,512]{1,0:T(8,128)S(1)} %copy-done.34), channel_id=1, source_target_pairs={{10,42},{26,58},{8,40},{24,56},{6,38},{22,54},{4,36},{20,52},{42,1... | collective-permute-start | bytes 835592 | tf_op jit(solution)/shard_map/ppermute | solution.py:405
  170.6 36.9 %all-to-all-start.1 = ((f32[16,8,640]{2,1,0:T(8,128)}), f32[16,8,640]{2,1,0:T(8,128)S(1)}, u32[]{:S(2)}, u32[]{:S(2)}) async-start(f32[16,8,640]{2,1,0:T(8,128)} %broadcast_in_dim.16), calls=%async_computation.1 | async-start | bytes 655360 | tf_op jit(solution)/shard_map/all_to_all | solution.py:478
  179.8 17.9 %collective-permute-start.17 = (f32[264,512]{1,0:T(8,128)S(1)}, f32[264,512]{1,0:T(8,128)S(1)}, u32[]{:S(2)}, u32[]{:S(2)}) collective-permute-start(f32[264,512]{1,0:T(8,128)S(1)} %copy-done.3), channel_id=1, source_target_pairs={{10,26},{26,10},{8,24},{24,8},{6,22},{22,6},{4,20},{20,4},{42,58},... | collective-permute-start | bytes 1622024 | tf_op jit(solution)/shard_map/ppermute | solution.py:406
  182.7 21.0 %collective-permute-start.18 = (f32[264,512]{1,0:T(8,128)S(1)}, f32[264,512]{1,0:T(8,128)S(1)}, u32[]{:S(2)}, u32[]{:S(2)}) collective-permute-start(f32[264,512]{1,0:T(8,128)S(1)} %copy-done.3), channel_id=1, source_target_pairs={{26,8},{8,26},{24,6},{6,24},{22,4},{4,22},{58,40},{40,58},{56,38},... | collective-permute-start | bytes 1622024 | tf_op jit(solution)/shard_map/ppermute | solution.py:404
  187.3 10.3 %collective-permute-start.19 = (f32[136,512]{1,0:T(8,128)S(1)}, f32[136,512]{1,0:T(8,128)S(1)}, u32[]{:S(2)}, u32[]{:S(2)}) collective-permute-start(f32[136,512]{1,0:T(8,128)S(1)} %copy-done.35), channel_id=1, source_target_pairs={{10,42},{26,58},{8,40},{24,56},{6,38},{22,54},{4,36},{20,52},{42,1... | collective-permute-start | bytes 835592 | tf_op jit(solution)/shard_map/ppermute | solution.py:405
  207.5 12.6 %collective-permute-start.20 = (f32[16,8,640]{2,1,0:T(8,128)S(1)}, f32[16,8,640]{2,1,0:T(8,128)S(1)}, u32[]{:S(2)}, u32[]{:S(2)}) collective-permute-start(f32[16,8,640]{2,1,0:T(8,128)S(1)} %all-to-all-done.1.mine), channel_id=1, source_target_pairs={{0,32},{16,48},{32,0},{48,16},{64,96},{80,112},{96,64},{112,80},{1... | collective-permute-start | bytes 983048 | tf_op jit(solution)/shard_map/ppermute | solution.py:481
  210.7 41.2 %collective-permute-start.24 = (f32[264,512]{1,0:T(8,128)}, f32[264,512]{1,0:T(8,128)S(1)}, u32[]{:S(2)}, u32[]{:S(2)}) collective-permute-start(f32[264,512]{1,0:T(8,128)} %shard_map.139), channel_id=1, source_target_pairs={{10,0},{26,2},{8,4},{24,6},{6,8},{22,10},{4,12},{20,14},{42,1},{58... | collective-permute-start | bytes 1622024 | tf_op jit(solution)/shard_map/ppermute | solution.py:485
  257.4 11.3 %collective-permute-start.25 = (f32[392,128]{1,0:T(8,128)S(1)}, f32[392,128]{1,0:T(8,128)S(1)}, u32[]{:S(2)}, u32[]{:S(2)}) collective-permute-start(f32[392,128]{1,0:T(8,128)S(1)} %add.87.mine), channel_id=1, source_target_pairs={{0,256},{16,272},{32,288},{48,304},{64,320},{80,336},{96,352},{112... | collective-permute-start | bytes 602120 | tf_op jit(solution)/shard_map/ppermute | solution.py:497
  (44 other events, 345.5 us)

commit v6 on v5

--- a/solution.py
+++ b/solution.py
@@ -24,8 +24,8 @@
     return linear(group * 4 + leaf, half * 8 + cell)
 
 
-def away(group, leaf, half, cell, side=0):
-    column = half ^ (leaf // 2) ^ side
+def away(group, leaf, half, cell):
+    column = half ^ (leaf // 2)
     z = (4 * QUARTER[leaf] + 3 - cell // 2 + Z_SHIFT) % 16
     return linear(group * 4 + column * 2 + cell % 2, z)
 
@@ -39,7 +39,6 @@
 
 
 MOVE_OUT = [(home(*at), away(*at)) for at in every_cell()]
-MOVE_SIDE = [(home(*at), away(*at, 1)) for at in every_cell()]
 MOVE_BACK = [(there, here) for here, there in MOVE_OUT]
 TO_CORE = [(away(g, l, h, c), away(g, l, h, c ^ 1)) for g, l, h, c in every_cell()]
 TO_HALF = [(away(g, l, h, c), away(g, l, h ^ 1, c)) for g, l, h, c in every_cell()]
@@ -164,7 +163,7 @@
     out[128:129, 0:128] = jnp.where(early, rows[1], rows[0])
 
 
-def start_kernel(flags, pack, early, later, scaled, message, to_half):
+def start_kernel(flags, pack, coupling, scaled, message, to_half):
     row, column = triangles()
     packed = pack[0:128]
     turned = packed.T
@@ -181,7 +180,7 @@
         down = across.T
         inverse = inverses_here[t]
         scaled[at] = down * inverse * across
-        field = dot3(inverse, (early, later)[t][...])
+        field = dot3(inverse, coupling[at])
         blocks.append(jnp.concatenate([down] * 4, axis=1) * field)
         message[at] = blocks[t]
         rows.append(dot(pack[128 + t : 129 + t], inverse) * weight)
@@ -360,7 +359,7 @@
             rhs[i] = rhs[i] - change[:, (4 - i) * 128 :]
             rows[i] = rows[i] - dot(row, left)
             upper[b * 128 : b * 128 + 128, i * 128 : i * 128 + 128] = wide[:, skip : skip + 128]
-        part = part + dot(rhs[b], done, TN)
+        part = part + dot3(rhs[b], done, TN)
         part_row = part_row + dot(row, rhs[b])
     root_part[0:128] = part[0:128, 0:128]
     root_part[128:256] = part[0:128, 128:256]
@@ -369,8 +368,25 @@
     root_part[388:392] = jnp.broadcast_to(part_row[:, 128:256], (4, 128))
 
 
+def back_kernel(upper, solved, solved_row, leaf_solved, pulled, link_solved, vector, reach, base):
+    pieces, rows = [None] * 4, [None] * 4
+    for b in range(3, -1, -1):
+        at = slice(b * 128, b * 128 + 128)
+        piece, row = solved[at], solved_row[0:1, at]
+        if b < 3:
+            after = upper[at, b * 128 + 128 : 512]
+            piece = piece - dot(after, jnp.concatenate(pieces[b + 1 :], axis=0))
+            row = row - dot(jnp.concatenate(rows[b + 1 :], axis=1), after, NT)
+        pieces[b], rows[b] = piece, row
+        link_solved[at] = piece
+    whole = jnp.concatenate(rows, axis=1)
+    vector[...] = jnp.broadcast_to(whole, (8, 512))
+    reach[...] = dot(leaf_solved[...], jnp.concatenate(pieces, axis=0))
+    base[...] = jnp.broadcast_to(pulled[0:1] - dot(whole, leaf_solved[...], NT), (8, 256))
+
+
 def root_kernel(
-    flags, mine, opposite, below, above, matrix, right, upper, solved, solved_row, leaf_solved, pulled, step, parent, move,
+    flags, mine, opposite, below, above, matrix, right, link_solved, vector, reach, base, step, parent, move
 ):
     part = (mine[...] + opposite[...]) + (below[...] + above[...])
     side = matrix[0:128, 128:256] + part[128:256]
@@ -382,22 +398,15 @@
     head = head - dot(tail, pushed, NT)
     root = jnp.concatenate([head, tail], axis=1)
     step[...] = root
-    pieces = [None] * 4
-    for b in range(3, -1, -1):
-        at = slice(b * 128, b * 128 + 128)
-        value = solved_row[0:1, at] + dot(root, solved[at], NT)
-        for j in range(b + 1, 4):
-            value = value - dot(pieces[j], upper[at, j * 128 : j * 128 + 128], NT)
-        pieces[b] = value
+    whole = vector[0:1] + dot(root, link_solved[...], NT)
+    last = base[0:1] - dot(root, reach[...], NT)
+    for t in range(2):
+        move[t : t + 1] = last[:, t * 128 : t * 128 + 128]
     chosen = jnp.zeros((1, 128), F32)
     for b in range(4):
-        chosen = chosen + jnp.where(flags[3] == b, pieces[b], 0.0)
+        chosen = chosen + jnp.where(flags[3] == b, whole[:, b * 128 : b * 128 + 128], 0.0)
     chosen = pltpu.roll(jnp.broadcast_to(chosen, (8, 128)), flags[4], 1)
     parent[...] = chosen[0:1, 0:32]
-    whole = jnp.concatenate(pieces, axis=1)
-    for t in range(2):
-        at = slice(t * 128, t * 128 + 128)
-        move[t : t + 1] = pulled[0:1, at] - dot(whole, leaf_solved[at], NT)
 
 
 def neighbours(message, to_half):
@@ -426,8 +435,7 @@
     rows = jnp.concatenate(
         [leaf_rhs[0].reshape(2, 128), weight.reshape(2, 128), jnp.zeros((4, 128), F32)], axis=0
     )
-    later = lax.ppermute(own_coupling[128:256].astype(F32), AXES, MOVE_SIDE)
-    early = lax.ppermute(own_coupling[0:128].astype(F32), AXES, MOVE_OUT)
+    field = lax.ppermute(own_coupling.astype(F32), AXES, MOVE_OUT)
     own_inverse, own_pack = call(invert_kernel, [(256, 128), (136, 128)], blocks[0].reshape(256, 128), rows)
     pack = lax.ppermute(own_pack, AXES, MOVE_OUT)
 
@@ -449,10 +457,9 @@
         gram_home_kernel, [(512, 384), (8, 512)], own_inverse, rows, own_coupling, right,
         scratch=[pltpu.VMEM((256, 512), F32)],
     )
-    later, gram = lax.optimization_barrier((later, gram))
-    later = lax.ppermute(later, "scen", flip(2))
+    pack, gram = lax.optimization_barrier((pack, gram))
     shapes = [(256, 128), (264, 512), (136, 512)]
-    scaled, own0, half0 = call(start_kernel, shapes, flags, pack, early, later, scalars=1)
+    scaled, own0, half0 = call(start_kernel, shapes, flags, pack, field, scalars=1)
     shapes = [(264, 512), (264, 512), (136, 512)]
     near0, own1, half1 = call(sweep_kernel, shapes, flags, scaled, own0, *neighbours(own0, half0), scalars=1)
     around1 = neighbours(own1, half1)
@@ -495,10 +502,14 @@
     across, leaf_solved = lax.optimization_barrier((lax.ppermute(part, "scen", flip(4)), leaf_solved))
     part = part + across
     others = [lax.ppermute(part, "scen", [(i, (i + by) % 32) for i in range(32)]) for by in (16, 8, 24)]
+    link_solved, vector, reach, base = call(
+        back_kernel, [(512, 256), (8, 512), (256, 256), (8, 256)], upper, solved, solved_row, leaf_solved, pulled
+    )
+    others[2], link_solved = lax.optimization_barrier((others[2], link_solved))
     step, parent, move = call(
         root_kernel,
         [(1, 256), (1, 32), (2, 128)],
-        flags, part, *others, root_mat, root_rhs.reshape(1, 256), upper, solved, solved_row, leaf_solved, pulled,
+        flags, part, *others, root_mat, root_rhs.reshape(1, 256), link_solved, vector, reach, base,
         scalars=1,
     )
     return move.reshape(1, 2, 1, 128), parent, step.reshape(256)

time: 290 us -> 284 us (0.979)
  starting transfers between devices: 135 us -> 127 us
    ppermute x5, starting transfers between devices: 15.9 us -> 31.8 us  [neighbours(): chip = lax.ppermute(message, AXES, TO_CHIP)]
    ppermute x5, starting transfers between devices: 20.4 us -> 12 us  [neighbours(): other = lax.ppermute(to_half, AXES, TO_HALF)]
    ppermute x1, waiting for transfers between devices: 1.89 us -> 9.43 us  [body(): pack = lax.ppermute(own_pack, AXES, MOVE_OUT)]
    ppermute x1, starting transfers between devices: 9.38 us -> 1.91 us  [body(): pack = lax.ppermute(own_pack, AXES, MOVE_OUT)]
    ppermute x3 -> x1, starting transfers between devices: 18.1 us -> 13.4 us  [body(): field = lax.ppermute(own_coupling.astype(F32), AXES, MOVE_OUT)]
    ppermute x3 -> x1, waiting for transfers between devices: 4.17 us -> 0.01 us  [body(): field = lax.ppermute(own_coupling.astype(F32), AXES, MOVE_OUT)]
    ppermute x5, waiting for transfers between devices: 33.9 us -> 29.8 us  [neighbours(): other = lax.ppermute(to_half, AXES, TO_HALF)]
    ppermute x5, starting transfers between devices: 19.6 us -> 16.2 us  [neighbours(): return (lax.ppermute(message, AXES, TO_CORE), chip, other)]
  transfers between devices with their start and end apart: 30 -> 28, of which waited for: 13 -> 11; matrix products, arithmetic and copies ran while one was open for 1% -> 1% of each run, Pallas kernels for 16% -> 18%
where the time goes in v6:
time: 284 us; the launch traced here: 281 us
  starting transfers between devices  127 us (45%)
  Pallas kernels  74.6 us (26%)
  waiting for transfers between devices  60.8 us (21%)
  local copies, waits for them, and re-layouts  13.3 us (5%)
  other arithmetic  3.47 us (1%)
    pallas_call x14, Pallas kernels, call(): pl.pallas_call(kernel, out_shape=[jax.ShapeDtypeStruct(s, F32) for s in s...  74.6 us
    ppermute x5, starting transfers between devices, neighbours(): chip = lax.ppermute(message, AXES, TO_CHIP)  31.8 us
    ppermute x5, waiting for transfers between devices, neighbours(): other = lax.ppermute(to_half, AXES, TO_HALF)  29.8 us
    ppermute x5, starting transfers between devices, neighbours(): return (lax.ppermute(message, AXES, TO_CORE), chip, other)  16.2 us
    ppermute x5, waiting for transfers between devices, neighbours(): chip = lax.ppermute(message, AXES, TO_CHIP)  13.8 us
    ppermute x1, starting transfers between devices, body(): field = lax.ppermute(own_coupling.astype(F32), AXES, MOVE_OUT)  13.4 us
    ppermute x5, starting transfers between devices, neighbours(): other = lax.ppermute(to_half, AXES, TO_HALF)  12 us
    all_to_all x1, starting transfers between devices, body(): shares = lax.all_to_all(half_sum, AXES, 0, 0, axis_index_groups=SAME_CORE)  11.4 us
  transfers between devices with their start and end apart: 28, of which 11 were waited for; matrix products, arithmetic and copies ran while one was open for 1% of the time, Pallas kernels for 18%

profile of v6, /device:TPU:1, one launch (start us, length us, event | category | flops | bytes accessed | tf_op | source)
XLA Modules:
  0.0 281.1 jit_solution(16669834685603817329)
XLA Ops:
  1.7 13.4 %collective-permute-start.1 = (f32[256,512]{1,0:T(8,128)S(1)}, f32[256,512]{1,0:T(8,128)S(1)}, u32[]{:S(2)}, u32[]{:S(2)}) collective-permute-start(f32[256,512]{1,0:T(8,128)S(1)} %bitcast_convert_fusion), channel_id=1, source_target_pairs={{0,10},{2,26},{4,8},{6,24},{8,6},{10,22},{12,4},{14,20},{1,42},{3,... | collective-permute-start | bytes 1572872 | tf_op jit(solution)/shard_map/ppermute | solution.py:438
  17.3 6.8 %shard_map.130 = (f32[256,128]{1,0:T(8,128)}, f32[136,128]{1,0:T(8,128)}) custom-call(f32[256,128]{1,0:T(8,128)} %bitcast.33, f32[8,128]{1,0:T(8,128)} %maximum_maximum_fusion.rows), custom_call_target="tpu_custom_call" | custom-call | tf_op jit(solution)/shard_map/pallas_call | solution.py:128
  31.8 9.4 %collective-permute-done.pack = f32[136,128]{1,0:T(8,128)S(1)} collective-permute-done((f32[136,128]{1,0:T(8,128)}, f32[136,128]{1,0:T(8,128)S(1)}, u32[]{:S(2)}, u32[]{:S(2)}) %collective-permute-start) | collective-permute-done | bytes 69664 | tf_op jit(solution)/shard_map/ppermute | solution.py:440
  45.1 7.3 %collective-permute-start.2 = (f32[264,512]{1,0:T(8,128)}, f32[264,512]{1,0:T(8,128)S(1)}, u32[]{:S(2)}, u32[]{:S(2)}) collective-permute-start(f32[264,512]{1,0:T(8,128)} %get-tuple-element.55.own.own0), channel_id=1, source_target_pairs={{10,26},{26,10},{8,24},{24,8},{6,22},{22,6},{4,20},{20,4},{42,58},... | collective-permute-start | bytes 1622024 | tf_op jit(solution)/shard_map/ppermute | solution.py:415
  52.4 11.8 %collective-permute-start.3 = (f32[264,512]{1,0:T(8,128)}, f32[264,512]{1,0:T(8,128)S(1)}, u32[]{:S(2)}, u32[]{:S(2)}) collective-permute-start(f32[264,512]{1,0:T(8,128)} %get-tuple-element.55.own.own0), channel_id=1, source_target_pairs={{26,8},{8,26},{24,6},{6,24},{22,4},{4,22},{58,40},{40,58},{56,38},... | collective-permute-start | bytes 1622024 | tf_op jit(solution)/shard_map/ppermute | solution.py:413
  66.2 5.6 %collective-permute-done.4.other = f32[136,512]{1,0:T(8,128)S(1)} collective-permute-done((f32[136,512]{1,0:T(8,128)}, f32[136,512]{1,0:T(8,128)S(1)}, u32[]{:S(2)}, u32[]{:S(2)}) %collective-permute-start.4) | collective-permute-done | bytes 278560 | tf_op jit(solution)/shard_map/ppermute | solution.py:414
  77.7 5.8 %collective-permute-start.6 = (f32[264,512]{1,0:T(8,128)}, f32[264,512]{1,0:T(8,128)S(1)}, u32[]{:S(2)}, u32[]{:S(2)}) collective-permute-start(f32[264,512]{1,0:T(8,128)} %get-tuple-element.61.own), channel_id=1, source_target_pairs={{26,8},{8,26},{24,6},{6,24},{22,4},{4,22},{58,40},{40,58},{56,38},... | collective-permute-start | bytes 1622024 | tf_op jit(solution)/shard_map/ppermute | solution.py:413
  85.4 5.6 %collective-permute-done.7.other = f32[136,512]{1,0:T(8,128)S(1)} collective-permute-done((f32[136,512]{1,0:T(8,128)}, f32[136,512]{1,0:T(8,128)S(1)}, u32[]{:S(2)}, u32[]{:S(2)}) %collective-permute-start.7) | collective-permute-done | bytes 278560 | tf_op jit(solution)/shard_map/ppermute | solution.py:414
  97.6 5.0 %collective-permute-start.9 = (f32[264,512]{1,0:T(8,128)}, f32[264,512]{1,0:T(8,128)S(1)}, u32[]{:S(2)}, u32[]{:S(2)}) collective-permute-start(f32[264,512]{1,0:T(8,128)} %get-tuple-element.63.own2), channel_id=1, source_target_pairs={{26,8},{8,26},{24,6},{6,24},{22,4},{4,22},{58,40},{40,58},{56,38},... | collective-permute-start | bytes 1622024 | tf_op jit(solution)/shard_map/ppermute | solution.py:413
  121.1 11.4 %all-to-all-start = ((f32[32,8,384]{2,1,0:T(8,128)}), f32[32,8,384]{2,1,0:T(8,128)S(1)}, u32[]{:S(2)}, u32[]{:S(2)}) async-start(f32[32,8,384]{2,1,0:T(8,128)} %bitcast.13), calls=%async_computation | async-start | bytes 786432 | tf_op jit(solution)/shard_map/all_to_all | solution.py:479
  134.8 4.5 %collective-permute-start.13 = (f32[264,512]{1,0:T(8,128)S(1)}, f32[264,512]{1,0:T(8,128)S(1)}, u32[]{:S(2)}, u32[]{:S(2)}) collective-permute-start(f32[264,512]{1,0:T(8,128)S(1)} %copy-done.6), channel_id=1, source_target_pairs={{26,8},{8,26},{24,6},{6,24},{22,4},{4,22},{58,40},{40,58},{56,38},... | collective-permute-start | bytes 1622024 | tf_op jit(solution)/shard_map/ppermute | solution.py:413
  143.3 7.8 %collective-permute-done.14.other = f32[136,512]{1,0:T(8,128)S(1)} collective-permute-done((f32[136,512]{1,0:T(8,128)S(1)}, f32[136,512]{1,0:T(8,128)S(1)}, u32[]{:S(2)}, u32[]{:S(2)}) %collective-permute-start.14) | collective-permute-done | bytes 278560 | tf_op jit(solution)/shard_map/ppermute | solution.py:414
  151.1 7.8 %collective-permute-done.13.chip = f32[264,512]{1,0:T(8,128)S(1)} collective-permute-done((f32[264,512]{1,0:T(8,128)S(1)}, f32[264,512]{1,0:T(8,128)S(1)}, u32[]{:S(2)}, u32[]{:S(2)}) %collective-permute-start.13) | collective-permute-done | bytes 540704 | tf_op jit(solution)/shard_map/ppermute | solution.py:413
  163.4 9.1 %all-to-all-start.1 = ((f32[16,8,640]{2,1,0:T(8,128)}), f32[16,8,640]{2,1,0:T(8,128)S(1)}, u32[]{:S(2)}, u32[]{:S(2)}) async-start(f32[16,8,640]{2,1,0:T(8,128)} %broadcast_in_dim.16), calls=%async_computation.1 | async-start | bytes 655360 | tf_op jit(solution)/shard_map/all_to_all | solution.py:485
  175.5 4.7 %collective-permute-start.16 = (f32[264,512]{1,0:T(8,128)S(1)}, f32[264,512]{1,0:T(8,128)S(1)}, u32[]{:S(2)}, u32[]{:S(2)}) collective-permute-start(f32[264,512]{1,0:T(8,128)S(1)} %copy-done.3), channel_id=1, source_target_pairs={{26,8},{8,26},{24,6},{6,24},{22,4},{4,22},{58,40},{40,58},{56,38},... | collective-permute-start | bytes 1622024 | tf_op jit(solution)/shard_map/ppermute | solution.py:413
  183.3 7.2 %collective-permute-done.17.other = f32[136,512]{1,0:T(8,128)S(1)} collective-permute-done((f32[136,512]{1,0:T(8,128)S(1)}, f32[136,512]{1,0:T(8,128)S(1)}, u32[]{:S(2)}, u32[]{:S(2)}) %collective-permute-start.17) | collective-permute-done | bytes 278560 | tf_op jit(solution)/shard_map/ppermute | solution.py:414
  190.5 6.0 %collective-permute-done.16.chip = f32[264,512]{1,0:T(8,128)S(1)} collective-permute-done((f32[264,512]{1,0:T(8,128)S(1)}, f32[264,512]{1,0:T(8,128)S(1)}, u32[]{:S(2)}, u32[]{:S(2)}) %collective-permute-start.16) | collective-permute-done | bytes 540704 | tf_op jit(solution)/shard_map/ppermute | solution.py:413
  203.5 7.5 %collective-permute-start.22 = (f32[264,512]{1,0:T(8,128)}, f32[264,512]{1,0:T(8,128)S(1)}, u32[]{:S(2)}, u32[]{:S(2)}) collective-permute-start(f32[264,512]{1,0:T(8,128)} %shard_map.139), channel_id=1, source_target_pairs={{10,0},{26,2},{8,4},{24,6},{6,8},{22,10},{4,12},{20,14},{42,1},{58... | collective-permute-start | bytes 1622024 | tf_op jit(solution)/shard_map/ppermute | solution.py:492
  217.4 22.3 %shard_map.140 = (f32[392,128]{1,0:T(8,128)}, f32[384,512]{1,0:T(8,128)}, f32[512,256]{1,0:T(8,128)}, f32[8,512]{1,0:T(8,128)}) custom-call(s32[5]{0:T(128)} %stack.23.flags, f32[16,8,640]{2,1,0:T(8,128)} %copy-done.1, f32[16,8,640]{2,1,0:T(8,128)} %copy-done.18, f32[16,8,640]{2,1,0:T(8,128)} %copy-done.19, f32[16,8,640]{2,1,0:T(8,128)} %copy-done.20), custom_call_target="tpu_custom_call" | custom-call | tf_op jit(solution)/shard_map/pallas_call | solution.py:128
  239.7 4.3 %collective-permute-start.21 = (f32[392,128]{1,0:T(8,128)}, f32[392,128]{1,0:T(8,128)S(1)}, u32[]{:S(2)}, u32[]{:S(2)}) collective-permute-start(f32[392,128]{1,0:T(8,128)} %get-tuple-element.77), channel_id=1, source_target_pairs={{0,64},{16,80},{32,96},{48,112},{64,0},{80,16},{96,32},{112,48},{1... | collective-permute-start | bytes 602120 | tf_op jit(solution)/shard_map/ppermute | solution.py:502
  249.7 4.6 %collective-permute-start.25 = (f32[392,128]{1,0:T(8,128)S(1)}, f32[392,128]{1,0:T(8,128)S(1)}, u32[]{:S(2)}, u32[]{:S(2)}) collective-permute-start(f32[392,128]{1,0:T(8,128)S(1)} %add.87.mine), channel_id=1, source_target_pairs={{0,384},{16,400},{32,416},{48,432},{64,448},{80,464},{96,480},{112... | collective-permute-start | bytes 602120 | tf_op jit(solution)/shard_map/ppermute | solution.py:504
  259.2 4.3 %shard_map.142 = (f32[512,256]{1,0:T(8,128)}, f32[8,512]{1,0:T(8,128)}, f32[256,256]{1,0:T(8,128)}, f32[8,256]{1,0:T(8,128)}) custom-call(f32[384,512]{1,0:T(8,128)} %get-tuple-element.81.upper, f32[512,256]{1,0:T(8,128)} %get-tuple-element.82.solved, f32[8,512]{1,0:T(8,128)} %get-tuple-element.83.solved_row, f32[256,512]{1,0:T(8,128)} %get-tuple-element.84.leaf_solved, ...), custom_call_target="tpu_custom_call" | custom-call | tf_op jit(solution)/shard_map/pallas_call | solution.py:128
  263.6 4.5 %collective-permute-done.24.below = f32[392,128]{1,0:T(8,128)S(1)} collective-permute-done((f32[392,128]{1,0:T(8,128)S(1)}, f32[392,128]{1,0:T(8,128)S(1)}, u32[]{:S(2)}, u32[]{:S(2)}) %collective-permute-start.24) | collective-permute-done | bytes 200736 | tf_op jit(solution)/shard_map/ppermute | solution.py:504
  268.8 12.4 %shard_map.143 = (f32[1,256]{1,0:T(1,128)}, f32[1,32]{1,0:T(1,128)}, f32[2,128]{1,0:T(2,128)}) custom-call(s32[5]{0:T(128)} %stack.23.flags, f32[392,128]{1,0:T(8,128)} %copy-done.2, f32[392,128]{1,0:T(8,128)} %copy-done.28, f32[392,128]{1,0:T(8,128)} %copy-done.29, f32[392,128]{1,0:T(8,128)} %copy-done.27, f32[256,256]{1,0:T(8,128)} %matrix.1, ...), custom_call_target="tpu_custom_call" | custom-call | tf_op jit(solution)/shard_map/pallas_call | solution.py:128
  (137 shorter events, 89.7 us)
Async XLA Ops:
  1.7 39.5 %collective-permute-start.1 = (f32[256,512]{1,0:T(8,128)S(1)}, f32[256,512]{1,0:T(8,128)S(1)}, u32[]{:S(2)}, u32[]{:S(2)}) collective-permute-start(f32[256,512]{1,0:T(8,128)S(1)} %bitcast_convert_fusion), channel_id=1, source_target_pairs={{0,10},{2,26},{4,8},{6,24},{8,6},{10,22},{12,4},{14,20},{1,42},{3,... | collective-permute-start | bytes 1572872 | tf_op jit(solution)/shard_map/ppermute | solution.py:438
  24.1 17.2 %collective-permute-start = (f32[136,128]{1,0:T(8,128)}, f32[136,128]{1,0:T(8,128)S(1)}, u32[]{:S(2)}, u32[]{:S(2)}) collective-permute-start(f32[136,128]{1,0:T(8,128)} %get-tuple-element.49), channel_id=1, source_target_pairs={{0,10},{2,26},{4,8},{6,24},{8,6},{10,22},{12,4},{14,20},{1,42},{3,... | collective-permute-start | bytes 208904 | tf_op jit(solution)/shard_map/ppermute | solution.py:440
  45.1 26.7 %collective-permute-start.2 = (f32[264,512]{1,0:T(8,128)}, f32[264,512]{1,0:T(8,128)S(1)}, u32[]{:S(2)}, u32[]{:S(2)}) collective-permute-start(f32[264,512]{1,0:T(8,128)} %get-tuple-element.55.own.own0), channel_id=1, source_target_pairs={{10,26},{26,10},{8,24},{24,8},{6,22},{22,6},{4,20},{20,4},{42,58},... | collective-permute-start | bytes 1622024 | tf_op jit(solution)/shard_map/ppermute | solution.py:415
  52.4 19.4 %collective-permute-start.3 = (f32[264,512]{1,0:T(8,128)}, f32[264,512]{1,0:T(8,128)S(1)}, u32[]{:S(2)}, u32[]{:S(2)}) collective-permute-start(f32[264,512]{1,0:T(8,128)} %get-tuple-element.55.own.own0), channel_id=1, source_target_pairs={{26,8},{8,26},{24,6},{6,24},{22,4},{4,22},{58,40},{40,58},{56,38},... | collective-permute-start | bytes 1622024 | tf_op jit(solution)/shard_map/ppermute | solution.py:413
  64.2 7.6 %collective-permute-start.4 = (f32[136,512]{1,0:T(8,128)}, f32[136,512]{1,0:T(8,128)S(1)}, u32[]{:S(2)}, u32[]{:S(2)}) collective-permute-start(f32[136,512]{1,0:T(8,128)} %get-tuple-element.57), channel_id=1, source_target_pairs={{10,42},{26,58},{8,40},{24,56},{6,38},{22,54},{4,36},{20,52},{42,1... | collective-permute-start | bytes 835592 | tf_op jit(solution)/shard_map/ppermute | solution.py:414
  75.7 15.3 %collective-permute-start.5 = (f32[264,512]{1,0:T(8,128)}, f32[264,512]{1,0:T(8,128)S(1)}, u32[]{:S(2)}, u32[]{:S(2)}) collective-permute-start(f32[264,512]{1,0:T(8,128)} %get-tuple-element.61.own), channel_id=1, source_target_pairs={{10,26},{26,10},{8,24},{24,8},{6,22},{22,6},{4,20},{20,4},{42,58},... | collective-permute-start | bytes 1622024 | tf_op jit(solution)/shard_map/ppermute | solution.py:415
  77.7 13.4 %collective-permute-start.6 = (f32[264,512]{1,0:T(8,128)}, f32[264,512]{1,0:T(8,128)S(1)}, u32[]{:S(2)}, u32[]{:S(2)}) collective-permute-start(f32[264,512]{1,0:T(8,128)} %get-tuple-element.61.own), channel_id=1, source_target_pairs={{26,8},{8,26},{24,6},{6,24},{22,4},{4,22},{58,40},{40,58},{56,38},... | collective-permute-start | bytes 1622024 | tf_op jit(solution)/shard_map/ppermute | solution.py:413
  95.7 15.3 %collective-permute-start.8 = (f32[264,512]{1,0:T(8,128)}, f32[264,512]{1,0:T(8,128)S(1)}, u32[]{:S(2)}, u32[]{:S(2)}) collective-permute-start(f32[264,512]{1,0:T(8,128)} %get-tuple-element.63.own2), channel_id=1, source_target_pairs={{10,26},{26,10},{8,24},{24,8},{6,22},{22,6},{4,20},{20,4},{42,58},... | collective-permute-start | bytes 1622024 | tf_op jit(solution)/shard_map/ppermute | solution.py:415
  97.6 13.4 %collective-permute-start.9 = (f32[264,512]{1,0:T(8,128)}, f32[264,512]{1,0:T(8,128)S(1)}, u32[]{:S(2)}, u32[]{:S(2)}) collective-permute-start(f32[264,512]{1,0:T(8,128)} %get-tuple-element.63.own2), channel_id=1, source_target_pairs={{26,8},{8,26},{24,6},{6,24},{22,4},{4,22},{58,40},{40,58},{56,38},... | collective-permute-start | bytes 1622024 | tf_op jit(solution)/shard_map/ppermute | solution.py:413
  102.6 8.3 %collective-permute-start.10 = (f32[136,512]{1,0:T(8,128)}, f32[136,512]{1,0:T(8,128)S(1)}, u32[]{:S(2)}, u32[]{:S(2)}) collective-permute-start(f32[136,512]{1,0:T(8,128)} %get-tuple-element.65), channel_id=1, source_target_pairs={{10,42},{26,58},{8,40},{24,56},{6,38},{22,54},{4,36},{20,52},{42,1... | collective-permute-start | bytes 835592 | tf_op jit(solution)/shard_map/ppermute | solution.py:414
  121.1 41.4 %all-to-all-start = ((f32[32,8,384]{2,1,0:T(8,128)}), f32[32,8,384]{2,1,0:T(8,128)S(1)}, u32[]{:S(2)}, u32[]{:S(2)}) async-start(f32[32,8,384]{2,1,0:T(8,128)} %bitcast.13), calls=%async_computation | async-start | bytes 786432 | tf_op jit(solution)/shard_map/all_to_all | solution.py:479
  132.6 18.5 %collective-permute-start.12 = (f32[264,512]{1,0:T(8,128)S(1)}, f32[264,512]{1,0:T(8,128)S(1)}, u32[]{:S(2)}, u32[]{:S(2)}) collective-permute-start(f32[264,512]{1,0:T(8,128)S(1)} %copy-done.6), channel_id=1, source_target_pairs={{10,26},{26,10},{8,24},{24,8},{6,22},{22,6},{4,20},{20,4},{42,58},... | collective-permute-start | bytes 1622024 | tf_op jit(solution)/shard_map/ppermute | solution.py:415
  134.8 24.1 %collective-permute-start.13 = (f32[264,512]{1,0:T(8,128)S(1)}, f32[264,512]{1,0:T(8,128)S(1)}, u32[]{:S(2)}, u32[]{:S(2)}) collective-permute-start(f32[264,512]{1,0:T(8,128)S(1)} %copy-done.6), channel_id=1, source_target_pairs={{26,8},{8,26},{24,6},{6,24},{22,4},{4,22},{58,40},{40,58},{56,38},... | collective-permute-start | bytes 1622024 | tf_op jit(solution)/shard_map/ppermute | solution.py:413
  139.4 11.7 %collective-permute-start.14 = (f32[136,512]{1,0:T(8,128)S(1)}, f32[136,512]{1,0:T(8,128)S(1)}, u32[]{:S(2)}, u32[]{:S(2)}) collective-permute-start(f32[136,512]{1,0:T(8,128)S(1)} %copy-done.33), channel_id=1, source_target_pairs={{10,42},{26,58},{8,40},{24,56},{6,38},{22,54},{4,36},{20,52},{42,1... | collective-permute-start | bytes 835592 | tf_op jit(solution)/shard_map/ppermute | solution.py:414
  163.4 36.9 %all-to-all-start.1 = ((f32[16,8,640]{2,1,0:T(8,128)}), f32[16,8,640]{2,1,0:T(8,128)S(1)}, u32[]{:S(2)}, u32[]{:S(2)}) async-start(f32[16,8,640]{2,1,0:T(8,128)} %broadcast_in_dim.16), calls=%async_computation.1 | async-start | bytes 655360 | tf_op jit(solution)/shard_map/all_to_all | solution.py:485
  172.6 17.9 %collective-permute-start.15 = (f32[264,512]{1,0:T(8,128)S(1)}, f32[264,512]{1,0:T(8,128)S(1)}, u32[]{:S(2)}, u32[]{:S(2)}) collective-permute-start(f32[264,512]{1,0:T(8,128)S(1)} %copy-done.3), channel_id=1, source_target_pairs={{10,26},{26,10},{8,24},{24,8},{6,22},{22,6},{4,20},{20,4},{42,58},... | collective-permute-start | bytes 1622024 | tf_op jit(solution)/shard_map/ppermute | solution.py:415
  175.5 21.0 %collective-permute-start.16 = (f32[264,512]{1,0:T(8,128)S(1)}, f32[264,512]{1,0:T(8,128)S(1)}, u32[]{:S(2)}, u32[]{:S(2)}) collective-permute-start(f32[264,512]{1,0:T(8,128)S(1)} %copy-done.3), channel_id=1, source_target_pairs={{26,8},{8,26},{24,6},{6,24},{22,4},{4,22},{58,40},{40,58},{56,38},... | collective-permute-start | bytes 1622024 | tf_op jit(solution)/shard_map/ppermute | solution.py:413
  180.2 10.3 %collective-permute-start.17 = (f32[136,512]{1,0:T(8,128)S(1)}, f32[136,512]{1,0:T(8,128)S(1)}, u32[]{:S(2)}, u32[]{:S(2)}) collective-permute-start(f32[136,512]{1,0:T(8,128)S(1)} %copy-done.34), channel_id=1, source_target_pairs={{10,42},{26,58},{8,40},{24,56},{6,38},{22,54},{4,36},{20,52},{42,1... | collective-permute-start | bytes 835592 | tf_op jit(solution)/shard_map/ppermute | solution.py:414
  200.4 12.6 %collective-permute-start.18 = (f32[16,8,640]{2,1,0:T(8,128)S(1)}, f32[16,8,640]{2,1,0:T(8,128)S(1)}, u32[]{:S(2)}, u32[]{:S(2)}) collective-permute-start(f32[16,8,640]{2,1,0:T(8,128)S(1)} %all-to-all-done.1.mine), channel_id=1, source_target_pairs={{0,32},{16,48},{32,0},{48,16},{64,96},{80,112},{96,64},{112,80},{1... | collective-permute-start | bytes 983048 | tf_op jit(solution)/shard_map/ppermute | solution.py:488
  203.5 40.5 %collective-permute-start.22 = (f32[264,512]{1,0:T(8,128)}, f32[264,512]{1,0:T(8,128)S(1)}, u32[]{:S(2)}, u32[]{:S(2)}) collective-permute-start(f32[264,512]{1,0:T(8,128)} %shard_map.139), channel_id=1, source_target_pairs={{10,0},{26,2},{8,4},{24,6},{6,8},{22,10},{4,12},{20,14},{42,1},{58... | collective-permute-start | bytes 1622024 | tf_op jit(solution)/shard_map/ppermute | solution.py:492
  239.7 9.9 %collective-permute-start.21 = (f32[392,128]{1,0:T(8,128)}, f32[392,128]{1,0:T(8,128)S(1)}, u32[]{:S(2)}, u32[]{:S(2)}) collective-permute-start(f32[392,128]{1,0:T(8,128)} %get-tuple-element.77), channel_id=1, source_target_pairs={{0,64},{16,80},{32,96},{48,112},{64,0},{80,16},{96,32},{112,48},{1... | collective-permute-start | bytes 602120 | tf_op jit(solution)/shard_map/ppermute | solution.py:502
  249.7 13.9 %collective-permute-start.25 = (f32[392,128]{1,0:T(8,128)S(1)}, f32[392,128]{1,0:T(8,128)S(1)}, u32[]{:S(2)}, u32[]{:S(2)}) collective-permute-start(f32[392,128]{1,0:T(8,128)S(1)} %add.87.mine), channel_id=1, source_target_pairs={{0,384},{16,400},{32,416},{48,432},{64,448},{80,464},{96,480},{112... | collective-permute-start | bytes 602120 | tf_op jit(solution)/shard_map/ppermute | solution.py:504
  254.3 9.2 %collective-permute-start.23 = (f32[392,128]{1,0:T(8,128)S(1)}, f32[392,128]{1,0:T(8,128)S(1)}, u32[]{:S(2)}, u32[]{:S(2)}) collective-permute-start(f32[392,128]{1,0:T(8,128)S(1)} %add.87.mine), channel_id=1, source_target_pairs={{0,256},{16,272},{32,288},{48,304},{64,320},{80,336},{96,352},{112... | collective-permute-start | bytes 602120 | tf_op jit(solution)/shard_map/ppermute | solution.py:504
  256.6 11.5 %collective-permute-start.24 = (f32[392,128]{1,0:T(8,128)S(1)}, f32[392,128]{1,0:T(8,128)S(1)}, u32[]{:S(2)}, u32[]{:S(2)}) collective-permute-start(f32[392,128]{1,0:T(8,128)S(1)} %add.87.mine), channel_id=1, source_target_pairs={{0,128},{16,144},{32,160},{48,176},{64,192},{80,208},{96,224},{112... | collective-permute-start | bytes 602120 | tf_op jit(solution)/shard_map/ppermute | solution.py:504
  (40 other events, 335.0 us)

commit v7 on v6

--- a/solution.py
+++ b/solution.py
@@ -368,7 +368,7 @@
     root_part[388:392] = jnp.broadcast_to(part_row[:, 128:256], (4, 128))
 
 
-def back_kernel(upper, solved, solved_row, leaf_solved, pulled, link_solved, vector, reach, base):
+def back_kernel(upper, solved, solved_row, link_solved, vector):
     pieces, rows = [None] * 4, [None] * 4
     for b in range(3, -1, -1):
         at = slice(b * 128, b * 128 + 128)
@@ -379,10 +379,12 @@
             row = row - dot(jnp.concatenate(rows[b + 1 :], axis=1), after, NT)
         pieces[b], rows[b] = piece, row
         link_solved[at] = piece
-    whole = jnp.concatenate(rows, axis=1)
-    vector[...] = jnp.broadcast_to(whole, (8, 512))
-    reach[...] = dot(leaf_solved[...], jnp.concatenate(pieces, axis=0))
-    base[...] = jnp.broadcast_to(pulled[0:1] - dot(whole, leaf_solved[...], NT), (8, 256))
+    vector[...] = jnp.broadcast_to(jnp.concatenate(rows, axis=1), (8, 512))
+
+
+def reach_kernel(link_solved, vector, leaf_solved, pulled, reach, base):
+    reach[...] = dot3(leaf_solved[...], link_solved[...])
+    base[...] = jnp.broadcast_to(pulled[0:1] - dot(vector[0:1], leaf_solved[...], NT), (8, 256))
 
 
 def root_kernel(
@@ -499,13 +501,13 @@
         scalars=1,
         scratch=[pltpu.VMEM((16, 4, 8, 640), F32)],
     )
-    across, leaf_solved = lax.optimization_barrier((lax.ppermute(part, "scen", flip(4)), leaf_solved))
+    across = lax.ppermute(part, "scen", flip(4))
+    link_solved, vector = call(back_kernel, [(512, 256), (8, 512)], upper, solved, solved_row)
+    across, leaf_solved, link_solved = lax.optimization_barrier((across, leaf_solved, link_solved))
     part = part + across
     others = [lax.ppermute(part, "scen", [(i, (i + by) % 32) for i in range(32)]) for by in (16, 8, 24)]
-    link_solved, vector, reach, base = call(
-        back_kernel, [(512, 256), (8, 512), (256, 256), (8, 256)], upper, solved, solved_row, leaf_solved, pulled
-    )
-    others[2], link_solved = lax.optimization_barrier((others[2], link_solved))
+    reach, base = call(reach_kernel, [(256, 256), (8, 256)], link_solved, vector, leaf_solved, pulled)
+    others[2], reach = lax.optimization_barrier((others[2], reach))
     step, parent, move = call(
         root_kernel,
         [(1, 256), (1, 32), (2, 128)],

time: 284 us -> 285 us (level)
    pallas_call x14 -> x15, Pallas kernels: 74.6 us -> 76.2 us  [call(): pl.pallas_call(kernel, out_shape=[jax.ShapeDtypeStruct(s, F32) for s in s...]
where the time goes in v7:
time: 285 us; the launch traced here: 283 us
  starting transfers between devices  127 us (45%)
  Pallas kernels  76.2 us (27%)
  waiting for transfers between devices  60.8 us (21%)
  local copies, waits for them, and re-layouts  13.3 us (5%)
  other arithmetic  3.47 us (1%)
    pallas_call x15, Pallas kernels, call(): pl.pallas_call(kernel, out_shape=[jax.ShapeDtypeStruct(s, F32) for s in s...  76.2 us
    ppermute x5, starting transfers between devices, neighbours(): chip = lax.ppermute(message, AXES, TO_CHIP)  31.8 us
    ppermute x5, waiting for transfers between devices, neighbours(): other = lax.ppermute(to_half, AXES, TO_HALF)  29.7 us
    ppermute x5, starting transfers between devices, neighbours(): return (lax.ppermute(message, AXES, TO_CORE), chip, other)  16.2 us
    ppermute x5, waiting for transfers between devices, neighbours(): chip = lax.ppermute(message, AXES, TO_CHIP)  13.8 us
    ppermute x1, starting transfers between devices, body(): field = lax.ppermute(own_coupling.astype(F32), AXES, MOVE_OUT)  13.4 us
    ppermute x5, starting transfers between devices, neighbours(): other = lax.ppermute(to_half, AXES, TO_HALF)  12 us
    all_to_all x1, starting transfers between devices, body(): shares = lax.all_to_all(half_sum, AXES, 0, 0, axis_index_groups=SAME_CORE)  11.4 us
  transfers between devices with their start and end apart: 28, of which 11 were waited for; matrix products, arithmetic and copies ran while one was open for 1% of the time, Pallas kernels for 18%

profile of v7, /device:TPU:1, one launch (start us, length us, event | category | flops | bytes accessed | tf_op | source)
XLA Modules:
  0.0 282.6 jit_solution(8953512524200503703)
XLA Ops:
  1.7 13.4 %collective-permute-start.1 = (f32[256,512]{1,0:T(8,128)S(1)}, f32[256,512]{1,0:T(8,128)S(1)}, u32[]{:S(2)}, u32[]{:S(2)}) collective-permute-start(f32[256,512]{1,0:T(8,128)S(1)} %bitcast_convert_fusion), channel_id=1, source_target_pairs={{0,10},{2,26},{4,8},{6,24},{8,6},{10,22},{12,4},{14,20},{1,42},{3,... | collective-permute-start | bytes 1572872 | tf_op jit(solution)/shard_map/ppermute | solution.py:440
  17.3 6.8 %shard_map.130 = (f32[256,128]{1,0:T(8,128)}, f32[136,128]{1,0:T(8,128)}) custom-call(f32[256,128]{1,0:T(8,128)} %bitcast.33, f32[8,128]{1,0:T(8,128)} %maximum_maximum_fusion.rows), custom_call_target="tpu_custom_call" | custom-call | tf_op jit(solution)/shard_map/pallas_call | solution.py:128
  31.9 9.4 %collective-permute-done.pack = f32[136,128]{1,0:T(8,128)S(1)} collective-permute-done((f32[136,128]{1,0:T(8,128)}, f32[136,128]{1,0:T(8,128)S(1)}, u32[]{:S(2)}, u32[]{:S(2)}) %collective-permute-start) | collective-permute-done | bytes 69664 | tf_op jit(solution)/shard_map/ppermute | solution.py:442
  45.1 7.3 %collective-permute-start.2 = (f32[264,512]{1,0:T(8,128)}, f32[264,512]{1,0:T(8,128)S(1)}, u32[]{:S(2)}, u32[]{:S(2)}) collective-permute-start(f32[264,512]{1,0:T(8,128)} %get-tuple-element.56.own.own0), channel_id=1, source_target_pairs={{10,26},{26,10},{8,24},{24,8},{6,22},{22,6},{4,20},{20,4},{42,58},... | collective-permute-start | bytes 1622024 | tf_op jit(solution)/shard_map/ppermute | solution.py:417
  52.5 11.8 %collective-permute-start.3 = (f32[264,512]{1,0:T(8,128)}, f32[264,512]{1,0:T(8,128)S(1)}, u32[]{:S(2)}, u32[]{:S(2)}) collective-permute-start(f32[264,512]{1,0:T(8,128)} %get-tuple-element.56.own.own0), channel_id=1, source_target_pairs={{26,8},{8,26},{24,6},{6,24},{22,4},{4,22},{58,40},{40,58},{56,38},... | collective-permute-start | bytes 1622024 | tf_op jit(solution)/shard_map/ppermute | solution.py:415
  66.2 5.6 %collective-permute-done.4.other = f32[136,512]{1,0:T(8,128)S(1)} collective-permute-done((f32[136,512]{1,0:T(8,128)}, f32[136,512]{1,0:T(8,128)S(1)}, u32[]{:S(2)}, u32[]{:S(2)}) %collective-permute-start.4) | collective-permute-done | bytes 278560 | tf_op jit(solution)/shard_map/ppermute | solution.py:416
  77.6 5.8 %collective-permute-start.6 = (f32[264,512]{1,0:T(8,128)}, f32[264,512]{1,0:T(8,128)S(1)}, u32[]{:S(2)}, u32[]{:S(2)}) collective-permute-start(f32[264,512]{1,0:T(8,128)} %get-tuple-element.62.own), channel_id=1, source_target_pairs={{26,8},{8,26},{24,6},{6,24},{22,4},{4,22},{58,40},{40,58},{56,38},... | collective-permute-start | bytes 1622024 | tf_op jit(solution)/shard_map/ppermute | solution.py:415
  85.4 5.6 %collective-permute-done.7.other = f32[136,512]{1,0:T(8,128)S(1)} collective-permute-done((f32[136,512]{1,0:T(8,128)}, f32[136,512]{1,0:T(8,128)S(1)}, u32[]{:S(2)}, u32[]{:S(2)}) %collective-permute-start.7) | collective-permute-done | bytes 278560 | tf_op jit(solution)/shard_map/ppermute | solution.py:416
  97.5 5.0 %collective-permute-start.9 = (f32[264,512]{1,0:T(8,128)}, f32[264,512]{1,0:T(8,128)S(1)}, u32[]{:S(2)}, u32[]{:S(2)}) collective-permute-start(f32[264,512]{1,0:T(8,128)} %get-tuple-element.64.own2), channel_id=1, source_target_pairs={{26,8},{8,26},{24,6},{6,24},{22,4},{4,22},{58,40},{40,58},{56,38},... | collective-permute-start | bytes 1622024 | tf_op jit(solution)/shard_map/ppermute | solution.py:415
  112.0 3.8 %shard_map.136 = (f32[264,512]{1,0:T(8,128)}, f32[2,128,384]{2,1,0:T(8,128)}, f32[2,128,384]{2,1,0:T(8,128)}) custom-call(s32[5]{0:T(128)} %stack.23.flags, f32[512,384]{1,0:T(8,128)} %get-tuple-element.60.gram, f32[8,512]{1,0:T(8,128)} %get-tuple-element.61.gather, f32[264,512]{1,0:T(8,128)} %get-tuple-element.56.own.own0, ...), custom_call_target="tpu_custom_call" | custom-call | tf_op jit(solution)/shard_map/pallas_call | solution.py:128
  121.1 11.4 %all-to-all-start = ((f32[32,8,384]{2,1,0:T(8,128)}), f32[32,8,384]{2,1,0:T(8,128)S(1)}, u32[]{:S(2)}, u32[]{:S(2)}) async-start(f32[32,8,384]{2,1,0:T(8,128)} %bitcast.13), calls=%async_computation | async-start | bytes 786432 | tf_op jit(solution)/shard_map/all_to_all | solution.py:481
  134.8 4.5 %collective-permute-start.13 = (f32[264,512]{1,0:T(8,128)S(1)}, f32[264,512]{1,0:T(8,128)S(1)}, u32[]{:S(2)}, u32[]{:S(2)}) collective-permute-start(f32[264,512]{1,0:T(8,128)S(1)} %copy-done.6), channel_id=1, source_target_pairs={{26,8},{8,26},{24,6},{6,24},{22,4},{4,22},{58,40},{40,58},{56,38},... | collective-permute-start | bytes 1622024 | tf_op jit(solution)/shard_map/ppermute | solution.py:415
  143.2 7.8 %collective-permute-done.14.other = f32[136,512]{1,0:T(8,128)S(1)} collective-permute-done((f32[136,512]{1,0:T(8,128)S(1)}, f32[136,512]{1,0:T(8,128)S(1)}, u32[]{:S(2)}, u32[]{:S(2)}) %collective-permute-start.14) | collective-permute-done | bytes 278560 | tf_op jit(solution)/shard_map/ppermute | solution.py:416
  151.1 7.8 %collective-permute-done.13.chip = f32[264,512]{1,0:T(8,128)S(1)} collective-permute-done((f32[264,512]{1,0:T(8,128)S(1)}, f32[264,512]{1,0:T(8,128)S(1)}, u32[]{:S(2)}, u32[]{:S(2)}) %collective-permute-start.13) | collective-permute-done | bytes 540704 | tf_op jit(solution)/shard_map/ppermute | solution.py:415
  163.4 9.1 %all-to-all-start.1 = ((f32[16,8,640]{2,1,0:T(8,128)}), f32[16,8,640]{2,1,0:T(8,128)S(1)}, u32[]{:S(2)}, u32[]{:S(2)}) async-start(f32[16,8,640]{2,1,0:T(8,128)} %broadcast_in_dim.16), calls=%async_computation.1 | async-start | bytes 655360 | tf_op jit(solution)/shard_map/all_to_all | solution.py:487
  175.4 4.7 %collective-permute-start.16 = (f32[264,512]{1,0:T(8,128)S(1)}, f32[264,512]{1,0:T(8,128)S(1)}, u32[]{:S(2)}, u32[]{:S(2)}) collective-permute-start(f32[264,512]{1,0:T(8,128)S(1)} %copy-done.3), channel_id=1, source_target_pairs={{26,8},{8,26},{24,6},{6,24},{22,4},{4,22},{58,40},{40,58},{56,38},... | collective-permute-start | bytes 1622024 | tf_op jit(solution)/shard_map/ppermute | solution.py:415
  183.2 7.2 %collective-permute-done.17.other = f32[136,512]{1,0:T(8,128)S(1)} collective-permute-done((f32[136,512]{1,0:T(8,128)S(1)}, f32[136,512]{1,0:T(8,128)S(1)}, u32[]{:S(2)}, u32[]{:S(2)}) %collective-permute-start.17) | collective-permute-done | bytes 278560 | tf_op jit(solution)/shard_map/ppermute | solution.py:416
  190.4 6.0 %collective-permute-done.16.chip = f32[264,512]{1,0:T(8,128)S(1)} collective-permute-done((f32[264,512]{1,0:T(8,128)S(1)}, f32[264,512]{1,0:T(8,128)S(1)}, u32[]{:S(2)}, u32[]{:S(2)}) %collective-permute-start.16) | collective-permute-done | bytes 540704 | tf_op jit(solution)/shard_map/ppermute | solution.py:415
  203.5 7.5 %collective-permute-start.22 = (f32[264,512]{1,0:T(8,128)}, f32[264,512]{1,0:T(8,128)S(1)}, u32[]{:S(2)}, u32[]{:S(2)}) collective-permute-start(f32[264,512]{1,0:T(8,128)} %shard_map.139), channel_id=1, source_target_pairs={{10,0},{26,2},{8,4},{24,6},{6,8},{22,10},{4,12},{20,14},{42,1},{58... | collective-permute-start | bytes 1622024 | tf_op jit(solution)/shard_map/ppermute | solution.py:494
  217.3 22.4 %shard_map.140 = (f32[392,128]{1,0:T(8,128)}, f32[384,512]{1,0:T(8,128)}, f32[512,256]{1,0:T(8,128)}, f32[8,512]{1,0:T(8,128)}) custom-call(s32[5]{0:T(128)} %stack.23.flags, f32[16,8,640]{2,1,0:T(8,128)} %copy-done.1, f32[16,8,640]{2,1,0:T(8,128)} %copy-done.18, f32[16,8,640]{2,1,0:T(8,128)} %copy-done.19, f32[16,8,640]{2,1,0:T(8,128)} %copy-done.20), custom_call_target="tpu_custom_call" | custom-call | tf_op jit(solution)/shard_map/pallas_call | solution.py:128
  239.7 4.2 %collective-permute-start.21 = (f32[392,128]{1,0:T(8,128)}, f32[392,128]{1,0:T(8,128)S(1)}, u32[]{:S(2)}, u32[]{:S(2)}) collective-permute-start(f32[392,128]{1,0:T(8,128)} %get-tuple-element.78), channel_id=1, source_target_pairs={{0,64},{16,80},{32,96},{48,112},{64,0},{80,16},{96,32},{112,48},{1... | collective-permute-start | bytes 602120 | tf_op jit(solution)/shard_map/ppermute | solution.py:504
  250.6 4.6 %collective-permute-start.25 = (f32[392,128]{1,0:T(8,128)S(1)}, f32[392,128]{1,0:T(8,128)S(1)}, u32[]{:S(2)}, u32[]{:S(2)}) collective-permute-start(f32[392,128]{1,0:T(8,128)S(1)} %add.87.mine), channel_id=1, source_target_pairs={{0,384},{16,400},{32,416},{48,432},{64,448},{80,464},{96,480},{112... | collective-permute-start | bytes 602120 | tf_op jit(solution)/shard_map/ppermute | solution.py:508
  264.3 5.3 %collective-permute-done.24.below = f32[392,128]{1,0:T(8,128)S(1)} collective-permute-done((f32[392,128]{1,0:T(8,128)S(1)}, f32[392,128]{1,0:T(8,128)S(1)}, u32[]{:S(2)}, u32[]{:S(2)}) %collective-permute-start.24) | collective-permute-done | bytes 200736 | tf_op jit(solution)/shard_map/ppermute | solution.py:508
  270.2 12.4 %shard_map.144 = (f32[1,256]{1,0:T(1,128)}, f32[1,32]{1,0:T(1,128)}, f32[2,128]{1,0:T(2,128)}) custom-call(s32[5]{0:T(128)} %stack.23.flags, f32[392,128]{1,0:T(8,128)} %copy-done.2, f32[392,128]{1,0:T(8,128)} %copy-done.28, f32[392,128]{1,0:T(8,128)} %copy-done.29, f32[392,128]{1,0:T(8,128)} %copy-done.27, f32[256,256]{1,0:T(8,128)} %matrix.1, ...), custom_call_target="tpu_custom_call" | custom-call | tf_op jit(solution)/shard_map/pallas_call | solution.py:128
  (138 shorter events, 91.2 us)
Async XLA Ops:
  1.7 39.5 %collective-permute-start.1 = (f32[256,512]{1,0:T(8,128)S(1)}, f32[256,512]{1,0:T(8,128)S(1)}, u32[]{:S(2)}, u32[]{:S(2)}) collective-permute-start(f32[256,512]{1,0:T(8,128)S(1)} %bitcast_convert_fusion), channel_id=1, source_target_pairs={{0,10},{2,26},{4,8},{6,24},{8,6},{10,22},{12,4},{14,20},{1,42},{3,... | collective-permute-start | bytes 1572872 | tf_op jit(solution)/shard_map/ppermute | solution.py:440
  24.1 17.1 %collective-permute-start = (f32[136,128]{1,0:T(8,128)}, f32[136,128]{1,0:T(8,128)S(1)}, u32[]{:S(2)}, u32[]{:S(2)}) collective-permute-start(f32[136,128]{1,0:T(8,128)} %get-tuple-element.50), channel_id=1, source_target_pairs={{0,10},{2,26},{4,8},{6,24},{8,6},{10,22},{12,4},{14,20},{1,42},{3,... | collective-permute-start | bytes 208904 | tf_op jit(solution)/shard_map/ppermute | solution.py:442
  45.1 26.7 %collective-permute-start.2 = (f32[264,512]{1,0:T(8,128)}, f32[264,512]{1,0:T(8,128)S(1)}, u32[]{:S(2)}, u32[]{:S(2)}) collective-permute-start(f32[264,512]{1,0:T(8,128)} %get-tuple-element.56.own.own0), channel_id=1, source_target_pairs={{10,26},{26,10},{8,24},{24,8},{6,22},{22,6},{4,20},{20,4},{42,58},... | collective-permute-start | bytes 1622024 | tf_op jit(solution)/shard_map/ppermute | solution.py:417
  52.5 19.4 %collective-permute-start.3 = (f32[264,512]{1,0:T(8,128)}, f32[264,512]{1,0:T(8,128)S(1)}, u32[]{:S(2)}, u32[]{:S(2)}) collective-permute-start(f32[264,512]{1,0:T(8,128)} %get-tuple-element.56.own.own0), channel_id=1, source_target_pairs={{26,8},{8,26},{24,6},{6,24},{22,4},{4,22},{58,40},{40,58},{56,38},... | collective-permute-start | bytes 1622024 | tf_op jit(solution)/shard_map/ppermute | solution.py:415
  64.2 7.6 %collective-permute-start.4 = (f32[136,512]{1,0:T(8,128)}, f32[136,512]{1,0:T(8,128)S(1)}, u32[]{:S(2)}, u32[]{:S(2)}) collective-permute-start(f32[136,512]{1,0:T(8,128)} %get-tuple-element.58), channel_id=1, source_target_pairs={{10,42},{26,58},{8,40},{24,56},{6,38},{22,54},{4,36},{20,52},{42,1... | collective-permute-start | bytes 835592 | tf_op jit(solution)/shard_map/ppermute | solution.py:416
  75.7 15.3 %collective-permute-start.5 = (f32[264,512]{1,0:T(8,128)}, f32[264,512]{1,0:T(8,128)S(1)}, u32[]{:S(2)}, u32[]{:S(2)}) collective-permute-start(f32[264,512]{1,0:T(8,128)} %get-tuple-element.62.own), channel_id=1, source_target_pairs={{10,26},{26,10},{8,24},{24,8},{6,22},{22,6},{4,20},{20,4},{42,58},... | collective-permute-start | bytes 1622024 | tf_op jit(solution)/shard_map/ppermute | solution.py:417
  77.6 13.4 %collective-permute-start.6 = (f32[264,512]{1,0:T(8,128)}, f32[264,512]{1,0:T(8,128)S(1)}, u32[]{:S(2)}, u32[]{:S(2)}) collective-permute-start(f32[264,512]{1,0:T(8,128)} %get-tuple-element.62.own), channel_id=1, source_target_pairs={{26,8},{8,26},{24,6},{6,24},{22,4},{4,22},{58,40},{40,58},{56,38},... | collective-permute-start | bytes 1622024 | tf_op jit(solution)/shard_map/ppermute | solution.py:415
  95.6 15.3 %collective-permute-start.8 = (f32[264,512]{1,0:T(8,128)}, f32[264,512]{1,0:T(8,128)S(1)}, u32[]{:S(2)}, u32[]{:S(2)}) collective-permute-start(f32[264,512]{1,0:T(8,128)} %get-tuple-element.64.own2), channel_id=1, source_target_pairs={{10,26},{26,10},{8,24},{24,8},{6,22},{22,6},{4,20},{20,4},{42,58},... | collective-permute-start | bytes 1622024 | tf_op jit(solution)/shard_map/ppermute | solution.py:417
  97.5 13.4 %collective-permute-start.9 = (f32[264,512]{1,0:T(8,128)}, f32[264,512]{1,0:T(8,128)S(1)}, u32[]{:S(2)}, u32[]{:S(2)}) collective-permute-start(f32[264,512]{1,0:T(8,128)} %get-tuple-element.64.own2), channel_id=1, source_target_pairs={{26,8},{8,26},{24,6},{6,24},{22,4},{4,22},{58,40},{40,58},{56,38},... | collective-permute-start | bytes 1622024 | tf_op jit(solution)/shard_map/ppermute | solution.py:415
  102.6 8.3 %collective-permute-start.10 = (f32[136,512]{1,0:T(8,128)}, f32[136,512]{1,0:T(8,128)S(1)}, u32[]{:S(2)}, u32[]{:S(2)}) collective-permute-start(f32[136,512]{1,0:T(8,128)} %get-tuple-element.66), channel_id=1, source_target_pairs={{10,42},{26,58},{8,40},{24,56},{6,38},{22,54},{4,36},{20,52},{42,1... | collective-permute-start | bytes 835592 | tf_op jit(solution)/shard_map/ppermute | solution.py:416
  121.1 41.4 %all-to-all-start = ((f32[32,8,384]{2,1,0:T(8,128)}), f32[32,8,384]{2,1,0:T(8,128)S(1)}, u32[]{:S(2)}, u32[]{:S(2)}) async-start(f32[32,8,384]{2,1,0:T(8,128)} %bitcast.13), calls=%async_computation | async-start | bytes 786432 | tf_op jit(solution)/shard_map/all_to_all | solution.py:481
  132.6 18.5 %collective-permute-start.12 = (f32[264,512]{1,0:T(8,128)S(1)}, f32[264,512]{1,0:T(8,128)S(1)}, u32[]{:S(2)}, u32[]{:S(2)}) collective-permute-start(f32[264,512]{1,0:T(8,128)S(1)} %copy-done.6), channel_id=1, source_target_pairs={{10,26},{26,10},{8,24},{24,8},{6,22},{22,6},{4,20},{20,4},{42,58},... | collective-permute-start | bytes 1622024 | tf_op jit(solution)/shard_map/ppermute | solution.py:417
  134.8 24.1 %collective-permute-start.13 = (f32[264,512]{1,0:T(8,128)S(1)}, f32[264,512]{1,0:T(8,128)S(1)}, u32[]{:S(2)}, u32[]{:S(2)}) collective-permute-start(f32[264,512]{1,0:T(8,128)S(1)} %copy-done.6), channel_id=1, source_target_pairs={{26,8},{8,26},{24,6},{6,24},{22,4},{4,22},{58,40},{40,58},{56,38},... | collective-permute-start | bytes 1622024 | tf_op jit(solution)/shard_map/ppermute | solution.py:415
  139.3 11.7 %collective-permute-start.14 = (f32[136,512]{1,0:T(8,128)S(1)}, f32[136,512]{1,0:T(8,128)S(1)}, u32[]{:S(2)}, u32[]{:S(2)}) collective-permute-start(f32[136,512]{1,0:T(8,128)S(1)} %copy-done.33), channel_id=1, source_target_pairs={{10,42},{26,58},{8,40},{24,56},{6,38},{22,54},{4,36},{20,52},{42,1... | collective-permute-start | bytes 835592 | tf_op jit(solution)/shard_map/ppermute | solution.py:416
  163.4 36.9 %all-to-all-start.1 = ((f32[16,8,640]{2,1,0:T(8,128)}), f32[16,8,640]{2,1,0:T(8,128)S(1)}, u32[]{:S(2)}, u32[]{:S(2)}) async-start(f32[16,8,640]{2,1,0:T(8,128)} %broadcast_in_dim.16), calls=%async_computation.1 | async-start | bytes 655360 | tf_op jit(solution)/shard_map/all_to_all | solution.py:487
  172.5 17.9 %collective-permute-start.15 = (f32[264,512]{1,0:T(8,128)S(1)}, f32[264,512]{1,0:T(8,128)S(1)}, u32[]{:S(2)}, u32[]{:S(2)}) collective-permute-start(f32[264,512]{1,0:T(8,128)S(1)} %copy-done.3), channel_id=1, source_target_pairs={{10,26},{26,10},{8,24},{24,8},{6,22},{22,6},{4,20},{20,4},{42,58},... | collective-permute-start | bytes 1622024 | tf_op jit(solution)/shard_map/ppermute | solution.py:417
  175.4 21.0 %collective-permute-start.16 = (f32[264,512]{1,0:T(8,128)S(1)}, f32[264,512]{1,0:T(8,128)S(1)}, u32[]{:S(2)}, u32[]{:S(2)}) collective-permute-start(f32[264,512]{1,0:T(8,128)S(1)} %copy-done.3), channel_id=1, source_target_pairs={{26,8},{8,26},{24,6},{6,24},{22,4},{4,22},{58,40},{40,58},{56,38},... | collective-permute-start | bytes 1622024 | tf_op jit(solution)/shard_map/ppermute | solution.py:415
  180.1 10.3 %collective-permute-start.17 = (f32[136,512]{1,0:T(8,128)S(1)}, f32[136,512]{1,0:T(8,128)S(1)}, u32[]{:S(2)}, u32[]{:S(2)}) collective-permute-start(f32[136,512]{1,0:T(8,128)S(1)} %copy-done.34), channel_id=1, source_target_pairs={{10,42},{26,58},{8,40},{24,56},{6,38},{22,54},{4,36},{20,52},{42,1... | collective-permute-start | bytes 835592 | tf_op jit(solution)/shard_map/ppermute | solution.py:416
  200.3 12.6 %collective-permute-start.18 = (f32[16,8,640]{2,1,0:T(8,128)S(1)}, f32[16,8,640]{2,1,0:T(8,128)S(1)}, u32[]{:S(2)}, u32[]{:S(2)}) collective-permute-start(f32[16,8,640]{2,1,0:T(8,128)S(1)} %all-to-all-done.1.mine), channel_id=1, source_target_pairs={{0,32},{16,48},{32,0},{48,16},{64,96},{80,112},{96,64},{112,80},{1... | collective-permute-start | bytes 983048 | tf_op jit(solution)/shard_map/ppermute | solution.py:490
  203.5 40.4 %collective-permute-start.22 = (f32[264,512]{1,0:T(8,128)}, f32[264,512]{1,0:T(8,128)S(1)}, u32[]{:S(2)}, u32[]{:S(2)}) collective-permute-start(f32[264,512]{1,0:T(8,128)} %shard_map.139), channel_id=1, source_target_pairs={{10,0},{26,2},{8,4},{24,6},{6,8},{22,10},{4,12},{20,14},{42,1},{58... | collective-permute-start | bytes 1622024 | tf_op jit(solution)/shard_map/ppermute | solution.py:494
  239.7 10.8 %collective-permute-start.21 = (f32[392,128]{1,0:T(8,128)}, f32[392,128]{1,0:T(8,128)S(1)}, u32[]{:S(2)}, u32[]{:S(2)}) collective-permute-start(f32[392,128]{1,0:T(8,128)} %get-tuple-element.78), channel_id=1, source_target_pairs={{0,64},{16,80},{32,96},{48,112},{64,0},{80,16},{96,32},{112,48},{1... | collective-permute-start | bytes 602120 | tf_op jit(solution)/shard_map/ppermute | solution.py:504
  250.6 12.1 %collective-permute-start.25 = (f32[392,128]{1,0:T(8,128)S(1)}, f32[392,128]{1,0:T(8,128)S(1)}, u32[]{:S(2)}, u32[]{:S(2)}) collective-permute-start(f32[392,128]{1,0:T(8,128)S(1)} %add.87.mine), channel_id=1, source_target_pairs={{0,384},{16,400},{32,416},{48,432},{64,448},{80,464},{96,480},{112... | collective-permute-start | bytes 602120 | tf_op jit(solution)/shard_map/ppermute | solution.py:508
  255.2 9.0 %collective-permute-start.23 = (f32[392,128]{1,0:T(8,128)S(1)}, f32[392,128]{1,0:T(8,128)S(1)}, u32[]{:S(2)}, u32[]{:S(2)}) collective-permute-start(f32[392,128]{1,0:T(8,128)S(1)} %add.87.mine), channel_id=1, source_target_pairs={{0,256},{16,272},{32,288},{48,304},{64,320},{80,336},{96,352},{112... | collective-permute-start | bytes 602120 | tf_op jit(solution)/shard_map/ppermute | solution.py:508
  257.5 12.1 %collective-permute-start.24 = (f32[392,128]{1,0:T(8,128)S(1)}, f32[392,128]{1,0:T(8,128)S(1)}, u32[]{:S(2)}, u32[]{:S(2)}) collective-permute-start(f32[392,128]{1,0:T(8,128)S(1)} %add.87.mine), channel_id=1, source_target_pairs={{0,128},{16,144},{32,160},{48,176},{64,192},{80,208},{96,224},{112... | collective-permute-start | bytes 602120 | tf_op jit(solution)/shard_map/ppermute | solution.py:508
  (40 other events, 329.8 us)
